TPU v7x, 256 devices: a whole 4x4x8 slice. The times are simulated.
256 devices in a mesh: slab: 64 (over y, z, x_hi), term: 4 (over x_lo, core).
Axes of the slice: x: 4 (x_hi: 2, x_lo: 2; x = x_hi * 2 + x_lo), y: 4, z: 8, core: 2. Of those that a mesh axis runs over, the one named last changes fastest.
Arguments:
- right_side: float32 [84, 128, 128, 128], P('term', 'slab'), may hold values from -24 to 24
- mean_cond: float32 [128, 128, 128], P('slab', 'term'), may hold values from 2 to 4
- cond_terms: float32 [6, 128, 128, 128], P(None, 'slab', 'term'), may hold values from -0.3 to 0.3
Outputs:
- solution: float32 [84, 128, 128, 128], P('term', 'slab')
- residual: float32 [84, 128, 128, 128], P('term', 'slab')
All inputs are finite; a program needn't handle non-finite values.
Results may differ from a plain program's by a relative error of at most 0.00013.
Values sent between devices are 32-bit elements; how exact they have to be, the bound alone decides.
No kernel may reach another device: no remote copies, remote signals or barrier semaphores. Data moves between devices by JAX's collectives and lax.ppermute only.
A program may use at most 64 MiB of HBM per device.

v0:
```python
import math

import jax
import jax.numpy as jnp
from jax import lax
from jax.sharding import PartitionSpec as P

DIM = 6
DEG = 3
ITERS = 2


lower_edge = 2.0
upper_edge = 72.0


def extended_2(array, sides, width):
    for axis, dim in sides:
        devices, length = (lax.axis_size(axis), array.shape[dim])
        up = [(i, (i + 1) % devices) for i in range(devices - 1)]
        down = [(j, i) for i, j in up]
        last = lax.slice_in_dim(array, length - width, length, axis=dim)
        leading = lax.slice_in_dim(array, 0, width, axis=dim)
        before = lax.ppermute(last, axis, up)
        after = lax.ppermute(leading, axis, down)
        array = jnp.concatenate([before, array, after], axis=dim)
    return array


def compositions(degree_sum, slots_left):
    if slots_left == 1:
        return [[degree_sum]]
    listing = []
    for leading in range(degree_sum, -1, -1):
        for remainder in compositions(degree_sum - leading, slots_left - 1):
            listing.append([leading] + remainder)
    return listing


def galerkin_tables(variables, degree):
    indices = []
    for degree_level in range(degree + 1):
        indices.extend(compositions(degree_level, variables))
    count = len(indices)
    tables = []
    for variable in range(variables):
        rows_list = []
        for row in range(count):
            first = indices[row]
            entries = []
            for col in range(count):
                second = indices[col]
                agreeing = all((first[m] == second[m] for m in range(variables) if m != variable))
                value = 0.0
                if agreeing and abs(first[variable] - second[variable]) == 1:
                    higher = max(first[variable], second[variable])
                    value = higher / math.sqrt(4.0 * higher * higher - 1.0)
                entries.append(value)
            rows_list.append(entries)
        tables.append(rows_list)
    return tables


def laplace(extended, field):
    beside = extended[:, 2:, 1:-1, 1:-1] + extended[:, :-2, 1:-1, 1:-1]
    beside = beside + extended[:, 1:-1, 2:, 1:-1] + extended[:, 1:-1, :-2, 1:-1]
    beside = beside + extended[:, 1:-1, 1:-1, 2:] + extended[:, 1:-1, 1:-1, :-2]
    return 6.0 * field - beside


def coupling(lap_field, mean_cond, cond_terms, tables):
    flat = lap_field.reshape(lap_field.shape[0], -1)
    result = mean_cond.reshape(1, -1) * flat
    terms_flat = cond_terms.reshape(cond_terms.shape[0], -1)
    for variable in range(cond_terms.shape[0]):
        mixed = jnp.dot(
            tables[variable],
            flat,
            precision=lax.Precision.HIGHEST,
            preferred_element_type=jnp.float32,
        )
        result = result + terms_flat[variable][None, :] * mixed
    return result.reshape(lap_field.shape)


def chebyshev(right_side, apply_operator):
    center_value = 0.5 * (upper_edge + lower_edge)
    half_width = 0.5 * (upper_edge - lower_edge)
    sigma_value = center_value / half_width
    rho_now = 1.0 / sigma_value
    residual = right_side
    direction = right_side / center_value
    solution = jnp.zeros_like(right_side)
    for iteration in range(ITERS):
        solution = solution + direction
        residual = residual - apply_operator(direction)
        rho_next = 1.0 / (2.0 * sigma_value - rho_now)
        if iteration + 1 < ITERS:
            direction = rho_next * rho_now * direction + 2.0 * rho_next / half_width * residual
        rho_now = rho_next
    return (solution, residual)


def shards(right_side, mean_cond, cond_terms):
    tables = jnp.asarray(galerkin_tables(DIM, DEG), jnp.float32)

    def apply_operator(field):
        extended = extended_2(field, (("slab", 1),), 1)
        extended = jnp.pad(extended, ((0, 0), (0, 0), (1, 1), (1, 1)))
        lap_field = laplace(extended, field)
        banded = lax.all_to_all(lap_field, "term", split_axis=2, concat_axis=0, tiled=True)
        mixed = coupling(banded, mean_cond, cond_terms, tables)
        return lax.all_to_all(mixed, "term", split_axis=0, concat_axis=2, tiled=True)

    solution, residual = chebyshev(right_side, apply_operator)
    return (solution, residual)


def solution(mesh):
    placed = (P("term", "slab", None, None), P("slab", "term", None), P(None, "slab", "term", None))
    return jax.shard_map(
        shards,
        mesh=mesh,
        in_specs=placed,
        out_specs=(P("term", "slab", None, None), P("term", "slab", None, None)),
        check_vma=False,
    )
```

profile of v0, /device:TPU:1, one launch (start us, length us, event | category | flops | bytes accessed | tf_op | source)
XLA Modules:
  0.0 371.6 jit_solution(4195840393375851876)
XLA Ops:
  2.9 5.6 %collective-permute-start.1 = (f32[21,1,128,128]{3,2,1,0:T(8,128)S(1)}, f32[21,1,128,128]{3,2,1,0:T(8,128)S(1)}, u32[]{:S(2)}, u32[]{:S(2)}) collective-permute-start(f32[21,1,128,128]{3,2,1,0:T(8,128)S(1)} %get-tuple-element.8), channel_id=1, source_target_pairs={{0,4},{4,8},{8,12},{12,16},{16,20},{20,24},{24,28},{28,32},{32,36}... | collective-permute-start | bytes 4128776 | tf_op jit(solution)/shard_map/ppermute | solution.py:24
  10.1 56.7 %collective-permute-done.1 = f32[21,1,128,128]{3,2,1,0:T(8,128)S(1)} collective-permute-done((f32[21,1,128,128]{3,2,1,0:T(8,128)S(1)}, f32[21,1,128,128]{3,2,1,0:T(8,128)S(1)}, u32[]{:S(2)}, u32[]{:S(2)}) %collective-permute-start.1) | collective-permute-done | bytes 1376288 | tf_op jit(solution)/shard_map/ppermute | solution.py:24
  66.7 7.0 %collective-permute-done = f32[21,1,128,128]{3,2,1,0:T(8,128)S(1)} collective-permute-done((f32[21,1,128,128]{3,2,1,0:T(8,128)S(1)}, f32[21,1,128,128]{3,2,1,0:T(8,128)S(1)}, u32[]{:S(2)}, u32[]{:S(2)}) %collective-permute-start) | collective-permute-done | bytes 1376288 | tf_op jit(solution)/shard_map/ppermute | solution.py:25
  74.8 4.8 %select_maximum_fusion.2 = f32[21,4,130,130]{3,2,1,0:T(8,128)S(1)} fusion(f32[21,1,128,128]{3,2,1,0:T(8,128)S(1)} %collective-permute-done, f32[21,2,128,128]{3,2,1,0:T(8,128)S(1)} %broadcast_multiply_fusion, f32[21,1,128,128]{3,2,1,0:T(8,128)S(1)} %collective-permute-done.1), kind=kLoop, calls=%fused_computation.6 | loop fusion | flops 21294000 | bytes 11183424 | tf_op jit(solution)/shard_map/concatenate | solution.py:26
  79.5 3.7 fusion.29
  83.2 3.3 copy.20
  86.5 4.4 %all-to-all-start = ((f32[21,2,128,128]{3,0,1,2:T(8,128)}), f32[21,2,128,128]{3,0,1,2:T(8,128)S(1)}, u32[]{:S(2)}, u32[]{:S(2)}) async-start(f32[21,2,128,128]{3,0,1,2:T(8,128)} %copy.20), calls=%async_computation | async-start | bytes 6291456 | tf_op jit(solution)/shard_map/all_to_all | solution.py:111
  90.9 36.0 %all-to-all-done = f32[21,2,128,128]{3,0,1,2:T(8,128)S(1)} async-done(((f32[21,2,128,128]{3,0,1,2:T(8,128)}), f32[21,2,128,128]{3,0,1,2:T(8,128)S(1)}, u32[]{:S(2)}, u32[]{:S(2)}) %all-to-all-start) | async-done | bytes 2752544 | tf_op jit(solution)/shard_map/all_to_all | solution.py:111
  132.2 3.2 fusion.26
  135.5 3.1 fusion.24
  138.6 3.1 fusion.22
  144.9 3.5 fusion.18
  148.5 3.1 fusion.16
  152.5 35.0 %all_to_all.66 = f32[84,2,32,128]{3,2,1,0:T(8,128)S(1)} all-to-all(f32[84,2,32,128]{3,2,1,0:T(8,128)S(1)} %bitcast.121), channel_id=1, replica_groups=mesh['slab'=64,'term'=4] {'term'}, dimensions={0} | all-to-all | bytes 5505024 | tf_op jit(solution)/shard_map/all_to_all | solution.py:113
  194.6 56.6 %collective-permute-done.3 = f32[21,1,128,128]{3,2,1,0:T(8,128)S(1)} collective-permute-done((f32[21,1,128,128]{3,2,1,0:T(8,128)S(1)}, f32[21,1,128,128]{3,2,1,0:T(8,128)S(1)}, u32[]{:S(2)}, u32[]{:S(2)}) %collective-permute-start.3) | collective-permute-done | bytes 1376288 | tf_op jit(solution)/shard_map/ppermute | solution.py:24
  251.3 5.4 %collective-permute-done.2 = f32[21,1,128,128]{3,2,1,0:T(8,128)S(1)} collective-permute-done((f32[21,1,128,128]{3,2,1,0:T(8,128)S(1)}, f32[21,1,128,128]{3,2,1,0:T(8,128)S(1)}, u32[]{:S(2)}, u32[]{:S(2)}) %collective-permute-start.2) | collective-permute-done | bytes 1376288 | tf_op jit(solution)/shard_map/ppermute | solution.py:25
  256.7 4.8 %select_maximum_fusion = f32[21,4,130,130]{3,2,1,0:T(8,128)S(1)} fusion(f32[21,1,128,128]{3,2,1,0:T(8,128)S(1)} %collective-permute-done.2, f32[21,2,128,128]{3,2,1,0:T(8,128)S(1)} %get-tuple-element.5, f32[21,1,128,128]{3,2,1,0:T(8,128)S(1)} %collective-permute-done.3), kind=kLoop, calls=%fused_computation.4 | loop fusion | flops 21294000 | bytes 11183424 | tf_op jit(solution)/shard_map/concatenate | solution.py:26
  265.7 40.5 %all_to_all.67 = f32[21,2,128,128]{3,0,1,2:T(8,128)S(1)} all-to-all(f32[21,2,128,128]{3,0,1,2:T(8,128)S(1)} %copy.23), channel_id=1, replica_groups=mesh['slab'=64,'term'=4] {'term'}, dimensions={2} | all-to-all | bytes 5505024 | tf_op jit(solution)/shard_map/all_to_all | solution.py:111
  311.5 3.2 fusion.14
  314.7 3.1 fusion.12
  317.8 3.1 fusion.10
  324.0 3.3 fusion.6
  327.4 3.1 fusion.4
  331.2 35.2 %all_to_all.68 = f32[84,2,32,128]{3,2,1,0:T(8,128)S(1)} all-to-all(f32[84,2,32,128]{3,2,1,0:T(8,128)S(1)} %bitcast.124), channel_id=1, replica_groups=mesh['slab'=64,'term'=4] {'term'}, dimensions={0} | all-to-all | bytes 5505024 | tf_op jit(solution)/shard_map/all_to_all | solution.py:113
  (51 shorter events, 39.5 us)
Async XLA Ops:
  2.9 63.8 %collective-permute-start.1 = (f32[21,1,128,128]{3,2,1,0:T(8,128)S(1)}, f32[21,1,128,128]{3,2,1,0:T(8,128)S(1)}, u32[]{:S(2)}, u32[]{:S(2)}) collective-permute-start(f32[21,1,128,128]{3,2,1,0:T(8,128)S(1)} %get-tuple-element.8), channel_id=1, source_target_pairs={{0,4},{4,8},{8,12},{12,16},{16,20},{20,24},{24,28},{28,32},{32,36}... | collective-permute-start | bytes 4128776 | tf_op jit(solution)/shard_map/ppermute | solution.py:24
  8.5 71.1 %copy-start = (f32[21,2,128,128]{3,2,1,0:T(8,128)S(1)}, f32[21,2,128,128]{3,2,1,0:T(8,128)}, u32[]{:S(2)}) copy-start(f32[21,2,128,128]{3,2,1,0:T(8,128)} %param.4) | copy-start | bytes 8257540
  8.5 65.2 %collective-permute-start = (f32[21,1,128,128]{3,2,1,0:T(8,128)S(1)}, f32[21,1,128,128]{3,2,1,0:T(8,128)S(1)}, u32[]{:S(2)}, u32[]{:S(2)}) collective-permute-start(f32[21,1,128,128]{3,2,1,0:T(8,128)S(1)} %get-tuple-element.9), channel_id=1, source_target_pairs={{4,0},{8,4},{12,8},{16,12},{20,16},{24,20},{28,24},{32,28},{36,32}... | collective-permute-start | bytes 4128776 | tf_op jit(solution)/shard_map/ppermute | solution.py:25
  73.7 1.1 copy-start.5
  86.5 4.4 %copy-start.6 = (f32[6,2,32,128]{3,2,1,0:T(8,128)S(1)}, f32[6,2,32,128]{3,2,1,0:T(8,128)}, u32[]{:S(2)}) copy-start(f32[6,2,32,128]{3,2,1,0:T(8,128)} %param.6) | copy-start | bytes 589828
  86.5 40.4 %all-to-all-start = ((f32[21,2,128,128]{3,0,1,2:T(8,128)}), f32[21,2,128,128]{3,0,1,2:T(8,128)S(1)}, u32[]{:S(2)}, u32[]{:S(2)}) async-start(f32[21,2,128,128]{3,0,1,2:T(8,128)} %copy.20), calls=%async_computation | async-start | bytes 6291456 | tf_op jit(solution)/shard_map/all_to_all | solution.py:111
  129.3 2.9 copy-start.11
  129.3 2.9 copy-start.13
  132.2 3.2 copy-start.12
  135.5 3.1 copy-start.10
  138.6 3.1 copy-start.9
  141.8 3.1 copy-start.8
  144.9 3.6 copy-start.7
  187.5 1.8 copy-start.1
  189.3 2.4 copy-start.3
  191.9 59.3 %collective-permute-start.3 = (f32[21,1,128,128]{3,2,1,0:T(8,128)S(1)}, f32[21,1,128,128]{3,2,1,0:T(8,128)S(1)}, u32[]{:S(2)}, u32[]{:S(2)}) collective-permute-start(f32[21,1,128,128]{3,2,1,0:T(8,128)S(1)} %get-tuple-element.6), channel_id=1, source_target_pairs={{0,4},{4,8},{8,12},{12,16},{16,20},{20,24},{24,28},{28,32},{32,36}... | collective-permute-start | bytes 4128776 | tf_op jit(solution)/shard_map/ppermute | solution.py:24
  193.3 63.4 %collective-permute-start.2 = (f32[21,1,128,128]{3,2,1,0:T(8,128)S(1)}, f32[21,1,128,128]{3,2,1,0:T(8,128)S(1)}, u32[]{:S(2)}, u32[]{:S(2)}) collective-permute-start(f32[21,1,128,128]{3,2,1,0:T(8,128)S(1)} %get-tuple-element.7), channel_id=1, source_target_pairs={{4,0},{8,4},{12,8},{16,12},{20,16},{24,20},{28,24},{32,28},{36,32}... | collective-permute-start | bytes 4128776 | tf_op jit(solution)/shard_map/ppermute | solution.py:25
  366.5 1.8 copy-start.2
  366.5 2.6 copy-start.4
where the time goes:
time: 378 us; the launch traced here: 372 us
  waiting for transfers between devices  162 us (43%)
  blocking collectives  111 us (29%)
  matrix products  38.3 us (10%)
  local copies, waits for them, and re-layouts  22.9 us (6%)
  other arithmetic  22.6 us (6%)
  starting transfers between devices  14.1 us (4%)
    ppermute x2, waiting for transfers between devices, extended_2(): before = lax.ppermute(last, axis, up)  113 us
    all_to_all x2, blocking collectives, apply_operator(): lax.all_to_all(mixed, 'term', split_axis=0, concat_axis=2, tiled=True)  70.3 us
    all_to_all x1, blocking collectives, apply_operator(): lax.all_to_all(lap_field, 'term', split_axis=2, concat_axis=0, tiled=True)  40.5 us
    dot_general x12, matrix products, coupling(): jnp.dot(tables[variable], flat, precision=lax.Precision.HIGHEST, preferre...  38.3 us
    all_to_all x1, waiting for transfers between devices, apply_operator(): lax.all_to_all(lap_field, 'term', split_axis=2, concat_axis=0, tiled=True)  36 us
    ppermute x2, waiting for transfers between devices, extended_2(): after = lax.ppermute(leading, axis, down)  12.4 us
    concatenate x2, other arithmetic, extended_2(): array = jnp.concatenate([before, array, after], axis=dim)  9.51 us
  transfers between devices with their start and end apart: 5, of which 5 were waited for; matrix products, arithmetic and copies ran while one was open for 0% of the time, Pallas kernels for 0%

commit v1 on v0

v1 whole, which is shorter than its diff:
```python
import math

import jax
import jax.numpy as jnp
from jax import lax
from jax.experimental import pallas as pl
from jax.experimental.pallas import tpu as pltpu
from jax.sharding import Mesh, PartitionSpec as P

DIM = 6
DEG = 3
LOWER = 2.0
UPPER = 72.0

TERMS = 84
T4 = 21
ROWS = 16
LANES = 128
F32 = jnp.float32
VMEM_BYTES = 48 * 1024 * 1024


def compositions(degree_sum, slots_left):
    if slots_left == 1:
        return [[degree_sum]]
    listing = []
    for leading in range(degree_sum, -1, -1):
        for remainder in compositions(degree_sum - leading, slots_left - 1):
            listing.append([leading] + remainder)
    return listing


def couplings(variables, degree):
    indices = []
    for level in range(degree + 1):
        indices.extend(compositions(level, variables))
    place = {tuple(m): n for n, m in enumerate(indices)}
    result = []
    for first in indices:
        rows = []
        for k in range(variables):
            found = []
            for step in (-1, 1):
                other = list(first)
                other[k] += step
                j = place.get(tuple(other))
                if j is not None:
                    n = max(first[k], other[k])
                    found.append((j, n / math.sqrt(4.0 * n * n - 1.0)))
            if found:
                rows.append((k, found))
        result.append(rows)
    return result


def scalars():
    center = 0.5 * (UPPER + LOWER)
    half = 0.5 * (UPPER - LOWER)
    sigma = center / half
    rho0 = 1.0 / sigma
    rho1 = 1.0 / (2.0 * sigma - rho0)
    keep = (1.0 + rho1 * rho0) / center + 2.0 * rho1 / half
    mix = -2.0 * rho1 / half / center
    return keep, mix


COUPLE = couplings(DIM, DEG)
KEEP, MIX = scalars()

ANY = pl.BlockSpec(memory_space=pl.ANY)
SMEM = pl.BlockSpec(memory_space=pltpu.SMEM)


def pack_kernel(s_ref, x_ref, *refs):
    outs = refs[:8]
    xv, hv, sem_in, sem_main, sem_halo = refs[8:]
    plane, band = s_ref[0], s_ref[1]
    load = pltpu.make_async_copy(x_ref.at[:, plane], xv, sem_in)
    load.start()
    load.wait()
    copies = []
    for k in range(8):
        d = jnp.bitwise_xor(band, k)
        start = pl.multiple_of(d * ROWS, ROWS)
        c = pltpu.make_async_copy(
            xv.at[:, pl.ds(start, ROWS), :], outs[k].at[pl.ds(0, T4)], sem_main.at[k]
        )
        c.start()
        copies.append(c)
        above = jnp.maximum(d * ROWS - 1, 0)
        below = jnp.minimum(d * ROWS + ROWS, 127)
        for j in range(T4):
            up = xv[j, pl.ds(above, 1), :]
            dn = xv[j, pl.ds(below, 1), :]
            up = jnp.where(d == 0, jnp.zeros_like(up), up)
            dn = jnp.where(d == 7, jnp.zeros_like(dn), dn)
            a, b = j, 24 + j
            hv[k, a // 16, pl.ds(a % 16, 1), :] = up
            hv[k, b // 16, pl.ds(b % 16, 1), :] = dn
        c = pltpu.make_async_copy(hv.at[k], outs[k].at[pl.ds(T4, 3)], sem_halo.at[k])
        c.start()
        copies.append(c)
    for c in copies:
        c.wait()


def pack(info, x):
    return pl.pallas_call(
        pack_kernel,
        out_shape=[jax.ShapeDtypeStruct((24, ROWS, LANES), F32)] * 8,
        in_specs=[SMEM, ANY],
        out_specs=[ANY] * 8,
        scratch_shapes=[
            pltpu.VMEM((T4, 128, LANES), F32),
            pltpu.VMEM((8, 3, ROWS, LANES), F32),
            pltpu.SemaphoreType.DMA,
            pltpu.SemaphoreType.DMA((8,)),
            pltpu.SemaphoreType.DMA((8,)),
        ],
        compiler_params=pltpu.CompilerParams(vmem_limit_bytes=VMEM_BYTES),
        name="pack",
    )(info, x)


def start_all(pairs, sems):
    copies = [pltpu.make_async_copy(a, b, sems.at[n]) for n, (a, b) in enumerate(pairs)]
    for c in copies:
        c.start()
    return copies


def laplace_plane(v_ref, lap, p, up_row, dn_row):
    row = lax.broadcasted_iota(jnp.int32, (ROWS, LANES), 0)
    lane = lax.broadcasted_iota(jnp.int32, (ROWS, LANES), 1)
    first_row, last_row = row == 0, row == ROWS - 1
    first_lane, last_lane = lane == 0, lane == LANES - 1

    def group(t, carry):
        for jj in range(T4):
            j = t * T4 + jj
            c = v_ref[j, p + 1]
            dn = jnp.where(last_row, dn_row(t, p, jj), pltpu.roll(c, ROWS - 1, 0))
            up = jnp.where(first_row, up_row(t, p, jj), pltpu.roll(c, 1, 0))
            right = jnp.where(last_lane, 0.0, pltpu.roll(c, LANES - 1, 1))
            left = jnp.where(first_lane, 0.0, pltpu.roll(c, 1, 1))
            beside = v_ref[j, p + 2] + v_ref[j, p]
            beside = beside + dn + up
            beside = beside + right + left
            lap[j] = 6.0 * c - beside
        return carry

    lax.fori_loop(0, 4, group, 0)


def coupled(lap, cond, p, i):
    acc = cond[0, p] * lap[i]
    for k, found in COUPLE[i]:
        mixed = None
        for j, weight in found:
            part = weight * lap[j]
            mixed = part if mixed is None else mixed + part
        acc = acc + cond[k + 1, p] * mixed
    return acc


def place_of(s_ref, k):
    h = jnp.bitwise_xor(s_ref[0], k >> 2)
    t = jnp.bitwise_xor(s_ref[1], k & 3)
    return h, t


def conductivity_pairs(s_ref, near, far, cond):
    odd = s_ref[2]
    return [
        (near, cond.at[:, pl.ds(2 * odd, 2)]),
        (far, cond.at[:, pl.ds(2 * (1 - odd), 2)]),
    ]


def first_kernel(s_ref, *refs):
    outer, inner = refs[0:8], refs[8:16]
    zlo, zhi, near, far = refs[16:20]
    outs = refs[20:28]
    z0, z3, y0, y15 = refs[28:32]
    v, halo, lap, out, cond, y0v, y15v, sem_v, sem_h, sem_o, sem_e = refs[32:]
    h = s_ref[0]

    pairs, halos = [], []
    for k in range(8):
        hk, tk = place_of(s_ref, k)
        terms = pl.ds(tk * T4, T4)
        pairs.append((outer[k].at[pl.ds(0, T4)], v.at[terms, 3 * hk + 1]))
        pairs.append((inner[k].at[pl.ds(0, T4)], v.at[terms, 2 + hk]))
        halos.append((outer[k].at[pl.ds(T4, 3)], halo.at[tk, 3 * hk]))
        halos.append((inner[k].at[pl.ds(T4, 3)], halo.at[tk, 1 + hk]))
    for k in range(4):
        tk = jnp.bitwise_xor(s_ref[1], k)
        terms = pl.ds(tk * T4, T4)
        pairs.append((zlo.at[pl.ds(k * T4, T4)], v.at[terms, 5 * (1 - h)]))
        pairs.append((zhi.at[pl.ds(k * T4, T4)], v.at[terms, 5 * h]))
    halos += conductivity_pairs(s_ref, near, far, cond)
    loads = start_all(pairs, sem_v) + start_all(halos, sem_h)
    for c in loads:
        c.wait()

    def up_row(t, p, jj):
        return halo[t, p, jj // 16, pl.ds(jj % 16, 1), :]

    def dn_row(t, p, jj):
        return halo[t, p, (24 + jj) // 16, pl.ds((24 + jj) % 16, 1), :]

    def sends(group):
        result = []
        for kk in range(4):
            k = group * 4 + kk
            hk, tk = place_of(s_ref, k)
            result.append(
                pltpu.make_async_copy(
                    out.at[pl.ds(tk * T4, T4), pl.ds(2 * hk, 2)], outs[k], sem_o.at[k]
                )
            )
        return result

    def plane_step(s, carry):
        p = 2 * jnp.bitwise_xor(h, s // 2) + s % 2
        laplace_plane(v, lap, p, up_row, dn_row)
        for i in range(TERMS):
            value = KEEP * v[i, p + 1] + MIX * coupled(lap, cond, p, i)
            out[i, p] = value
            y0v[i // T4, p, pl.ds(i % T4, 1), :] = value[0:1]
            y15v[i // T4, p, pl.ds(i % T4, 1), :] = value[ROWS - 1 : ROWS]
        for group in range(2):

            @pl.when(s == 2 * group + 1)
            def _():
                for c in sends(group):
                    c.start()

        return carry

    for t in range(4):
        for n in range(4):
            y0v[t, n, T4:24, :] = jnp.zeros((24 - T4, LANES), F32)
            y15v[t, n, T4:24, :] = jnp.zeros((24 - T4, LANES), F32)
    lax.fori_loop(0, 4, plane_step, 0)
    edges = start_all(
        [(out.at[:, 0], z0), (out.at[:, 3], z3), (y0v, y0), (y15v, y15)], sem_e
    )
    for c in edges + sends(0) + sends(1):
        c.wait()


def second_kernel(s_ref, *refs):
    outer, inner, sol = refs[0:8], refs[8:16], refs[16:24]
    below, above, yup, ydn, near, far = refs[24:30]
    outs = refs[30:38]
    v, r, lap, out, cond, upv, dnv, sem_v, sem_e, sem_o = refs[38:]
    h = s_ref[0]

    pairs = []
    for k in range(8):
        hk, tk = place_of(s_ref, k)
        terms = pl.ds(tk * T4, T4)
        pairs.append((sol[k], v.at[terms, pl.ds(2 * hk + 1, 2)]))
        pairs.append((outer[k].at[pl.ds(0, T4)], r.at[terms, 3 * hk]))
        pairs.append((inner[k].at[pl.ds(0, T4)], r.at[terms, 1 + hk]))
    edges = [(below, v.at[:, 0]), (above, v.at[:, 5]), (yup, upv), (ydn, dnv)]
    edges += conductivity_pairs(s_ref, near, far, cond)
    loads = start_all(pairs, sem_v) + start_all(edges, sem_e)
    for c in loads:
        c.wait()

    def up_row(t, p, jj):
        return upv[t, p, pl.ds(jj, 1), :]

    def dn_row(t, p, jj):
        return dnv[t, p, pl.ds(jj, 1), :]

    def sends(group):
        result = []
        for kk in range(4):
            k = group * 4 + kk
            hk, tk = place_of(s_ref, k)
            result.append(
                pltpu.make_async_copy(
                    out.at[pl.ds(tk * T4, T4), pl.ds(2 * hk, 2)], outs[k], sem_o.at[k]
                )
            )
        return result

    def plane_step(s, carry):
        p = 2 * jnp.bitwise_xor(h, s // 2) + s % 2
        laplace_plane(v, lap, p, up_row, dn_row)
        for i in range(TERMS):
            out[i, p] = r[i, p] - coupled(lap, cond, p, i)
        for group in range(2):

            @pl.when(s == 2 * group + 1)
            def _():
                for c in sends(group):
                    c.start()

        return carry

    lax.fori_loop(0, 4, plane_step, 0)
    for c in sends(0) + sends(1):
        c.wait()


PIECE = jax.ShapeDtypeStruct((T4, 2, ROWS, LANES), F32)
FACE = jax.ShapeDtypeStruct((TERMS, ROWS, LANES), F32)
EDGE = jax.ShapeDtypeStruct((4, 4, 24, LANES), F32)


def dma(count):
    return pltpu.SemaphoreType.DMA((count,))


def first(info, *arrays):
    return pl.pallas_call(
        first_kernel,
        out_shape=[PIECE] * 8 + [FACE] * 2 + [EDGE] * 2,
        in_specs=[SMEM] + [ANY] * 20,
        out_specs=[ANY] * 12,
        scratch_shapes=[
            pltpu.VMEM((TERMS, 6, ROWS, LANES), F32),
            pltpu.VMEM((4, 4, 3, ROWS, LANES), F32),
            pltpu.VMEM((TERMS, ROWS, LANES), F32),
            pltpu.VMEM((TERMS, 4, ROWS, LANES), F32),
            pltpu.VMEM((DIM + 1, 4, ROWS, LANES), F32),
            pltpu.VMEM((4, 4, 24, LANES), F32),
            pltpu.VMEM((4, 4, 24, LANES), F32),
            dma(24), dma(18), dma(8), dma(4),
        ],
        compiler_params=pltpu.CompilerParams(vmem_limit_bytes=VMEM_BYTES),
        name="first",
    )(info, *arrays)


def second(info, *arrays):
    return pl.pallas_call(
        second_kernel,
        out_shape=[PIECE] * 8,
        in_specs=[SMEM] + [ANY] * 30,
        out_specs=[ANY] * 8,
        scratch_shapes=[
            pltpu.VMEM((TERMS, 6, ROWS, LANES), F32),
            pltpu.VMEM((TERMS, 4, ROWS, LANES), F32),
            pltpu.VMEM((TERMS, ROWS, LANES), F32),
            pltpu.VMEM((TERMS, 4, ROWS, LANES), F32),
            pltpu.VMEM((DIM + 1, 4, ROWS, LANES), F32),
            pltpu.VMEM((4, 4, 24, LANES), F32),
            pltpu.VMEM((4, 4, 24, LANES), F32),
            dma(24), dma(6), dma(8),
        ],
        compiler_params=pltpu.CompilerParams(vmem_limit_bytes=VMEM_BYTES),
        name="second",
    )(info, *arrays)


BAND = ("half", "term")
ORDER = (4, 6, 2, 5, 7, 3, 1)


def exchange(pieces):
    got = [None] * 8
    got[0] = pieces[0]
    for k in ORDER:
        got[k] = lax.ppermute(pieces[k], BAND, [(i, i ^ k) for i in range(8)])
    return got


def unpacked(got, band):
    whole = jnp.zeros((T4, 2, 128, LANES), F32)
    for k in range(8):
        start = jnp.bitwise_xor(band, k) * ROWS
        whole = lax.dynamic_update_slice(whole, got[k], (0, 0, start, 0))
    return whole


def shards(right_side, mean_cond, cond_terms):
    quads = lax.axis_size("quad")
    band = lax.axis_index(BAND)
    h, t = band // 4, band % 4
    info = jnp.stack([h, t, band % 2]).astype(jnp.int32)

    outer = exchange(pack(jnp.stack([h, band]).astype(jnp.int32), right_side))
    inner = exchange(pack(jnp.stack([1 - h, band]).astype(jnp.int32), right_side))

    local = jnp.concatenate([mean_cond[None], cond_terms], axis=0)
    own = lax.dynamic_slice_in_dim(local, h * ROWS, ROWS, axis=2)
    rest = lax.dynamic_slice_in_dim(local, (1 - h) * ROWS, ROWS, axis=2)
    near = lax.ppermute(own, BAND, [(4 * a + b, 2 * b + a) for a in range(2) for b in range(4)])
    far = lax.ppermute(rest, BAND, [(4 * a + b, 2 * b + 1 - a) for a in range(2) for b in range(4)])

    def z_shift(arrays, lower_half):
        face = jnp.concatenate([a[:T4] for a in arrays], axis=0)
        pairs = []
        for q in range(quads):
            for b in range(8):
                other = q - 1 if (b // 4) == lower_half else q + 1
                if 0 <= other < quads:
                    pairs.append((q * 8 + b, other * 8 + b))
        return lax.ppermute(face, ("quad", "half", "term"), pairs)

    zlo = z_shift(outer[0:4], 0)
    zhi = z_shift(outer[4:8], 1)

    made = first(info, *outer, *inner, zlo, zhi, near, far)
    sol, (z0, z3, y0, y15) = made[:8], made[8:]

    up = [(i, i + 1) for i in range(quads - 1)]
    down = [(i + 1, i) for i in range(quads - 1)]
    below = lax.ppermute(z3, "quad", up)
    above = lax.ppermute(z0, "quad", down)
    yup = lax.ppermute(y15, BAND, [(i, i + 1) for i in range(7)])
    ydn = lax.ppermute(y0, BAND, [(i + 1, i) for i in range(7)])

    solution = unpacked(exchange(sol), band)
    res = second(info, *outer, *inner, *sol, below, above, yup, ydn, near, far)
    residual = unpacked(exchange(res), band)
    return (solution, residual)


def solution(mesh):
    grid = Mesh(mesh.devices.reshape(-1, 2, 4), ("quad", "half", "term"))
    field = P("term", ("quad", "half"), None, None)
    return jax.shard_map(
        shards,
        mesh=grid,
        in_specs=(field, P(("quad", "half"), "term", None), P(None, ("quad", "half"), "term", None)),
        out_specs=(field, field),
        check_vma=False,
    )
```

time: 378 us -> 185 us (0.49)
  the two profiles are of different devices: /device:TPU:1 before, /device:TPU:25 now
where the time goes in v1:
time: 185 us
  waiting for transfers between devices  76.8 us (42%)
  starting transfers between devices  70.9 us (38%)
  Pallas kernels  19.1 us (10%)
  local copies, waits for them, and re-layouts  14.9 us (8%)
  other arithmetic  1.97 us (1%)
    ppermute x28, waiting for transfers between devices, exchange(): got[k] = lax.ppermute(pieces[k], BAND, [(i, i ^ k) for i in range(8)])  72.4 us
    ppermute x28, starting transfers between devices, exchange(): got[k] = lax.ppermute(pieces[k], BAND, [(i, i ^ k) for i in range(8)])  45.4 us
    unnamed x52, local copies, waits for them, and re-layouts  11.7 us
    ppermute x2, starting transfers between devices, z_shift(): return lax.ppermute(face, ('quad', 'half', 'term'), pairs)  9.7 us
    pallas_call x1, Pallas kernels, first(): pl.pallas_call(first_kernel, out_shape=[PIECE] * 8 + [FACE] * 2 + [EDGE]...  8.13 us
    pallas_call x1, Pallas kernels, second(): pl.pallas_call(second_kernel, out_shape=[PIECE] * 8, in_specs=[SMEM] + [A...  7.83 us
    ppermute x1, starting transfers between devices, shards(): above = lax.ppermute(z0, 'quad', down)  5.47 us
    ppermute x1, waiting for transfers between devices, shards(): lax.ppermute(own, BAND, [(4 * a + b, 2 * b + a) for a in range(2) for b i...  3.73 us
  transfers between devices with their start and end apart: 36, of which 19 were waited for; matrix products, arithmetic and copies ran while one was open for 3% of the time, Pallas kernels for 5%

profile of v1, /device:TPU:25, one launch (start us, length us, event | category | flops | bytes accessed | tf_op | source)
XLA Modules:
  0.0 184.8 jit_solution(18122837211260323184)
XLA Ops:
  4.0 2.8 %collective-permute-start.3 = (f32[24,16,128]{2,1,0:T(8,128)S(1)}, f32[24,16,128]{2,1,0:T(8,128)S(1)}, u32[]{:S(2)}, u32[]{:S(2)}) collective-permute-start(f32[24,16,128]{2,1,0:T(8,128)S(1)} %get-tuple-element.42), channel_id=1, source_target_pairs={{0,4},{1,5},{2,6},{3,7},{4,0},{5,1},{6,2},{7,3},{8,12},{9,13},{10,... | collective-permute-start | bytes 589832 | tf_op jit(solution)/shard_map/ppermute | solution.py:369
  12.6 4.3 %collective-permute-done.4.refs_5_ = f32[24,16,128]{2,1,0:T(8,128)S(1)} collective-permute-done((f32[24,16,128]{2,1,0:T(8,128)S(1)}, f32[24,16,128]{2,1,0:T(8,128)S(1)}, u32[]{:S(2)}, u32[]{:S(2)}) %collective-permute-start.4) | collective-permute-done | bytes 196640 | tf_op jit(solution)/shard_map/ppermute | solution.py:369
  17.6 3.3 %collective-permute-done.5.refs_6_ = f32[24,16,128]{2,1,0:T(8,128)S(1)} collective-permute-done((f32[24,16,128]{2,1,0:T(8,128)S(1)}, f32[24,16,128]{2,1,0:T(8,128)S(1)}, u32[]{:S(2)}, u32[]{:S(2)}) %collective-permute-start.5) | collective-permute-done | bytes 196640 | tf_op jit(solution)/shard_map/ppermute | solution.py:369
  20.9 4.2 %collective-permute-done.6.refs_7_ = f32[24,16,128]{2,1,0:T(8,128)S(1)} collective-permute-done((f32[24,16,128]{2,1,0:T(8,128)S(1)}, f32[24,16,128]{2,1,0:T(8,128)S(1)}, u32[]{:S(2)}, u32[]{:S(2)}) %collective-permute-start.6) | collective-permute-done | bytes 196640 | tf_op jit(solution)/shard_map/ppermute | solution.py:369
  26.0 3.7 %collective-permute-start.15 = (f32[84,16,128]{2,1,0:T(8,128)}, f32[84,16,128]{2,1,0:T(8,128)}, u32[]{:S(2)}, u32[]{:S(2)}) collective-permute-start(f32[84,16,128]{2,1,0:T(8,128)} %pad_maximum_fusion.1), channel_id=1, source_target_pairs={{0,8},{1,9},{2,10},{3,11},{8,16},{9,17},{10,18},{11,19},{12,4},{13... | collective-permute-start | bytes 2064392 | tf_op jit(solution)/shard_map/ppermute | solution.py:404
  30.7 6.0 %collective-permute-start.14 = (f32[84,16,128]{2,1,0:T(8,128)}, f32[84,16,128]{2,1,0:T(8,128)}, u32[]{:S(2)}, u32[]{:S(2)}) collective-permute-start(f32[84,16,128]{2,1,0:T(8,128)} %pad_maximum_fusion), channel_id=1, source_target_pairs={{4,12},{5,13},{6,14},{7,15},{8,0},{9,1},{10,2},{11,3},{12,20},{13,... | collective-permute-start | bytes 2064392 | tf_op jit(solution)/shard_map/ppermute | solution.py:404
  38.4 2.9 %collective-permute-start.10 = (f32[24,16,128]{2,1,0:T(8,128)S(1)}, f32[24,16,128]{2,1,0:T(8,128)S(1)}, u32[]{:S(2)}, u32[]{:S(2)}) collective-permute-start(f32[24,16,128]{2,1,0:T(8,128)S(1)} %get-tuple-element.50), channel_id=1, source_target_pairs={{0,4},{1,5},{2,6},{3,7},{4,0},{5,1},{6,2},{7,3},{8,12},{9,13},{10,... | collective-permute-start | bytes 589832 | tf_op jit(solution)/shard_map/ppermute | solution.py:369
  41.3 3.1 %collective-permute-start.16 = (f32[7,2,16,128]{3,2,1,0:T(8,128)S(1)}, f32[7,2,16,128]{3,2,1,0:T(8,128)S(1)}, u32[]{:S(2)}, u32[]{:S(2)}) collective-permute-start(f32[7,2,16,128]{3,2,1,0:T(8,128)S(1)} %get-tuple-element.75), channel_id=1, source_target_pairs={{0,0},{1,2},{2,4},{3,6},{4,1},{5,3},{6,5},{7,7},{8,8},{9,10},{10,1... | collective-permute-start | bytes 344072 | tf_op jit(solution)/shard_map/ppermute | solution.py:393
  45.6 3.7 %collective-permute-done.16.refs_18_.refs_28_ = f32[7,2,16,128]{3,2,1,0:T(8,128)S(1)} collective-permute-done((f32[7,2,16,128]{3,2,1,0:T(8,128)S(1)}, f32[7,2,16,128]{3,2,1,0:T(8,128)S(1)}, u32[]{:S(2)}, u32[]{:S(2)}) %collective-permute-start.16) | collective-permute-done | bytes 114720 | tf_op jit(solution)/shard_map/ppermute | solution.py:393
  56.6 4.4 %collective-permute-done.12.refs_14_ = f32[24,16,128]{2,1,0:T(8,128)S(1)} collective-permute-done((f32[24,16,128]{2,1,0:T(8,128)S(1)}, f32[24,16,128]{2,1,0:T(8,128)S(1)}, u32[]{:S(2)}, u32[]{:S(2)}) %collective-permute-start.12) | collective-permute-done | bytes 196640 | tf_op jit(solution)/shard_map/ppermute | solution.py:369
  68.1 4.4 %collective-permute-done.9.refs_11_ = f32[24,16,128]{2,1,0:T(8,128)S(1)} collective-permute-done((f32[24,16,128]{2,1,0:T(8,128)S(1)}, f32[24,16,128]{2,1,0:T(8,128)S(1)}, u32[]{:S(2)}, u32[]{:S(2)}) %collective-permute-start.9) | collective-permute-done | bytes 196640 | tf_op jit(solution)/shard_map/ppermute | solution.py:369
  74.3 8.1 %first.1 = (f32[21,2,16,128]{3,2,1,0:T(8,128)S(1)}, f32[21,2,16,128]{3,2,1,0:T(8,128)}, f32[21,2,16,128]{3,2,1,0:T(8,128)}, f32[21,2,16,128]{3,2,1,0:T(8,128)S(1...) custom-call(s32[3]{0:T(128)S(1)} %pad_add_fusion.s_ref, ...), custom_call_target="tpu_custom_call" | custom-call | tf_op jit(solution)/shard_map/first/pallas_call | solution.py:320
  92.2 5.5 %collective-permute-start.26 = (f32[84,16,128]{2,1,0:T(8,128)}, f32[84,16,128]{2,1,0:T(8,128)S(1)}, u32[]{:S(2)}, u32[]{:S(2)}) collective-permute-start(f32[84,16,128]{2,1,0:T(8,128)} %get-tuple-element.63), channel_id=1, source_target_pairs={{8,0},{16,8},{24,16},{32,24},{40,32},{48,40},{56,48},{64,56},{72,6... | collective-permute-start | bytes 2064392 | tf_op jit(solution)/shard_map/ppermute | solution.py:415
  105.1 4.8 %collective-permute-done.20 = f32[21,2,16,128]{3,2,1,0:T(8,128)S(1)} collective-permute-done((f32[21,2,16,128]{3,2,1,0:T(8,128)}, f32[21,2,16,128]{3,2,1,0:T(8,128)S(1)}, u32[]{:S(2)}, u32[]{:S(2)}) %collective-permute-start.20) | collective-permute-done | bytes 344096 | tf_op jit(solution)/shard_map/ppermute | solution.py:369
  110.0 7.8 %collective-permute-done.21 = f32[21,2,16,128]{3,2,1,0:T(8,128)S(1)} collective-permute-done((f32[21,2,16,128]{3,2,1,0:T(8,128)S(1)}, f32[21,2,16,128]{3,2,1,0:T(8,128)S(1)}, u32[]{:S(2)}, u32[]{:S(2)}) %collective-permute-start.21) | collective-permute-done | bytes 344096 | tf_op jit(solution)/shard_map/ppermute | solution.py:369
  119.7 2.7 %collective-permute-done.22 = f32[21,2,16,128]{3,2,1,0:T(8,128)S(1)} collective-permute-done((f32[21,2,16,128]{3,2,1,0:T(8,128)S(1)}, f32[21,2,16,128]{3,2,1,0:T(8,128)S(1)}, u32[]{:S(2)}, u32[]{:S(2)}) %collective-permute-start.22) | collective-permute-done | bytes 344096 | tf_op jit(solution)/shard_map/ppermute | solution.py:369
  122.4 4.3 %collective-permute-start.24 = (f32[21,2,16,128]{3,2,1,0:T(8,128)S(1)}, f32[21,2,16,128]{3,2,1,0:T(8,128)S(1)}, u32[]{:S(2)}, u32[]{:S(2)}) collective-permute-start(f32[21,2,16,128]{3,2,1,0:T(8,128)S(1)} %copy-done.22), channel_id=1, source_target_pairs={{0,7},{1,6},{2,5},{3,4},{4,3},{5,2},{6,1},{7,0},{8,15},{9,14},{10,... | collective-permute-start | bytes 1032200 | tf_op jit(solution)/shard_map/ppermute | solution.py:369
  128.5 7.8 %second.1 = (f32[21,2,16,128]{3,2,1,0:T(8,128)S(1)}, f32[21,2,16,128]{3,2,1,0:T(8,128)S(1)}, f32[21,2,16,128]{3,2,1,0:T(8,128)S(1)}, f32[21,2,16,128]{3,2,1,0:T(...) custom-call(s32[3]{0:T(128)S(1)} %pad_add_fusion.s_ref, ...), custom_call_target="tpu_custom_call" | custom-call | tf_op jit(solution)/shard_map/second/pallas_call | solution.py:341
  136.7 8.7 %collective-permute-start.30 = (f32[21,2,16,128]{3,2,1,0:T(8,128)S(1)}, f32[21,2,16,128]{3,2,1,0:T(8,128)S(1)}, u32[]{:S(2)}, u32[]{:S(2)}) collective-permute-start(f32[21,2,16,128]{3,2,1,0:T(8,128)S(1)} %get-tuple-element.68), channel_id=1, source_target_pairs={{0,2},{1,3},{2,0},{3,1},{4,6},{5,7},{6,4},{7,5},{8,10},{9,11},{10,... | collective-permute-start | bytes 1032200 | tf_op jit(solution)/shard_map/ppermute | solution.py:369
  150.6 2.8 %collective-permute-done.30 = f32[21,2,16,128]{3,2,1,0:T(8,128)S(1)} collective-permute-done((f32[21,2,16,128]{3,2,1,0:T(8,128)S(1)}, f32[21,2,16,128]{3,2,1,0:T(8,128)S(1)}, u32[]{:S(2)}, u32[]{:S(2)}) %collective-permute-start.30) | collective-permute-done | bytes 344096 | tf_op jit(solution)/shard_map/ppermute | solution.py:369
  154.8 7.2 %collective-permute-done.31 = f32[21,2,16,128]{3,2,1,0:T(8,128)S(1)} collective-permute-done((f32[21,2,16,128]{3,2,1,0:T(8,128)S(1)}, f32[21,2,16,128]{3,2,1,0:T(8,128)S(1)}, u32[]{:S(2)}, u32[]{:S(2)}) %collective-permute-start.31) | collective-permute-done | bytes 344096 | tf_op jit(solution)/shard_map/ppermute | solution.py:369
  162.1 6.5 %collective-permute-done.32 = f32[21,2,16,128]{3,2,1,0:T(8,128)S(1)} collective-permute-done((f32[21,2,16,128]{3,2,1,0:T(8,128)S(1)}, f32[21,2,16,128]{3,2,1,0:T(8,128)S(1)}, u32[]{:S(2)}, u32[]{:S(2)}) %collective-permute-start.32) | collective-permute-done | bytes 344096 | tf_op jit(solution)/shard_map/ppermute | solution.py:369
  168.6 7.3 %collective-permute-done.33 = f32[21,2,16,128]{3,2,1,0:T(8,128)S(1)} collective-permute-done((f32[21,2,16,128]{3,2,1,0:T(8,128)S(1)}, f32[21,2,16,128]{3,2,1,0:T(8,128)S(1)}, u32[]{:S(2)}, u32[]{:S(2)}) %collective-permute-start.33) | collective-permute-done | bytes 344096 | tf_op jit(solution)/shard_map/ppermute | solution.py:369
  176.1 7.2 %collective-permute-done.35 = f32[21,2,16,128]{3,2,1,0:T(8,128)S(1)} collective-permute-done((f32[21,2,16,128]{3,2,1,0:T(8,128)S(1)}, f32[21,2,16,128]{3,2,1,0:T(8,128)S(1)}, u32[]{:S(2)}, u32[]{:S(2)}) %collective-permute-start.35) | collective-permute-done | bytes 344096 | tf_op jit(solution)/shard_map/ppermute | solution.py:369
  (135 shorter events, 59.9 us)
Async XLA Ops:
  7.9 13.0 %collective-permute-start.5 = (f32[24,16,128]{2,1,0:T(8,128)S(1)}, f32[24,16,128]{2,1,0:T(8,128)S(1)}, u32[]{:S(2)}, u32[]{:S(2)}) collective-permute-start(f32[24,16,128]{2,1,0:T(8,128)S(1)} %get-tuple-element.44), channel_id=1, source_target_pairs={{0,6},{1,7},{2,4},{3,5},{4,2},{5,3},{6,0},{7,1},{8,14},{9,15},{10,... | collective-permute-start | bytes 589832 | tf_op jit(solution)/shard_map/ppermute | solution.py:369
  10.4 14.7 %collective-permute-start.6 = (f32[24,16,128]{2,1,0:T(8,128)S(1)}, f32[24,16,128]{2,1,0:T(8,128)S(1)}, u32[]{:S(2)}, u32[]{:S(2)}) collective-permute-start(f32[24,16,128]{2,1,0:T(8,128)S(1)} %get-tuple-element.45), channel_id=1, source_target_pairs={{0,7},{1,6},{2,5},{3,4},{4,3},{5,2},{6,1},{7,0},{8,15},{9,14},{10,... | collective-permute-start | bytes 589832 | tf_op jit(solution)/shard_map/ppermute | solution.py:369
  10.6 19.1 %collective-permute-start = (f32[24,16,128]{2,1,0:T(8,128)S(1)}, f32[24,16,128]{2,1,0:T(8,128)S(1)}, u32[]{:S(2)}, u32[]{:S(2)}) collective-permute-start(f32[24,16,128]{2,1,0:T(8,128)S(1)} %get-tuple-element.39), channel_id=1, source_target_pairs={{0,1},{1,0},{2,3},{3,2},{4,5},{5,4},{6,7},{7,6},{8,9},{9,8},{10,11... | collective-permute-start | bytes 589832 | tf_op jit(solution)/shard_map/ppermute | solution.py:369
  11.3 18.4 %collective-permute-start.1 = (f32[24,16,128]{2,1,0:T(8,128)S(1)}, f32[24,16,128]{2,1,0:T(8,128)S(1)}, u32[]{:S(2)}, u32[]{:S(2)}) collective-permute-start(f32[24,16,128]{2,1,0:T(8,128)S(1)} %get-tuple-element.40), channel_id=1, source_target_pairs={{0,2},{1,3},{2,0},{3,1},{4,6},{5,7},{6,4},{7,5},{8,10},{9,11},{10,... | collective-permute-start | bytes 589832 | tf_op jit(solution)/shard_map/ppermute | solution.py:369
  16.9 12.9 %collective-permute-start.2 = (f32[24,16,128]{2,1,0:T(8,128)S(1)}, f32[24,16,128]{2,1,0:T(8,128)S(1)}, u32[]{:S(2)}, u32[]{:S(2)}) collective-permute-start(f32[24,16,128]{2,1,0:T(8,128)S(1)} %get-tuple-element.41), channel_id=1, source_target_pairs={{0,3},{1,2},{2,1},{3,0},{4,7},{5,6},{6,5},{7,4},{8,11},{9,10},{10,... | collective-permute-start | bytes 589832 | tf_op jit(solution)/shard_map/ppermute | solution.py:369
  26.0 46.5 %collective-permute-start.15 = (f32[84,16,128]{2,1,0:T(8,128)}, f32[84,16,128]{2,1,0:T(8,128)}, u32[]{:S(2)}, u32[]{:S(2)}) collective-permute-start(f32[84,16,128]{2,1,0:T(8,128)} %pad_maximum_fusion.1), channel_id=1, source_target_pairs={{0,8},{1,9},{2,10},{3,11},{8,16},{9,17},{10,18},{11,19},{12,4},{13... | collective-permute-start | bytes 2064392 | tf_op jit(solution)/shard_map/ppermute | solution.py:404
  30.7 41.8 %collective-permute-start.14 = (f32[84,16,128]{2,1,0:T(8,128)}, f32[84,16,128]{2,1,0:T(8,128)}, u32[]{:S(2)}, u32[]{:S(2)}) collective-permute-start(f32[84,16,128]{2,1,0:T(8,128)} %pad_maximum_fusion), channel_id=1, source_target_pairs={{4,12},{5,13},{6,14},{7,15},{8,0},{9,1},{10,2},{11,3},{12,20},{13,... | collective-permute-start | bytes 2064392 | tf_op jit(solution)/shard_map/ppermute | solution.py:404
  38.4 15.0 %collective-permute-start.10 = (f32[24,16,128]{2,1,0:T(8,128)S(1)}, f32[24,16,128]{2,1,0:T(8,128)S(1)}, u32[]{:S(2)}, u32[]{:S(2)}) collective-permute-start(f32[24,16,128]{2,1,0:T(8,128)S(1)} %get-tuple-element.50), channel_id=1, source_target_pairs={{0,4},{1,5},{2,6},{3,7},{4,0},{5,1},{6,2},{7,3},{8,12},{9,13},{10,... | collective-permute-start | bytes 589832 | tf_op jit(solution)/shard_map/ppermute | solution.py:369
  53.4 11.9 %collective-permute-start.13 = (f32[24,16,128]{2,1,0:T(8,128)S(1)}, f32[24,16,128]{2,1,0:T(8,128)S(1)}, u32[]{:S(2)}, u32[]{:S(2)}) collective-permute-start(f32[24,16,128]{2,1,0:T(8,128)S(1)} %get-tuple-element.53), channel_id=1, source_target_pairs={{0,7},{1,6},{2,5},{3,4},{4,3},{5,2},{6,1},{7,0},{8,15},{9,14},{10,... | collective-permute-start | bytes 589832 | tf_op jit(solution)/shard_map/ppermute | solution.py:369
  86.1 15.2 %collective-permute-start.18 = (f32[21,2,16,128]{3,2,1,0:T(8,128)}, f32[21,2,16,128]{3,2,1,0:T(8,128)}, u32[]{:S(2)}, u32[]{:S(2)}) collective-permute-start(f32[21,2,16,128]{3,2,1,0:T(8,128)} %get-tuple-element.55.refs_17_), channel_id=1, source_target_pairs={{0,1},{1,0},{2,3},{3,2},{4,5},{5,4},{6,7},{7,6},{8,9},{9,8},{10,11... | collective-permute-start | bytes 1032200 | tf_op jit(solution)/shard_map/ppermute | solution.py:369
  86.4 15.8 %collective-permute-start.19 = (f32[21,2,16,128]{3,2,1,0:T(8,128)}, f32[21,2,16,128]{3,2,1,0:T(8,128)}, u32[]{:S(2)}, u32[]{:S(2)}) collective-permute-start(f32[21,2,16,128]{3,2,1,0:T(8,128)} %get-tuple-element.56.refs_18_), channel_id=1, source_target_pairs={{0,2},{1,3},{2,0},{3,1},{4,6},{5,7},{6,4},{7,5},{8,10},{9,11},{10,... | collective-permute-start | bytes 1032200 | tf_op jit(solution)/shard_map/ppermute | solution.py:369
  90.2 36.6 %collective-permute-start.25 = (f32[84,16,128]{2,1,0:T(8,128)}, f32[84,16,128]{2,1,0:T(8,128)S(1)}, u32[]{:S(2)}, u32[]{:S(2)}) collective-permute-start(f32[84,16,128]{2,1,0:T(8,128)} %get-tuple-element.62), channel_id=1, source_target_pairs={{0,8},{8,16},{16,24},{24,32},{32,40},{40,48},{48,56},{56,64},{64,7... | collective-permute-start | bytes 2064392 | tf_op jit(solution)/shard_map/ppermute | solution.py:414
  92.2 34.6 %collective-permute-start.26 = (f32[84,16,128]{2,1,0:T(8,128)}, f32[84,16,128]{2,1,0:T(8,128)S(1)}, u32[]{:S(2)}, u32[]{:S(2)}) collective-permute-start(f32[84,16,128]{2,1,0:T(8,128)} %get-tuple-element.63), channel_id=1, source_target_pairs={{8,0},{16,8},{24,16},{32,24},{40,32},{48,40},{56,48},{64,56},{72,6... | collective-permute-start | bytes 2064392 | tf_op jit(solution)/shard_map/ppermute | solution.py:415
  101.3 16.5 %collective-permute-start.21 = (f32[21,2,16,128]{3,2,1,0:T(8,128)S(1)}, f32[21,2,16,128]{3,2,1,0:T(8,128)S(1)}, u32[]{:S(2)}, u32[]{:S(2)}) collective-permute-start(f32[21,2,16,128]{3,2,1,0:T(8,128)S(1)} %copy-done.13), channel_id=1, source_target_pairs={{0,4},{1,5},{2,6},{3,7},{4,0},{5,1},{6,2},{7,3},{8,12},{9,13},{10,... | collective-permute-start | bytes 1032200 | tf_op jit(solution)/shard_map/ppermute | solution.py:369
  102.2 20.2 %collective-permute-start.22 = (f32[21,2,16,128]{3,2,1,0:T(8,128)S(1)}, f32[21,2,16,128]{3,2,1,0:T(8,128)S(1)}, u32[]{:S(2)}, u32[]{:S(2)}) collective-permute-start(f32[21,2,16,128]{3,2,1,0:T(8,128)S(1)} %copy-done.15), channel_id=1, source_target_pairs={{0,5},{1,4},{2,7},{3,6},{4,1},{5,0},{6,3},{7,2},{8,13},{9,12},{10,... | collective-permute-start | bytes 1032200 | tf_op jit(solution)/shard_map/ppermute | solution.py:369
  109.9 26.7 %collective-permute-start.23 = (f32[21,2,16,128]{3,2,1,0:T(8,128)S(1)}, f32[21,2,16,128]{3,2,1,0:T(8,128)S(1)}, u32[]{:S(2)}, u32[]{:S(2)}) collective-permute-start(f32[21,2,16,128]{3,2,1,0:T(8,128)S(1)} %copy-done.10), channel_id=1, source_target_pairs={{0,6},{1,7},{2,4},{3,5},{4,2},{5,3},{6,0},{7,1},{8,14},{9,15},{10,... | collective-permute-start | bytes 1032200 | tf_op jit(solution)/shard_map/ppermute | solution.py:369
  122.4 23.0 %collective-permute-start.24 = (f32[21,2,16,128]{3,2,1,0:T(8,128)S(1)}, f32[21,2,16,128]{3,2,1,0:T(8,128)S(1)}, u32[]{:S(2)}, u32[]{:S(2)}) collective-permute-start(f32[21,2,16,128]{3,2,1,0:T(8,128)S(1)} %copy-done.22), channel_id=1, source_target_pairs={{0,7},{1,6},{2,5},{3,4},{4,3},{5,2},{6,1},{7,0},{8,15},{9,14},{10,... | collective-permute-start | bytes 1032200 | tf_op jit(solution)/shard_map/ppermute | solution.py:369
  136.4 13.6 %collective-permute-start.29 = (f32[21,2,16,128]{3,2,1,0:T(8,128)S(1)}, f32[21,2,16,128]{3,2,1,0:T(8,128)S(1)}, u32[]{:S(2)}, u32[]{:S(2)}) collective-permute-start(f32[21,2,16,128]{3,2,1,0:T(8,128)S(1)} %get-tuple-element.67), channel_id=1, source_target_pairs={{0,1},{1,0},{2,3},{3,2},{4,5},{5,4},{6,7},{7,6},{8,9},{9,8},{10,11... | collective-permute-start | bytes 1032200 | tf_op jit(solution)/shard_map/ppermute | solution.py:369
  136.7 16.7 %collective-permute-start.30 = (f32[21,2,16,128]{3,2,1,0:T(8,128)S(1)}, f32[21,2,16,128]{3,2,1,0:T(8,128)S(1)}, u32[]{:S(2)}, u32[]{:S(2)}) collective-permute-start(f32[21,2,16,128]{3,2,1,0:T(8,128)S(1)} %get-tuple-element.68), channel_id=1, source_target_pairs={{0,2},{1,3},{2,0},{3,1},{4,6},{5,7},{6,4},{7,5},{8,10},{9,11},{10,... | collective-permute-start | bytes 1032200 | tf_op jit(solution)/shard_map/ppermute | solution.py:369
  145.5 16.6 %collective-permute-start.31 = (f32[21,2,16,128]{3,2,1,0:T(8,128)S(1)}, f32[21,2,16,128]{3,2,1,0:T(8,128)S(1)}, u32[]{:S(2)}, u32[]{:S(2)}) collective-permute-start(f32[21,2,16,128]{3,2,1,0:T(8,128)S(1)} %get-tuple-element.69), channel_id=1, source_target_pairs={{0,3},{1,2},{2,1},{3,0},{4,7},{5,6},{6,5},{7,4},{8,11},{9,10},{10,... | collective-permute-start | bytes 1032200 | tf_op jit(solution)/shard_map/ppermute | solution.py:369
  146.0 22.6 %collective-permute-start.32 = (f32[21,2,16,128]{3,2,1,0:T(8,128)S(1)}, f32[21,2,16,128]{3,2,1,0:T(8,128)S(1)}, u32[]{:S(2)}, u32[]{:S(2)}) collective-permute-start(f32[21,2,16,128]{3,2,1,0:T(8,128)S(1)} %get-tuple-element.70), channel_id=1, source_target_pairs={{0,4},{1,5},{2,6},{3,7},{4,0},{5,1},{6,2},{7,3},{8,12},{9,13},{10,... | collective-permute-start | bytes 1032200 | tf_op jit(solution)/shard_map/ppermute | solution.py:369
  147.2 28.8 %collective-permute-start.33 = (f32[21,2,16,128]{3,2,1,0:T(8,128)S(1)}, f32[21,2,16,128]{3,2,1,0:T(8,128)S(1)}, u32[]{:S(2)}, u32[]{:S(2)}) collective-permute-start(f32[21,2,16,128]{3,2,1,0:T(8,128)S(1)} %get-tuple-element.71), channel_id=1, source_target_pairs={{0,5},{1,4},{2,7},{3,6},{4,1},{5,0},{6,3},{7,2},{8,13},{9,12},{10,... | collective-permute-start | bytes 1032200 | tf_op jit(solution)/shard_map/ppermute | solution.py:369
  149.9 26.1 %collective-permute-start.34 = (f32[21,2,16,128]{3,2,1,0:T(8,128)S(1)}, f32[21,2,16,128]{3,2,1,0:T(8,128)S(1)}, u32[]{:S(2)}, u32[]{:S(2)}) collective-permute-start(f32[21,2,16,128]{3,2,1,0:T(8,128)S(1)} %get-tuple-element.72), channel_id=1, source_target_pairs={{0,6},{1,7},{2,4},{3,5},{4,2},{5,3},{6,0},{7,1},{8,14},{9,15},{10,... | collective-permute-start | bytes 1032200 | tf_op jit(solution)/shard_map/ppermute | solution.py:369
  153.4 29.8 %collective-permute-start.35 = (f32[21,2,16,128]{3,2,1,0:T(8,128)S(1)}, f32[21,2,16,128]{3,2,1,0:T(8,128)S(1)}, u32[]{:S(2)}, u32[]{:S(2)}) collective-permute-start(f32[21,2,16,128]{3,2,1,0:T(8,128)S(1)} %copy-done.25), channel_id=1, source_target_pairs={{0,7},{1,6},{2,5},{3,4},{4,3},{5,2},{6,1},{7,0},{8,15},{9,14},{10,... | collective-permute-start | bytes 1032200 | tf_op jit(solution)/shard_map/ppermute | solution.py:369
  (38 other events, 359.2 us)

commit v2 on v1

v2 whole, which is shorter than its diff:
```python
import functools
import math

import jax
import jax.numpy as jnp
from jax import lax
from jax.experimental import pallas as pl
from jax.experimental.pallas import tpu as pltpu
from jax.sharding import Mesh, PartitionSpec as P

DIM = 6
DEG = 3
LOWER = 2.0
UPPER = 72.0

TERMS = 84
T4 = 21
ROWS = 16
LANES = 128
F32 = jnp.float32
WEIGHT = pl.CostEstimate(flops=10**12, transcendentals=0, bytes_accessed=10**9)
VMEM_BYTES = 20 * 1024 * 1024


def compositions(degree_sum, slots_left):
    if slots_left == 1:
        return [[degree_sum]]
    listing = []
    for leading in range(degree_sum, -1, -1):
        for remainder in compositions(degree_sum - leading, slots_left - 1):
            listing.append([leading] + remainder)
    return listing


def couplings(variables, degree):
    indices = []
    for level in range(degree + 1):
        indices.extend(compositions(level, variables))
    place = {tuple(m): n for n, m in enumerate(indices)}
    result = []
    for first in indices:
        found = []
        for k in range(variables):
            for step in (-1, 1):
                other = list(first)
                other[k] += step
                j = place.get(tuple(other))
                if j is not None:
                    found.append((j, k, max(first[k], other[k])))
        result.append(found)
    return result


def scalars():
    center = 0.5 * (UPPER + LOWER)
    half = 0.5 * (UPPER - LOWER)
    sigma = center / half
    rho0 = 1.0 / sigma
    rho1 = 1.0 / (2.0 * sigma - rho0)
    keep = (1.0 + rho1 * rho0) / center + 2.0 * rho1 / half
    mix = -2.0 * rho1 / half / center
    return keep, mix


COUPLE = couplings(DIM, DEG)
MEANS = [n / math.sqrt(4.0 * n * n - 1.0) for n in range(1, DEG + 1)]
KEEP, MIX = scalars()

HBM = pl.BlockSpec(memory_space=pltpu.HBM)
SMEM = pl.BlockSpec(memory_space=pltpu.SMEM)
BANDS = 8


def held(*shape):
    return pltpu.HBM(shape, F32)


def fixed(array):
    return pltpu.with_memory_space_constraint(array, pltpu.HBM)


def dma(count):
    return pltpu.SemaphoreType.DMA((count,))


def pack_kernel(split, s_ref, x_ref, *refs):
    count = BANDS if split else 1
    outs, (xv, hv, sem_in, sem_main, sem_halo) = refs[:count], refs[count:]
    h = s_ref[0]
    band = 4 * h + s_ref[1]
    load = pltpu.make_async_copy(x_ref.at[:, h if split else 1 - h], xv, sem_in)
    load.start()
    load.wait()
    copies = []
    for k in range(BANDS):
        if split:
            d, out = jnp.bitwise_xor(band, k), outs[k]
            rows = pl.ds(pl.multiple_of(d * ROWS, ROWS), ROWS)
            above = jnp.maximum(d * ROWS - 1, 0)
            below = jnp.minimum(d * ROWS + ROWS, 127)
        else:
            d, out = k, outs[0].at[k]
            rows = pl.ds(d * ROWS, ROWS)
            above, below = max(d * ROWS - 1, 0), min(d * ROWS + ROWS, 127)
        c = pltpu.make_async_copy(xv.at[:, rows, :], out.at[pl.ds(0, T4)], sem_main.at[k])
        c.start()
        copies.append(c)
        for j in range(T4):
            up = xv[j, pl.ds(above, 1), :]
            dn = xv[j, pl.ds(below, 1), :]
            up = jnp.where(d == 0, jnp.zeros_like(up), up)
            dn = jnp.where(d == BANDS - 1, jnp.zeros_like(dn), dn)
            a, b = j, 24 + j
            hv[k, a // 16, pl.ds(a % 16, 1), :] = up
            hv[k, b // 16, pl.ds(b % 16, 1), :] = dn
        c = pltpu.make_async_copy(hv.at[k], out.at[pl.ds(T4, 3)], sem_halo.at[k])
        c.start()
        copies.append(c)
    for c in copies:
        c.wait()


def pack(split, info, x):
    return pl.pallas_call(
        functools.partial(pack_kernel, split),
        out_shape=[held(24, ROWS, LANES)] * BANDS if split else [held(BANDS, 24, ROWS, LANES)],
        in_specs=[SMEM, HBM],
        out_specs=[HBM] * (BANDS if split else 1),
        scratch_shapes=[
            pltpu.VMEM((T4, 128, LANES), F32),
            pltpu.VMEM((BANDS, 3, ROWS, LANES), F32),
            pltpu.SemaphoreType.DMA, dma(8), dma(8),
        ],
        compiler_params=pltpu.CompilerParams(vmem_limit_bytes=VMEM_BYTES),
        name="pack_edge" if split else "pack_middle",
    )(info, fixed(x))


def start_all(pairs, sems):
    copies = [pltpu.make_async_copy(a, b, sems.at[n]) for n, (a, b) in enumerate(pairs)]
    for c in copies:
        c.start()
    return copies


def weigh(cond, w, planes, scale):
    for p in planes:
        w[p, 0] = scale * cond[0, p]
        for k in range(DIM):
            for n in range(DEG):
                w[p, 1 + DEG * k + n] = (scale * MEANS[n]) * cond[k + 1, p]


def laplace_plane(v, lap, p, zero, up_row, dn_row):
    lane = lax.broadcasted_iota(jnp.int32, (ROWS, LANES), 1)
    first_lane, last_lane = lane == 0, lane == LANES - 1
    rows = pl.ds(TOP, ROWS)

    def group(t, carry):
        for jj in range(T4):
            j = t * T4 + jj
            v[j, p + 1, pl.ds(TOP - 1, 1), :] = up_row(t, p, jj)
            v[j, p + 1, pl.ds(TOP + ROWS, 1), :] = dn_row(t, p, jj)
        for jj in range(T4):
            j = t * T4 + jj
            c = v[j, p + 1, rows, :]
            up = v[j, p + 1, pl.ds(zero + (TOP - 1), ROWS), :]
            dn = v[j, p + 1, pl.ds(zero + (TOP + 1), ROWS), :]
            right = jnp.where(last_lane, 0.0, pltpu.roll(c, LANES - 1, 1))
            left = jnp.where(first_lane, 0.0, pltpu.roll(c, 1, 1))
            beside = v[j, p + 2, rows, :] + v[j, p, rows, :]
            beside = beside + dn + up
            beside = beside + right + left
            lap[j] = 6.0 * c - beside
        return carry

    lax.fori_loop(0, 4, group, 0)


def couple_plane(lap, w, p, emit):
    for half in range(2):
        rows = pl.ds(8 * half, 8)
        weights = [w[p, m, rows, :] for m in range(1 + DEG * DIM)]
        for i in range(TERMS):
            acc = weights[0] * lap[i, rows, :]
            for j, k, n in COUPLE[i]:
                acc = acc + weights[DEG * k + n] * lap[j, rows, :]
            emit(i, half, acc)


def waiting(groups, sems):
    at, held_back = 0, []
    for pairs in groups:
        copies = []
        for a, b in pairs:
            copies.append(pltpu.make_async_copy(a, b, sems.at[at]))
            at += 1
        for c in copies:
            c.start()
        held_back.append(copies)
    return held_back


def place_of(s_ref, k):
    h = jnp.bitwise_xor(s_ref[0], k >> 2)
    t = jnp.bitwise_xor(s_ref[1], k & 3)
    return h, t


def conductivity_pairs(s_ref, near, far, cond):
    odd = s_ref[2]
    return [
        (near, cond.at[:, pl.ds(2 * odd, 2)]),
        (far, cond.at[:, pl.ds(2 * (1 - odd), 2)]),
    ]


def first_kernel(edge, s_ref, *refs):
    outer, inner, near, far = refs[0:8], refs[8], refs[9], refs[10]
    if edge:
        zlo, zhi = refs[11:13]
        sol, y0, y15, z0, z3 = refs[15:20]
        scratch = refs[20:]
    else:
        sol, y0, y15 = refs[11:14]
        scratch = refs[14:]
    v, halo, lap, out, cond, w, y0v, y15v, sem_v, sem_o, sem_e = scratch
    h, zero = s_ref[0], s_ref[3]
    planes = (0, 3) if edge else (1, 2)
    rows = pl.ds(TOP, ROWS)

    early = conductivity_pairs(s_ref, near, far, cond)
    late = []
    for n in range(8):
        hk, tk = n // 4, n % 4
        group = late if edge and hk == 1 else early
        group.append((inner.at[n, pl.ds(0, T4)], v.at[pl.ds(tk * T4, T4), 2 + hk, rows]))
        if not edge:
            early.append((inner.at[n, pl.ds(T4, 3)], halo.at[tk, 1 + hk]))
        hk, tk = place_of(s_ref, n)
        early.append((outer[n].at[pl.ds(0, T4)], v.at[pl.ds(tk * T4, T4), 3 * hk + 1, rows]))
        if edge:
            early.append((outer[n].at[pl.ds(T4, 3)], halo.at[tk, 3 * hk]))
    if edge:
        for k in range(4):
            _, tk = place_of(s_ref, k)
            terms = pl.ds(tk * T4, T4)
            early.append((zlo.at[pl.ds(k * T4, T4)], v.at[terms, 5 * (1 - h), rows]))
            early.append((zhi.at[pl.ds(k * T4, T4)], v.at[terms, 5 * h, rows]))
    early, late = waiting([early, late], sem_v)
    for t in range(4):
        for n in planes:
            y0v[t, n, T4:24, :] = jnp.zeros((24 - T4, LANES), F32)
            y15v[t, n, T4:24, :] = jnp.zeros((24 - T4, LANES), F32)
    for c in early:
        c.wait()
    weigh(cond, w, planes, MIX)

    def up_row(t, p, jj):
        return halo[t, p, jj // 16, pl.ds(jj % 16, 1), :]

    def dn_row(t, p, jj):
        return halo[t, p, (24 + jj) // 16, pl.ds((24 + jj) % 16, 1), :]

    def plane_step(n, carry):
        @pl.when(n == 1)
        def _():
            for c in late:
                c.wait()

        p = planes[0] + (planes[1] - planes[0]) * n
        laplace_plane(v, lap, p, zero, up_row, dn_row)

        def emit(i, half, acc):
            value = KEEP * v[i, p + 1, pl.ds(TOP + 8 * half, 8), :] + acc
            out[i, p, pl.ds(8 * half, 8), :] = value
            if half == 0:
                y0v[i // T4, p, pl.ds(i % T4, 1), :] = value[0:1]
            else:
                y15v[i // T4, p, pl.ds(i % T4, 1), :] = value[7:8]

        couple_plane(lap, w, p, emit)
        for c in sends(out, sol, sem_o, p):
            c.start()
        if edge:
            for m in range(2):

                @pl.when(n == m)
                def _():
                    face(m).start()

        return carry

    def face(m):
        return pltpu.make_async_copy(out.at[:, planes[m]], (z0, z3)[m], sem_e.at[4 + m])

    lax.fori_loop(0, 2, plane_step, 0)
    ends = [(a.at[:, p], b.at[:, p]) for p in planes for a, b in ((y0v, y0), (y15v, y15))]
    ends = start_all(ends, sem_e)
    if edge:
        ends += [face(0), face(1)]
    for c in ends:
        c.wait()
    for p in planes:
        for c in sends(out, sol, sem_o, p):
            c.wait()


def sends(out, to, sem, p):
    half = p // 2
    return [
        pltpu.make_async_copy(
            out.at[pl.ds(t * T4, T4), p], to.at[half * 4 + t], sem.at[p * 4 + t]
        )
        for t in range(4)
    ]


def second_kernel(s_ref, *refs):
    outer, (inner, middle, edge, below, above, yup, ydn, near, far) = refs[0:8], refs[8:17]
    outs = refs[17:25]
    v, r, lap, out, cond, w, upv, dnv, sem_v, sem_o = refs[25:]
    h, zero = s_ref[0], s_ref[3]
    rows = pl.ds(TOP, ROWS)

    groups = [[(yup, upv), (ydn, dnv), (below, v.at[:, 0, rows])], [], [], []]
    groups[0] += conductivity_pairs(s_ref, near, far, cond)
    for n in range(8):
        hk, tk = n // 4, n % 4
        terms = pl.ds(tk * T4, T4)
        groups[hk].append((middle.at[n], v.at[terms, 2 + hk, rows]))
        groups[2 * hk].append((edge.at[n], v.at[terms, 1 + 3 * hk, rows]))
        groups[hk].append((inner.at[n, pl.ds(0, T4)], r.at[terms, 1 + hk]))
        hk, tk = place_of(s_ref, n)
        groups[0].append((outer[n].at[pl.ds(0, T4)], r.at[pl.ds(tk * T4, T4), 3 * hk]))
    groups[3].append((above, v.at[:, 5, rows]))
    groups = waiting(groups, sem_v)
    for c in groups[0]:
        c.wait()
    weigh(cond, w, range(4), -1.0)

    def up_row(t, p, jj):
        return upv[t, p, pl.ds(jj, 1), :]

    def dn_row(t, p, jj):
        return dnv[t, p, pl.ds(jj, 1), :]

    def scattered(group):
        result = []
        for kk in range(4):
            k = group * 4 + kk
            hk, tk = place_of(s_ref, k)
            result.append(
                pltpu.make_async_copy(
                    out.at[pl.ds(tk * T4, T4), pl.ds(2 * hk, 2)], outs[k], sem_o.at[k]
                )
            )
        return result

    def plane_step(p, carry):
        for m in range(1, 4):

            @pl.when(p == m)
            def _():
                for c in groups[m]:
                    c.wait()

        laplace_plane(v, lap, p, zero, up_row, dn_row)

        def emit(i, half, acc):
            own = pl.ds(8 * half, 8)
            out[i, p, own, :] = r[i, p, own, :] + acc

        couple_plane(lap, w, p, emit)
        for group in range(2):

            @pl.when((p % 2 == 1) & (jnp.bitwise_xor(h, group) == p // 2))
            def _():
                for c in scattered(group):
                    c.start()

        return carry

    lax.fori_loop(0, 4, plane_step, 0)
    for c in scattered(0) + scattered(1):
        c.wait()


TOP = 8
PIECE = held(T4, 2, ROWS, LANES)
PIECES = held(BANDS, T4, ROWS, LANES)
FACE = held(TERMS, ROWS, LANES)
EDGE = held(4, 4, 24, LANES)
RES_SHAPES = [PIECE] * 8


def first(edge, info, *arrays):
    return pl.pallas_call(
        functools.partial(first_kernel, edge),
        out_shape=[PIECES, EDGE, EDGE] + ([FACE, FACE] if edge else []),
        in_specs=[SMEM] + [HBM] * len(arrays),
        out_specs=[HBM] * (5 if edge else 3),
        scratch_shapes=[
            pltpu.VMEM((TERMS, 6, 32, LANES), F32),
            pltpu.VMEM((4, 4, 3, ROWS, LANES), F32),
            pltpu.VMEM((TERMS, ROWS, LANES), F32),
            pltpu.VMEM((TERMS, 4, ROWS, LANES), F32),
            pltpu.VMEM((DIM + 1, 4, ROWS, LANES), F32),
            pltpu.VMEM((4, 1 + DEG * DIM, ROWS, LANES), F32),
            pltpu.VMEM((4, 4, 24, LANES), F32),
            pltpu.VMEM((4, 4, 24, LANES), F32),
            dma(34), dma(16), dma(6),
        ],
        compiler_params=pltpu.CompilerParams(vmem_limit_bytes=VMEM_BYTES),
        input_output_aliases={14: 1, 15: 2} if edge else {},
        name="first_edge" if edge else "first_middle",
    )(info, *arrays)


def second(info, *arrays):
    return pl.pallas_call(
        second_kernel,
        out_shape=RES_SHAPES,
        in_specs=[SMEM] + [HBM] * 17,
        out_specs=[HBM] * len(RES_SHAPES),
        scratch_shapes=[
            pltpu.VMEM((TERMS, 6, 32, LANES), F32),
            pltpu.VMEM((TERMS, 4, ROWS, LANES), F32),
            pltpu.VMEM((TERMS, ROWS, LANES), F32),
            pltpu.VMEM((TERMS, 4, ROWS, LANES), F32),
            pltpu.VMEM((DIM + 1, 4, ROWS, LANES), F32),
            pltpu.VMEM((4, 1 + DEG * DIM, ROWS, LANES), F32),
            pltpu.VMEM((4, 4, 24, LANES), F32),
            pltpu.VMEM((4, 4, 24, LANES), F32),
            dma(38), dma(8),
        ],
        compiler_params=pltpu.CompilerParams(vmem_limit_bytes=VMEM_BYTES),
        cost_estimate=WEIGHT,
        name="second",
    )(info, *arrays)


BAND = ("half", "term")
ORDER = (4, 2, 6, 5, 3, 7, 1)


def swapped(pieces):
    return lax.all_to_all(pieces, BAND, 0, 0, tiled=True)


def exchange(pieces):
    got = [None] * 8
    got[0] = pieces[0]
    for k in ORDER:
        got[k] = lax.ppermute(pieces[k], BAND, [(i, i ^ k) for i in range(8)])
    return got


def unpacked(got, band, other):
    whole = jnp.zeros((T4, 2, 128, LANES), F32)
    for n, k in enumerate((0,) + ORDER):
        if n == 5:
            whole, other = lax.optimization_barrier((whole, other))
        start = jnp.bitwise_xor(band, k) * ROWS
        whole = lax.dynamic_update_slice(whole, got[k], (0, 0, start, 0))
    return whole, other


def joined(pieces):
    return jnp.transpose(pieces, (1, 0, 2, 3)).reshape(T4, 128, LANES)


def shards(right_side, mean_cond, cond_terms):
    quads = lax.axis_size("quad")
    band = lax.axis_index(BAND)
    h, t = band // 4, band % 4
    info = jnp.stack([h, t, band % 2, 0 * band]).astype(jnp.int32)
    up = [(i, i + 1) for i in range(quads - 1)]
    down = [(i + 1, i) for i in range(quads - 1)]

    outer = exchange(pack(True, info, right_side))
    inner = pack(False, info, right_side)[0]
    inner, *outer[2:] = lax.optimization_barrier((inner, *outer[2:]))
    inner = swapped(inner)

    def z_shift(arrays, lower_half):
        face = jnp.concatenate([a[:T4] for a in arrays], axis=0)
        pairs = []
        for q in range(quads):
            for b in range(BANDS):
                other = q - 1 if (b // 4) == lower_half else q + 1
                if 0 <= other < quads:
                    pairs.append((q * BANDS + b, other * BANDS + b))
        return lax.ppermute(face, ("quad",) + BAND, pairs)

    zlo = z_shift(outer[0:4], 0)
    zhi = z_shift(outer[4:8], 1)

    local = jnp.concatenate([mean_cond[None], cond_terms], axis=0)
    own = lax.dynamic_slice_in_dim(local, h * ROWS, ROWS, axis=2)
    rest = lax.dynamic_slice_in_dim(local, (1 - h) * ROWS, ROWS, axis=2)
    near = lax.ppermute(own, BAND, [(4 * a + b, 2 * b + a) for a in range(2) for b in range(4)])
    far = lax.ppermute(rest, BAND, [(4 * a + b, 2 * b + 1 - a) for a in range(2) for b in range(4)])

    sol_middle, y0, y15 = first(False, info, *outer, inner, near, far)
    sol_edge, y0, y15, z0, z3 = first(True, info, *outer, inner, near, far, zlo, zhi, y0, y15)

    below = lax.ppermute(z3, "quad", up)
    above = lax.ppermute(z0, "quad", down)
    yup = lax.ppermute(y15, BAND, [(i, i + 1) for i in range(7)])
    ydn = lax.ppermute(y0, BAND, [(i + 1, i) for i in range(7)])

    solution = jnp.zeros((T4, 2, 128, LANES), F32)
    for plane, part in ((1 - h, swapped(sol_middle)), (h, swapped(sol_edge))):
        solution = lax.dynamic_update_slice(solution, joined(part)[:, None], (0, plane, 0, 0))
    res = second(
        info, *outer, inner, fixed(sol_middle), fixed(sol_edge), below, above, yup, ydn, near, far
    )
    residual, solution = unpacked(exchange(res), band, solution)
    return (solution, residual)


def solution(mesh):
    grid = Mesh(mesh.devices.reshape(-1, 2, 4), ("quad", "half", "term"))
    field = P("term", ("quad", "half"), None, None)
    return jax.shard_map(
        shards,
        mesh=grid,
        in_specs=(field, P(("quad", "half"), "term", None), P(None, ("quad", "half"), "term", None)),
        out_specs=(field, field),
        check_vma=False,
    )
```

time: 185 us -> 143 us (0.77)
  the two profiles are of different devices: /device:TPU:25 before, /device:TPU:1 now
where the time goes in v2:
time: 143 us; the launch traced here: 141 us
  starting transfers between devices  65.1 us (46%)
  waiting for transfers between devices  40.5 us (28%)
  Pallas kernels  24.3 us (17%)
  local copies, waits for them, and re-layouts  8.38 us (6%)
  other arithmetic  1.91 us (1%)
    ppermute x14, starting transfers between devices, exchange(): got[k] = lax.ppermute(pieces[k], BAND, [(i, i ^ k) for i in range(8)])  28 us
    ppermute x14, waiting for transfers between devices, exchange(): got[k] = lax.ppermute(pieces[k], BAND, [(i, i ^ k) for i in range(8)])  26.6 us
    all_to_all x3, starting transfers between devices, swapped(): return lax.all_to_all(pieces, BAND, 0, 0, tiled=True)  14.6 us
    pallas_call x2, Pallas kernels, first(): pl.pallas_call(functools.partial(first_kernel, edge), out_shape=[PIECES,...  10.5 us
    pallas_call x1, Pallas kernels, second(): pl.pallas_call(second_kernel, out_shape=RES_SHAPES, in_specs=[SMEM] + [HB...  7.48 us
    ppermute x1, waiting for transfers between devices, shards(): lax.ppermute(own, BAND, [(4 * a + b, 2 * b + a) for a in range(2) for b i...  7.24 us
    pallas_call x2, Pallas kernels, pack(): pl.pallas_call(functools.partial(pack_kernel, split), out_shape=[held(24,...  6.3 us
    ppermute x2, starting transfers between devices, z_shift(): return lax.ppermute(face, ('quad',) + BAND, pairs)  6.12 us
  transfers between devices with their start and end apart: 25, of which 13 were waited for; matrix products, arithmetic and copies ran while one was open for 6% of the time, Pallas kernels for 15%

profile of v2, /device:TPU:1, one launch (start us, length us, event | category | flops | bytes accessed | tf_op | source)
XLA Modules:
  0.0 141.2 jit_solution(10860877064299026283)
XLA Ops:
  0.7 3.1 %pack_edge.1 = (f32[24,16,128]{2,1,0:T(8,128)}, f32[24,16,128]{2,1,0:T(8,128)}, f32[24,16,128]{2,1,0:T(8,128)}, f32[24,16,128]{2,1,0:T(8,128)}, f32[24,16,128]{2...) custom-call(s32[4]{0:T(128)S(1)} %pad_add_fusion.s_ref, ...), custom_call_target="tpu_custom_call" | custom-call | tf_op jit(solution)/shard_map/pack_edge/pallas_call | solution.py:124
  6.0 2.8 %collective-permute-start.2 = (f32[24,16,128]{2,1,0:T(8,128)}, f32[24,16,128]{2,1,0:T(8,128)S(1)}, u32[]{:S(2)}, u32[]{:S(2)}) collective-permute-start(f32[24,16,128]{2,1,0:T(8,128)} %get-tuple-element.38), channel_id=1, source_target_pairs={{0,3},{1,2},{2,1},{3,0},{4,7},{5,6},{6,5},{7,4},{8,11},{9,10},{10,... | collective-permute-start | bytes 589832 | tf_op jit(solution)/shard_map/ppermute | solution.py:455
  12.3 3.6 %collective-permute-start.6 = (f32[24,16,128]{2,1,0:T(8,128)}, f32[24,16,128]{2,1,0:T(8,128)S(1)}, u32[]{:S(2)}, u32[]{:S(2)}) collective-permute-start(f32[24,16,128]{2,1,0:T(8,128)} %get-tuple-element.42), channel_id=1, source_target_pairs={{0,7},{1,6},{2,5},{3,4},{4,3},{5,2},{6,1},{7,0},{8,15},{9,14},{10,... | collective-permute-start | bytes 589832 | tf_op jit(solution)/shard_map/ppermute | solution.py:455
  15.9 3.2 %pack_middle.1 = f32[8,24,16,128]{3,2,1,0:T(8,128)} custom-call(s32[4]{0:T(128)S(1)} %pad_add_fusion.s_ref, f32[21,2,128,128]{3,2,1,0:T(8,128)} %x_ref.3), custom_call_target="tpu_custom_call" | custom-call | tf_op jit(solution)/shard_map/pack_middle/pallas_call | solution.py:124
  21.4 5.2 %collective-permute-done.4.refs_5_ = f32[24,16,128]{2,1,0:T(8,128)S(1)} collective-permute-done((f32[24,16,128]{2,1,0:T(8,128)}, f32[24,16,128]{2,1,0:T(8,128)S(1)}, u32[]{:S(2)}, u32[]{:S(2)}) %collective-permute-start.4) | collective-permute-done | bytes 196640 | tf_op jit(solution)/shard_map/ppermute | solution.py:455
  26.6 4.7 %collective-permute-done.6.refs_7_ = f32[24,16,128]{2,1,0:T(8,128)S(1)} collective-permute-done((f32[24,16,128]{2,1,0:T(8,128)}, f32[24,16,128]{2,1,0:T(8,128)S(1)}, u32[]{:S(2)}, u32[]{:S(2)}) %collective-permute-start.6) | collective-permute-done | bytes 196640 | tf_op jit(solution)/shard_map/ppermute | solution.py:455
  31.3 3.5 %all-to-all-start = ((f32[8,24,16,128]{3,2,1,0:T(8,128)}), f32[8,24,16,128]{3,2,1,0:T(8,128)S(1)}, u32[]{:S(2)}, u32[]{:S(2)}) async-start(f32[8,24,16,128]{3,2,1,0:T(8,128)} %pack_middle.1), calls=%async_computation | async-start | bytes 3145728 | tf_op jit(solution)/shard_map/all_to_all | solution.py:448
  39.7 4.8 %collective-permute-start.10 = (f32[84,16,128]{2,1,0:T(8,128)}, f32[84,16,128]{2,1,0:T(8,128)}, u32[]{:S(2)}, u32[]{:S(2)}) collective-permute-start(f32[84,16,128]{2,1,0:T(8,128)} %pad_maximum_fusion.1), channel_id=1, source_target_pairs={{0,8},{1,9},{2,10},{3,11},{8,16},{9,17},{10,18},{11,19},{12,4},{13... | collective-permute-start | bytes 2064392 | tf_op jit(solution)/shard_map/ppermute | solution.py:494
  44.6 4.0 %collective-permute-start.7 = (f32[7,2,16,128]{3,2,1,0:T(8,128)S(1)}, f32[7,2,16,128]{3,2,1,0:T(8,128)S(1)}, u32[]{:S(2)}, u32[]{:S(2)}) collective-permute-start(f32[7,2,16,128]{3,2,1,0:T(8,128)S(1)} %get-tuple-element.69), channel_id=1, source_target_pairs={{0,0},{1,2},{2,4},{3,6},{4,1},{5,3},{6,5},{7,7},{8,8},{9,10},{10,1... | collective-permute-start | bytes 344072 | tf_op jit(solution)/shard_map/ppermute | solution.py:502
  49.6 7.2 %collective-permute-done.7.refs_9_.refs_15_ = f32[7,2,16,128]{3,2,1,0:T(8,128)S(1)} collective-permute-done((f32[7,2,16,128]{3,2,1,0:T(8,128)S(1)}, f32[7,2,16,128]{3,2,1,0:T(8,128)S(1)}, u32[]{:S(2)}, u32[]{:S(2)}) %collective-permute-start.7) | collective-permute-done | bytes 114720 | tf_op jit(solution)/shard_map/ppermute | solution.py:502
  56.9 4.5 %first_middle.1 = (f32[8,21,16,128]{3,2,1,0:T(8,128)}, f32[4,4,24,128]{3,2,1,0:T(8,128)}, f32[4,4,24,128]{3,2,1,0:T(8,128)}) custom-call(s32[4]{0:T(128)S(1)} %pad_add_fusion.s_ref, f32[24,16,128]{2,1,0:T(8,128)S(1)} %copy-done, f32[24,16,128]{2,1,0:T(8,128)S(1)} %collective-permute-done.refs_1_, f32[24,16,128]{2,1,0:T(8,128)S(1)} %collective-permute-done.1.refs_2_, ...), custom_call_target="tpu_custom_call" | custom-call | tf_op jit(solution)/shard_map/first_middle/pallas_call | solution.py:398
  61.4 6.1 %all-to-all-start.1 = ((f32[8,21,16,128]{3,2,1,0:T(8,128)}), f32[8,21,16,128]{3,2,1,0:T(8,128)}, u32[]{:S(2)}, u32[]{:S(2)}) async-start(f32[8,21,16,128]{3,2,1,0:T(8,128)} %get-tuple-element.50.refs_9_), calls=%async_computation.1 | async-start | bytes 2752512 | tf_op jit(solution)/shard_map/all_to_all | solution.py:448
  67.4 6.0 %first_edge.1 = (f32[8,21,16,128]{3,2,1,0:T(8,128)}, f32[4,4,24,128]{3,2,1,0:T(8,128)}, f32[4,4,24,128]{3,2,1,0:T(8,128)}, f32[84,16,128]{2,1,0:T(8,128)}, f32[84,16,128]{2,1,0:T(8,128)}) custom-call(s32[4]{0:T(128)S(1)} %pad_add_fusion.s_ref, f32[24,16,128]{2,1,0:T(8,128)S(1)} %copy-done, ...), custom_call_target="tpu_custom_call", output_to_operand_aliasing={{1}: (14, {}), {2}: (15, {})} | custom-call | tf_op jit(solution)/shard_map/first_edge/pallas_call | solution.py:398
  73.5 4.3 %collective-permute-start.11 = (f32[84,16,128]{2,1,0:T(8,128)}, f32[84,16,128]{2,1,0:T(8,128)}, u32[]{:S(2)}, u32[]{:S(2)}) collective-permute-start(f32[84,16,128]{2,1,0:T(8,128)} %get-tuple-element.54), channel_id=1, source_target_pairs={{0,8},{8,16},{16,24},{24,32},{32,40},{40,48},{48,56},{56,64},{64,7... | collective-permute-start | bytes 2064392 | tf_op jit(solution)/shard_map/ppermute | solution.py:508
  79.1 3.8 %collective-permute-start.13 = (f32[4,4,24,128]{3,2,1,0:T(8,128)}, f32[4,4,24,128]{3,2,1,0:T(8,128)}, u32[]{:S(2)}, u32[]{:S(2)}) collective-permute-start(f32[4,4,24,128]{3,2,1,0:T(8,128)} %get-tuple-element.56), channel_id=1, source_target_pairs={{0,1},{1,2},{2,3},{3,4},{4,5},{5,6},{6,7},{8,9},{9,10},{10,11},{11... | collective-permute-start | bytes 589832 | tf_op jit(solution)/shard_map/ppermute | solution.py:510
  86.2 5.0 %all-to-all-start.2 = ((f32[8,21,16,128]{3,2,1,0:T(8,128)}), f32[8,21,16,128]{3,2,1,0:T(8,128)}, u32[]{:S(2)}, u32[]{:S(2)}) async-start(f32[8,21,16,128]{3,2,1,0:T(8,128)} %get-tuple-element.53.refs_10_), calls=%async_computation.2 | async-start | bytes 2752512 | tf_op jit(solution)/shard_map/all_to_all | solution.py:448
  91.9 4.6 %collective-permute-done.12.refs_12_ = f32[84,16,128]{2,1,0:T(8,128)} collective-permute-done((f32[84,16,128]{2,1,0:T(8,128)}, f32[84,16,128]{2,1,0:T(8,128)}, u32[]{:S(2)}, u32[]{:S(2)}) %collective-permute-start.12) | collective-permute-done | bytes 688160 | tf_op jit(solution)/shard_map/ppermute | solution.py:509
  96.6 7.5 %second.1 = (f32[21,2,16,128]{3,2,1,0:T(8,128)}, f32[21,2,16,128]{3,2,1,0:T(8,128)}, f32[21,2,16,128]{3,2,1,0:T(8,128)}, f32[21,2,16,128]{3,2,1,0:T(8,128)}, f32...) custom-call(s32[4]{0:T(128)S(1)} %pad_add_fusion.s_ref, ...), custom_call_target="tpu_custom_call" | custom-call | flops 999999995904 | bytes 1000000000 | tf_op jit(solution)/shard_map/second/pallas_call | solution.py:421
  104.1 2.8 %collective-permute-start.15 = (f32[21,2,16,128]{3,2,1,0:T(8,128)}, f32[21,2,16,128]{3,2,1,0:T(8,128)S(1)}, u32[]{:S(2)}, u32[]{:S(2)}) collective-permute-start(f32[21,2,16,128]{3,2,1,0:T(8,128)} %get-tuple-element.59), channel_id=1, source_target_pairs={{0,4},{1,5},{2,6},{3,7},{4,0},{5,1},{6,2},{7,3},{8,12},{9,13},{10,... | collective-permute-start | bytes 1032200 | tf_op jit(solution)/shard_map/ppermute | solution.py:455
  107.7 4.6 %collective-permute-start.18 = (f32[21,2,16,128]{3,2,1,0:T(8,128)}, f32[21,2,16,128]{3,2,1,0:T(8,128)S(1)}, u32[]{:S(2)}, u32[]{:S(2)}) collective-permute-start(f32[21,2,16,128]{3,2,1,0:T(8,128)} %get-tuple-element.62), channel_id=1, source_target_pairs={{0,5},{1,4},{2,7},{3,6},{4,1},{5,0},{6,3},{7,2},{8,13},{9,12},{10,... | collective-permute-start | bytes 1032200 | tf_op jit(solution)/shard_map/ppermute | solution.py:455
  112.7 4.5 %collective-permute-done.15 = f32[21,2,16,128]{3,2,1,0:T(8,128)S(1)} collective-permute-done((f32[21,2,16,128]{3,2,1,0:T(8,128)}, f32[21,2,16,128]{3,2,1,0:T(8,128)S(1)}, u32[]{:S(2)}, u32[]{:S(2)}) %collective-permute-start.15) | collective-permute-done | bytes 344096 | tf_op jit(solution)/shard_map/ppermute | solution.py:455
  117.3 3.5 %collective-permute-start.20 = (f32[21,2,16,128]{3,2,1,0:T(8,128)S(1)}, f32[21,2,16,128]{3,2,1,0:T(8,128)S(1)}, u32[]{:S(2)}, u32[]{:S(2)}) collective-permute-start(f32[21,2,16,128]{3,2,1,0:T(8,128)S(1)} %copy-done.7), channel_id=1, source_target_pairs={{0,7},{1,6},{2,5},{3,4},{4,3},{5,2},{6,1},{7,0},{8,15},{9,14},{10,... | collective-permute-start | bytes 1032200 | tf_op jit(solution)/shard_map/ppermute | solution.py:455
  121.7 4.1 %collective-permute-start.21 = (f32[21,2,16,128]{3,2,1,0:T(8,128)S(1)}, f32[21,2,16,128]{3,2,1,0:T(8,128)S(1)}, u32[]{:S(2)}, u32[]{:S(2)}) collective-permute-start(f32[21,2,16,128]{3,2,1,0:T(8,128)S(1)} %copy-done.6), channel_id=1, source_target_pairs={{0,1},{1,0},{2,3},{3,2},{4,5},{5,4},{6,7},{7,6},{8,9},{9,8},{10,11... | collective-permute-start | bytes 1032200 | tf_op jit(solution)/shard_map/ppermute | solution.py:455
  125.9 6.8 %collective-permute-done.18 = f32[21,2,16,128]{3,2,1,0:T(8,128)S(1)} collective-permute-done((f32[21,2,16,128]{3,2,1,0:T(8,128)}, f32[21,2,16,128]{3,2,1,0:T(8,128)S(1)}, u32[]{:S(2)}, u32[]{:S(2)}) %collective-permute-start.18) | collective-permute-done | bytes 344096 | tf_op jit(solution)/shard_map/ppermute | solution.py:455
  (73 shorter events, 29.9 us)
Async XLA Ops:
  3.9 8.4 %collective-permute-start.1 = (f32[24,16,128]{2,1,0:T(8,128)}, f32[24,16,128]{2,1,0:T(8,128)S(1)}, u32[]{:S(2)}, u32[]{:S(2)}) collective-permute-start(f32[24,16,128]{2,1,0:T(8,128)} %get-tuple-element.37), channel_id=1, source_target_pairs={{0,2},{1,3},{2,0},{3,1},{4,6},{5,7},{6,4},{7,5},{8,10},{9,11},{10,... | collective-permute-start | bytes 589832 | tf_op jit(solution)/shard_map/ppermute | solution.py:455
  6.0 13.0 %collective-permute-start.2 = (f32[24,16,128]{2,1,0:T(8,128)}, f32[24,16,128]{2,1,0:T(8,128)S(1)}, u32[]{:S(2)}, u32[]{:S(2)}) collective-permute-start(f32[24,16,128]{2,1,0:T(8,128)} %get-tuple-element.38), channel_id=1, source_target_pairs={{0,3},{1,2},{2,1},{3,0},{4,7},{5,6},{6,5},{7,4},{8,11},{9,10},{10,... | collective-permute-start | bytes 589832 | tf_op jit(solution)/shard_map/ppermute | solution.py:455
  8.8 12.6 %collective-permute-start.3 = (f32[24,16,128]{2,1,0:T(8,128)}, f32[24,16,128]{2,1,0:T(8,128)S(1)}, u32[]{:S(2)}, u32[]{:S(2)}) collective-permute-start(f32[24,16,128]{2,1,0:T(8,128)} %get-tuple-element.39), channel_id=1, source_target_pairs={{0,4},{1,5},{2,6},{3,7},{4,0},{5,1},{6,2},{7,3},{8,12},{9,13},{10,... | collective-permute-start | bytes 589832 | tf_op jit(solution)/shard_map/ppermute | solution.py:455
  9.9 16.7 %collective-permute-start.4 = (f32[24,16,128]{2,1,0:T(8,128)}, f32[24,16,128]{2,1,0:T(8,128)S(1)}, u32[]{:S(2)}, u32[]{:S(2)}) collective-permute-start(f32[24,16,128]{2,1,0:T(8,128)} %get-tuple-element.40), channel_id=1, source_target_pairs={{0,5},{1,4},{2,7},{3,6},{4,1},{5,0},{6,3},{7,2},{8,13},{9,12},{10,... | collective-permute-start | bytes 589832 | tf_op jit(solution)/shard_map/ppermute | solution.py:455
  10.6 16.0 %collective-permute-start.5 = (f32[24,16,128]{2,1,0:T(8,128)}, f32[24,16,128]{2,1,0:T(8,128)S(1)}, u32[]{:S(2)}, u32[]{:S(2)}) collective-permute-start(f32[24,16,128]{2,1,0:T(8,128)} %get-tuple-element.41), channel_id=1, source_target_pairs={{0,6},{1,7},{2,4},{3,5},{4,2},{5,3},{6,0},{7,1},{8,14},{9,15},{10,... | collective-permute-start | bytes 589832 | tf_op jit(solution)/shard_map/ppermute | solution.py:455
  12.3 19.0 %collective-permute-start.6 = (f32[24,16,128]{2,1,0:T(8,128)}, f32[24,16,128]{2,1,0:T(8,128)S(1)}, u32[]{:S(2)}, u32[]{:S(2)}) collective-permute-start(f32[24,16,128]{2,1,0:T(8,128)} %get-tuple-element.42), channel_id=1, source_target_pairs={{0,7},{1,6},{2,5},{3,4},{4,3},{5,2},{6,1},{7,0},{8,15},{9,14},{10,... | collective-permute-start | bytes 589832 | tf_op jit(solution)/shard_map/ppermute | solution.py:455
  31.3 25.6 %all-to-all-start = ((f32[8,24,16,128]{3,2,1,0:T(8,128)}), f32[8,24,16,128]{3,2,1,0:T(8,128)S(1)}, u32[]{:S(2)}, u32[]{:S(2)}) async-start(f32[8,24,16,128]{3,2,1,0:T(8,128)} %pack_middle.1), calls=%async_computation | async-start | bytes 3145728 | tf_op jit(solution)/shard_map/all_to_all | solution.py:448
  37.5 30.0 %collective-permute-start.9 = (f32[84,16,128]{2,1,0:T(8,128)}, f32[84,16,128]{2,1,0:T(8,128)}, u32[]{:S(2)}, u32[]{:S(2)}) collective-permute-start(f32[84,16,128]{2,1,0:T(8,128)} %pad_maximum_fusion), channel_id=1, source_target_pairs={{4,12},{5,13},{6,14},{7,15},{8,0},{9,1},{10,2},{11,3},{12,20},{13,... | collective-permute-start | bytes 2064392 | tf_op jit(solution)/shard_map/ppermute | solution.py:494
  39.7 27.7 %collective-permute-start.10 = (f32[84,16,128]{2,1,0:T(8,128)}, f32[84,16,128]{2,1,0:T(8,128)}, u32[]{:S(2)}, u32[]{:S(2)}) collective-permute-start(f32[84,16,128]{2,1,0:T(8,128)} %pad_maximum_fusion.1), channel_id=1, source_target_pairs={{0,8},{1,9},{2,10},{3,11},{8,16},{9,17},{10,18},{11,19},{12,4},{13... | collective-permute-start | bytes 2064392 | tf_op jit(solution)/shard_map/ppermute | solution.py:494
  44.6 12.3 %collective-permute-start.7 = (f32[7,2,16,128]{3,2,1,0:T(8,128)S(1)}, f32[7,2,16,128]{3,2,1,0:T(8,128)S(1)}, u32[]{:S(2)}, u32[]{:S(2)}) collective-permute-start(f32[7,2,16,128]{3,2,1,0:T(8,128)S(1)} %get-tuple-element.69), channel_id=1, source_target_pairs={{0,0},{1,2},{2,4},{3,6},{4,1},{5,3},{6,5},{7,7},{8,8},{9,10},{10,1... | collective-permute-start | bytes 344072 | tf_op jit(solution)/shard_map/ppermute | solution.py:502
  48.6 8.3 %collective-permute-start.8 = (f32[7,2,16,128]{3,2,1,0:T(8,128)S(1)}, f32[7,2,16,128]{3,2,1,0:T(8,128)S(1)}, u32[]{:S(2)}, u32[]{:S(2)}) collective-permute-start(f32[7,2,16,128]{3,2,1,0:T(8,128)S(1)} %get-tuple-element.68), channel_id=1, source_target_pairs={{0,1},{1,3},{2,5},{3,7},{4,0},{5,2},{6,4},{7,6},{8,9},{9,11},{10,1... | collective-permute-start | bytes 344072 | tf_op jit(solution)/shard_map/ppermute | solution.py:503
  61.4 24.8 %all-to-all-start.1 = ((f32[8,21,16,128]{3,2,1,0:T(8,128)}), f32[8,21,16,128]{3,2,1,0:T(8,128)}, u32[]{:S(2)}, u32[]{:S(2)}) async-start(f32[8,21,16,128]{3,2,1,0:T(8,128)} %get-tuple-element.50.refs_9_), calls=%async_computation.1 | async-start | bytes 2752512 | tf_op jit(solution)/shard_map/all_to_all | solution.py:448
  73.5 18.4 %collective-permute-start.11 = (f32[84,16,128]{2,1,0:T(8,128)}, f32[84,16,128]{2,1,0:T(8,128)}, u32[]{:S(2)}, u32[]{:S(2)}) collective-permute-start(f32[84,16,128]{2,1,0:T(8,128)} %get-tuple-element.54), channel_id=1, source_target_pairs={{0,8},{8,16},{16,24},{24,32},{32,40},{40,48},{48,56},{56,64},{64,7... | collective-permute-start | bytes 2064392 | tf_op jit(solution)/shard_map/ppermute | solution.py:508
  77.8 18.8 %collective-permute-start.12 = (f32[84,16,128]{2,1,0:T(8,128)}, f32[84,16,128]{2,1,0:T(8,128)}, u32[]{:S(2)}, u32[]{:S(2)}) collective-permute-start(f32[84,16,128]{2,1,0:T(8,128)} %get-tuple-element.55), channel_id=1, source_target_pairs={{8,0},{16,8},{24,16},{32,24},{40,32},{48,40},{56,48},{64,56},{72,6... | collective-permute-start | bytes 2064392 | tf_op jit(solution)/shard_map/ppermute | solution.py:509
  79.1 12.1 %collective-permute-start.13 = (f32[4,4,24,128]{3,2,1,0:T(8,128)}, f32[4,4,24,128]{3,2,1,0:T(8,128)}, u32[]{:S(2)}, u32[]{:S(2)}) collective-permute-start(f32[4,4,24,128]{3,2,1,0:T(8,128)} %get-tuple-element.56), channel_id=1, source_target_pairs={{0,1},{1,2},{2,3},{3,4},{4,5},{5,6},{6,7},{8,9},{9,10},{10,11},{11... | collective-permute-start | bytes 589832 | tf_op jit(solution)/shard_map/ppermute | solution.py:510
  82.9 8.3 %collective-permute-start.14 = (f32[4,4,24,128]{3,2,1,0:T(8,128)}, f32[4,4,24,128]{3,2,1,0:T(8,128)}, u32[]{:S(2)}, u32[]{:S(2)}) collective-permute-start(f32[4,4,24,128]{3,2,1,0:T(8,128)} %get-tuple-element.57), channel_id=1, source_target_pairs={{1,0},{2,1},{3,2},{4,3},{5,4},{6,5},{7,6},{9,8},{10,9},{11,10},{12... | collective-permute-start | bytes 589832 | tf_op jit(solution)/shard_map/ppermute | solution.py:511
  86.2 49.6 %all-to-all-start.2 = ((f32[8,21,16,128]{3,2,1,0:T(8,128)}), f32[8,21,16,128]{3,2,1,0:T(8,128)}, u32[]{:S(2)}, u32[]{:S(2)}) async-start(f32[8,21,16,128]{3,2,1,0:T(8,128)} %get-tuple-element.53.refs_10_), calls=%async_computation.2 | async-start | bytes 2752512 | tf_op jit(solution)/shard_map/all_to_all | solution.py:448
  104.1 13.2 %collective-permute-start.15 = (f32[21,2,16,128]{3,2,1,0:T(8,128)}, f32[21,2,16,128]{3,2,1,0:T(8,128)S(1)}, u32[]{:S(2)}, u32[]{:S(2)}) collective-permute-start(f32[21,2,16,128]{3,2,1,0:T(8,128)} %get-tuple-element.59), channel_id=1, source_target_pairs={{0,4},{1,5},{2,6},{3,7},{4,0},{5,1},{6,2},{7,3},{8,12},{9,13},{10,... | collective-permute-start | bytes 1032200 | tf_op jit(solution)/shard_map/ppermute | solution.py:455
  106.9 14.8 %collective-permute-start.16 = (f32[21,2,16,128]{3,2,1,0:T(8,128)}, f32[21,2,16,128]{3,2,1,0:T(8,128)S(1)}, u32[]{:S(2)}, u32[]{:S(2)}) collective-permute-start(f32[21,2,16,128]{3,2,1,0:T(8,128)} %get-tuple-element.60), channel_id=1, source_target_pairs={{0,2},{1,3},{2,0},{3,1},{4,6},{5,7},{6,4},{7,5},{8,10},{9,11},{10,... | collective-permute-start | bytes 1032200 | tf_op jit(solution)/shard_map/ppermute | solution.py:455
  107.2 18.7 %collective-permute-start.17 = (f32[21,2,16,128]{3,2,1,0:T(8,128)}, f32[21,2,16,128]{3,2,1,0:T(8,128)S(1)}, u32[]{:S(2)}, u32[]{:S(2)}) collective-permute-start(f32[21,2,16,128]{3,2,1,0:T(8,128)} %get-tuple-element.61), channel_id=1, source_target_pairs={{0,6},{1,7},{2,4},{3,5},{4,2},{5,3},{6,0},{7,1},{8,14},{9,15},{10,... | collective-permute-start | bytes 1032200 | tf_op jit(solution)/shard_map/ppermute | solution.py:455
  107.7 25.0 %collective-permute-start.18 = (f32[21,2,16,128]{3,2,1,0:T(8,128)}, f32[21,2,16,128]{3,2,1,0:T(8,128)S(1)}, u32[]{:S(2)}, u32[]{:S(2)}) collective-permute-start(f32[21,2,16,128]{3,2,1,0:T(8,128)} %get-tuple-element.62), channel_id=1, source_target_pairs={{0,5},{1,4},{2,7},{3,6},{4,1},{5,0},{6,3},{7,2},{8,13},{9,12},{10,... | collective-permute-start | bytes 1032200 | tf_op jit(solution)/shard_map/ppermute | solution.py:455
  112.4 26.0 %collective-permute-start.19 = (f32[21,2,16,128]{3,2,1,0:T(8,128)}, f32[21,2,16,128]{3,2,1,0:T(8,128)S(1)}, u32[]{:S(2)}, u32[]{:S(2)}) collective-permute-start(f32[21,2,16,128]{3,2,1,0:T(8,128)} %get-tuple-element.65), channel_id=1, source_target_pairs={{0,3},{1,2},{2,1},{3,0},{4,7},{5,6},{6,5},{7,4},{8,11},{9,10},{10,... | collective-permute-start | bytes 1032200 | tf_op jit(solution)/shard_map/ppermute | solution.py:455
  117.3 22.5 %collective-permute-start.20 = (f32[21,2,16,128]{3,2,1,0:T(8,128)S(1)}, f32[21,2,16,128]{3,2,1,0:T(8,128)S(1)}, u32[]{:S(2)}, u32[]{:S(2)}) collective-permute-start(f32[21,2,16,128]{3,2,1,0:T(8,128)S(1)} %copy-done.7), channel_id=1, source_target_pairs={{0,7},{1,6},{2,5},{3,4},{4,3},{5,2},{6,1},{7,0},{8,15},{9,14},{10,... | collective-permute-start | bytes 1032200 | tf_op jit(solution)/shard_map/ppermute | solution.py:455
  121.7 18.7 %collective-permute-start.21 = (f32[21,2,16,128]{3,2,1,0:T(8,128)S(1)}, f32[21,2,16,128]{3,2,1,0:T(8,128)S(1)}, u32[]{:S(2)}, u32[]{:S(2)}) collective-permute-start(f32[21,2,16,128]{3,2,1,0:T(8,128)S(1)} %copy-done.6), channel_id=1, source_target_pairs={{0,1},{1,0},{2,3},{3,2},{4,5},{5,4},{6,7},{7,6},{8,9},{9,8},{10,11... | collective-permute-start | bytes 1032200 | tf_op jit(solution)/shard_map/ppermute | solution.py:455
  (9 other events, 88.0 us)

commit v3 on v2

--- a/solution.py
+++ b/solution.py
@@ -136,6 +136,35 @@
     )(info, fixed(x))
 
 
+def faces_kernel(*refs):
+    pieces, faces, (held_v, sems) = refs[:BANDS], refs[BANDS : BANDS + 2], refs[BANDS + 2 :]
+    loads = start_all(
+        [
+            (pieces[k].at[pl.ds(0, T4)], held_v.at[k // 4, pl.ds(k % 4 * T4, T4)])
+            for k in range(BANDS)
+        ],
+        sems,
+    )
+    for c in loads:
+        c.wait()
+    stores = start_all([(held_v.at[n], faces[n]) for n in range(2)], sems)
+    for c in stores:
+        c.wait()
+
+
+def faces(*pieces):
+    return pl.pallas_call(
+        faces_kernel,
+        out_shape=[held(TERMS, ROWS, LANES)] * 2,
+        in_specs=[HBM] * BANDS,
+        out_specs=[HBM] * 2,
+        scratch_shapes=[pltpu.VMEM((2, TERMS, ROWS, LANES), F32), dma(BANDS)],
+        compiler_params=pltpu.CompilerParams(vmem_limit_bytes=VMEM_BYTES),
+        cost_estimate=WEIGHT,
+        name="faces",
+    )(*pieces)
+
+
 def start_all(pairs, sems):
     copies = [pltpu.make_async_copy(a, b, sems.at[n]) for n, (a, b) in enumerate(pairs)]
     for c in copies:
@@ -480,11 +509,9 @@
 
     outer = exchange(pack(True, info, right_side))
     inner = pack(False, info, right_side)[0]
-    inner, *outer[2:] = lax.optimization_barrier((inner, *outer[2:]))
     inner = swapped(inner)
 
-    def z_shift(arrays, lower_half):
-        face = jnp.concatenate([a[:T4] for a in arrays], axis=0)
+    def z_shift(face, lower_half):
         pairs = []
         for q in range(quads):
             for b in range(BANDS):
@@ -493,8 +520,9 @@
                     pairs.append((q * BANDS + b, other * BANDS + b))
         return lax.ppermute(face, ("quad",) + BAND, pairs)
 
-    zlo = z_shift(outer[0:4], 0)
-    zhi = z_shift(outer[4:8], 1)
+    low, high = faces(*outer)
+    zlo = z_shift(low, 0)
+    zhi = z_shift(high, 1)
 
     local = jnp.concatenate([mean_cond[None], cond_terms], axis=0)
     own = lax.dynamic_slice_in_dim(local, h * ROWS, ROWS, axis=2)

time: 143 us -> 139 us (0.972)
  starting transfers between devices: 65.1 us -> 55.6 us
  waiting for transfers between devices: 40.5 us -> 44.5 us
  Pallas kernels: 24.3 us -> 27.7 us
  other arithmetic: 1.91 us -> 0.1 us
    ppermute x14, waiting for transfers between devices: 26.6 us -> 33.2 us  [exchange(): got[k] = lax.ppermute(pieces[k], BAND, [(i, i ^ k) for i in range(8)])]
    ppermute x14, starting transfers between devices: 28 us -> 22.6 us  [exchange(): got[k] = lax.ppermute(pieces[k], BAND, [(i, i ^ k) for i in range(8)])]
    all_to_all x3, waiting for transfers between devices: 1.33 us -> 4.3 us  [swapped(): return lax.all_to_all(pieces, BAND, 0, 0, tiled=True)]
    pallas_call x0 -> x1, Pallas kernels: none -> 2.93 us  [faces(): pl.pallas_call(faces_kernel, out_shape=[held(TERMS, ROWS, LANES)] * 2, in...]
    ppermute x1, waiting for transfers between devices: 4.65 us -> 2.11 us  [shards(): above = lax.ppermute(z0, 'quad', down)]
    ppermute x1, waiting for transfers between devices: 7.24 us -> 4.81 us  [shards(): lax.ppermute(own, BAND, [(4 * a + b, 2 * b + a) for a in range(2) for b i...]
    ppermute x1, starting transfers between devices: 4.3 us -> 1.99 us  [shards(): below = lax.ppermute(z3, 'quad', up)]
    ppermute x1, starting transfers between devices: 3.96 us -> 1.92 us  [shards(): lax.ppermute(own, BAND, [(4 * a + b, 2 * b + a) for a in range(2) for b i...]
  transfers between devices with their start and end apart: 25 -> 25, of which waited for: 13 -> 13; matrix products, arithmetic and copies ran while one was open for 6% -> 4% of each run, Pallas kernels for 15% -> 18%
where the time goes in v3:
time: 139 us; the launch traced here: 137 us
  starting transfers between devices  55.6 us (40%)
  waiting for transfers between devices  44.5 us (32%)
  Pallas kernels  27.7 us (20%)
  local copies, waits for them, and re-layouts  8.28 us (6%)
    ppermute x14, waiting for transfers between devices, exchange(): got[k] = lax.ppermute(pieces[k], BAND, [(i, i ^ k) for i in range(8)])  33.2 us
    ppermute x14, starting transfers between devices, exchange(): got[k] = lax.ppermute(pieces[k], BAND, [(i, i ^ k) for i in range(8)])  22.6 us
    all_to_all x3, starting transfers between devices, swapped(): return lax.all_to_all(pieces, BAND, 0, 0, tiled=True)  15.8 us
    pallas_call x2, Pallas kernels, first(): pl.pallas_call(functools.partial(first_kernel, edge), out_shape=[PIECES,...  10.7 us
    pallas_call x1, Pallas kernels, second(): pl.pallas_call(second_kernel, out_shape=RES_SHAPES, in_specs=[SMEM] + [HB...  7.76 us
    pallas_call x2, Pallas kernels, pack(): pl.pallas_call(functools.partial(pack_kernel, split), out_shape=[held(24,...  6.31 us
    ppermute x2, starting transfers between devices, z_shift(): return lax.ppermute(face, ('quad',) + BAND, pairs)  5.32 us
    ppermute x1, waiting for transfers between devices, shards(): lax.ppermute(own, BAND, [(4 * a + b, 2 * b + a) for a in range(2) for b i...  4.81 us
  transfers between devices with their start and end apart: 25, of which 13 were waited for; matrix products, arithmetic and copies ran while one was open for 4% of the time, Pallas kernels for 18%

profile of v3, /device:TPU:1, one launch (start us, length us, event | category | flops | bytes accessed | tf_op | source)
XLA Modules:
  0.0 137.2 jit_solution(8403637365812367660)
XLA Ops:
  0.7 3.2 %pack_edge.1 = (f32[24,16,128]{2,1,0:T(8,128)}, f32[24,16,128]{2,1,0:T(8,128)}, f32[24,16,128]{2,1,0:T(8,128)}, f32[24,16,128]{2,1,0:T(8,128)}, f32[24,16,128]{2...) custom-call(s32[4]{0:T(128)S(1)} %pad_add_fusion.s_ref, ...), custom_call_target="tpu_custom_call" | custom-call | tf_op jit(solution)/shard_map/pack_edge/pallas_call | solution.py:124
  3.9 3.3 %collective-permute-start = (f32[24,16,128]{2,1,0:T(8,128)}, f32[24,16,128]{2,1,0:T(8,128)S(1)}, u32[]{:S(2)}, u32[]{:S(2)}) collective-permute-start(f32[24,16,128]{2,1,0:T(8,128)} %get-tuple-element.31), channel_id=1, source_target_pairs={{0,1},{1,0},{2,3},{3,2},{4,5},{5,4},{6,7},{7,6},{8,9},{9,8},{10,11... | collective-permute-start | bytes 589832 | tf_op jit(solution)/shard_map/ppermute | solution.py:484
  10.0 2.3 %collective-permute-start.4 = (f32[24,16,128]{2,1,0:T(8,128)}, f32[24,16,128]{2,1,0:T(8,128)S(1)}, u32[]{:S(2)}, u32[]{:S(2)}) collective-permute-start(f32[24,16,128]{2,1,0:T(8,128)} %get-tuple-element.35), channel_id=1, source_target_pairs={{0,5},{1,4},{2,7},{3,6},{4,1},{5,0},{6,3},{7,2},{8,13},{9,12},{10,... | collective-permute-start | bytes 589832 | tf_op jit(solution)/shard_map/ppermute | solution.py:484
  15.9 3.2 %pack_middle.1 = f32[8,24,16,128]{3,2,1,0:T(8,128)} custom-call(s32[4]{0:T(128)S(1)} %pad_add_fusion.s_ref, f32[21,2,128,128]{3,2,1,0:T(8,128)} %x_ref.3), custom_call_target="tpu_custom_call" | custom-call | tf_op jit(solution)/shard_map/pack_middle/pallas_call | solution.py:124
  19.0 4.3 %all-to-all-start = ((f32[8,24,16,128]{3,2,1,0:T(8,128)}), f32[8,24,16,128]{3,2,1,0:T(8,128)}, u32[]{:S(2)}, u32[]{:S(2)}) async-start(f32[8,24,16,128]{3,2,1,0:T(8,128)} %pack_middle.1), calls=%async_computation | async-start | bytes 3145728 | tf_op jit(solution)/shard_map/all_to_all | solution.py:477
  23.3 4.8 %collective-permute-done.4.refs_5_ = f32[24,16,128]{2,1,0:T(8,128)S(1)} collective-permute-done((f32[24,16,128]{2,1,0:T(8,128)}, f32[24,16,128]{2,1,0:T(8,128)S(1)}, u32[]{:S(2)}, u32[]{:S(2)}) %collective-permute-start.4) | collective-permute-done | bytes 196640 | tf_op jit(solution)/shard_map/ppermute | solution.py:484
  30.2 5.3 %collective-permute-done.6.refs_7_ = f32[24,16,128]{2,1,0:T(8,128)S(1)} collective-permute-done((f32[24,16,128]{2,1,0:T(8,128)}, f32[24,16,128]{2,1,0:T(8,128)S(1)}, u32[]{:S(2)}, u32[]{:S(2)}) %collective-permute-start.6) | collective-permute-done | bytes 196640 | tf_op jit(solution)/shard_map/ppermute | solution.py:484
  35.5 2.9 %faces.1 = (f32[84,16,128]{2,1,0:T(8,128)}, f32[84,16,128]{2,1,0:T(8,128)}) custom-call(f32[24,16,128]{2,1,0:T(8,128)S(1)} %copy-done, f32[24,16,128]{2,1,0:T(8,128)S(1)} %collective-permute-done.refs_1_, f32[24,16,128]{2,1,0:T(8,128)S(1)} %collective-permute-done.1.refs_2_, f32[24,16,128]{2,1,0:T(8,128)S(1)} %collective-permute-done.2.refs_3_, ...), custom_call_target="tpu_custom_call" | custom-call | flops 999999995904 | bytes 1000000000 | tf_op jit(solution)/shard_map/faces/pallas_call | solution.py:156
  39.8 4.0 %collective-permute-start.10 = (f32[84,16,128]{2,1,0:T(8,128)}, f32[84,16,128]{2,1,0:T(8,128)S(1)}, u32[]{:S(2)}, u32[]{:S(2)}) collective-permute-start(f32[84,16,128]{2,1,0:T(8,128)} %get-tuple-element.40), channel_id=1, source_target_pairs={{0,8},{1,9},{2,10},{3,11},{8,16},{9,17},{10,18},{11,19},{12,4},{13... | collective-permute-start | bytes 2064392 | tf_op jit(solution)/shard_map/ppermute | solution.py:521
  46.7 4.8 %collective-permute-done.7.refs_9_.refs_15_ = f32[7,2,16,128]{3,2,1,0:T(8,128)S(1)} collective-permute-done((f32[7,2,16,128]{3,2,1,0:T(8,128)S(1)}, f32[7,2,16,128]{3,2,1,0:T(8,128)S(1)}, u32[]{:S(2)}, u32[]{:S(2)}) %collective-permute-start.7) | collective-permute-done | bytes 114720 | tf_op jit(solution)/shard_map/ppermute | solution.py:530
  51.5 5.4 %first_middle.1 = (f32[8,21,16,128]{3,2,1,0:T(8,128)}, f32[4,4,24,128]{3,2,1,0:T(8,128)}, f32[4,4,24,128]{3,2,1,0:T(8,128)}) custom-call(s32[4]{0:T(128)S(1)} %copy-done.2, f32[24,16,128]{2,1,0:T(8,128)S(1)} %copy-done, f32[24,16,128]{2,1,0:T(8,128)S(1)} %collective-permute-done.refs_1_, f32[24,16,128]{2,1,0:T(8,128)S(1)} %collective-permute-done.1.refs_2_, ...), custom_call_target="tpu_custom_call" | custom-call | tf_op jit(solution)/shard_map/first_middle/pallas_call | solution.py:427
  56.9 6.1 %all-to-all-start.1 = ((f32[8,21,16,128]{3,2,1,0:T(8,128)}), f32[8,21,16,128]{3,2,1,0:T(8,128)}, u32[]{:S(2)}, u32[]{:S(2)}) async-start(f32[8,21,16,128]{3,2,1,0:T(8,128)} %get-tuple-element.38.refs_9_), calls=%async_computation.1 | async-start | bytes 2752512 | tf_op jit(solution)/shard_map/all_to_all | solution.py:477
  63.0 5.4 %first_edge.1 = (f32[8,21,16,128]{3,2,1,0:T(8,128)}, f32[4,4,24,128]{3,2,1,0:T(8,128)}, f32[4,4,24,128]{3,2,1,0:T(8,128)}, f32[84,16,128]{2,1,0:T(8,128)}, f32[84,16,128]{2,1,0:T(8,128)}) custom-call(s32[4]{0:T(128)S(1)} %copy-done.2, f32[24,16,128]{2,1,0:T(8,128)S(1)} %copy-done, ...), custom_call_target="tpu_custom_call", output_to_operand_aliasing={{1}: (14, {}), {2}: (15, {})} | custom-call | tf_op jit(solution)/shard_map/first_edge/pallas_call | solution.py:427
  71.6 3.8 %collective-permute-start.13 = (f32[4,4,24,128]{3,2,1,0:T(8,128)}, f32[4,4,24,128]{3,2,1,0:T(8,128)S(1)}, u32[]{:S(2)}, u32[]{:S(2)}) collective-permute-start(f32[4,4,24,128]{3,2,1,0:T(8,128)} %get-tuple-element.46), channel_id=1, source_target_pairs={{0,1},{1,2},{2,3},{3,4},{4,5},{5,6},{6,7},{8,9},{9,10},{10,11},{11... | collective-permute-start | bytes 589832 | tf_op jit(solution)/shard_map/ppermute | solution.py:538
  77.4 4.3 %all-to-all-done.1 = f32[8,21,16,128]{3,2,1,0:T(8,128)} async-done(((f32[8,21,16,128]{3,2,1,0:T(8,128)}), f32[8,21,16,128]{3,2,1,0:T(8,128)}, u32[]{:S(2)}, u32[]{:S(2)}) %all-to-all-start.1) | async-done | bytes 1376288 | tf_op jit(solution)/shard_map/all_to_all | solution.py:477
  81.7 5.5 %all-to-all-start.2 = ((f32[8,21,16,128]{3,2,1,0:T(8,128)}), f32[8,21,16,128]{3,2,1,0:T(8,128)}, u32[]{:S(2)}, u32[]{:S(2)}) async-start(f32[8,21,16,128]{3,2,1,0:T(8,128)} %get-tuple-element.43.refs_10_), calls=%async_computation.2 | async-start | bytes 2752512 | tf_op jit(solution)/shard_map/all_to_all | solution.py:477
  87.2 2.1 %collective-permute-done.12.refs_12_ = f32[84,16,128]{2,1,0:T(8,128)S(1)} collective-permute-done((f32[84,16,128]{2,1,0:T(8,128)}, f32[84,16,128]{2,1,0:T(8,128)S(1)}, u32[]{:S(2)}, u32[]{:S(2)}) %collective-permute-start.12) | collective-permute-done | bytes 688160 | tf_op jit(solution)/shard_map/ppermute | solution.py:537
  89.3 7.8 %second.1 = (f32[21,2,16,128]{3,2,1,0:T(8,128)}, f32[21,2,16,128]{3,2,1,0:T(8,128)}, f32[21,2,16,128]{3,2,1,0:T(8,128)}, f32[21,2,16,128]{3,2,1,0:T(8,128)}, f32...) custom-call(s32[4]{0:T(128)S(1)} %copy-done.2, ...), custom_call_target="tpu_custom_call" | custom-call | flops 999999995904 | bytes 1000000000 | tf_op jit(solution)/shard_map/second/pallas_call | solution.py:450
  97.1 2.9 %collective-permute-start.15 = (f32[21,2,16,128]{3,2,1,0:T(8,128)}, f32[21,2,16,128]{3,2,1,0:T(8,128)S(1)}, u32[]{:S(2)}, u32[]{:S(2)}) collective-permute-start(f32[21,2,16,128]{3,2,1,0:T(8,128)} %get-tuple-element.49), channel_id=1, source_target_pairs={{0,4},{1,5},{2,6},{3,7},{4,0},{5,1},{6,2},{7,3},{8,12},{9,13},{10,... | collective-permute-start | bytes 1032200 | tf_op jit(solution)/shard_map/ppermute | solution.py:484
  100.8 4.5 %collective-permute-start.18 = (f32[21,2,16,128]{3,2,1,0:T(8,128)}, f32[21,2,16,128]{3,2,1,0:T(8,128)S(1)}, u32[]{:S(2)}, u32[]{:S(2)}) collective-permute-start(f32[21,2,16,128]{3,2,1,0:T(8,128)} %get-tuple-element.52), channel_id=1, source_target_pairs={{0,5},{1,4},{2,7},{3,6},{4,1},{5,0},{6,3},{7,2},{8,13},{9,12},{10,... | collective-permute-start | bytes 1032200 | tf_op jit(solution)/shard_map/ppermute | solution.py:484
  105.6 7.6 %collective-permute-done.15 = f32[21,2,16,128]{3,2,1,0:T(8,128)S(1)} collective-permute-done((f32[21,2,16,128]{3,2,1,0:T(8,128)}, f32[21,2,16,128]{3,2,1,0:T(8,128)S(1)}, u32[]{:S(2)}, u32[]{:S(2)}) %collective-permute-start.15) | collective-permute-done | bytes 344096 | tf_op jit(solution)/shard_map/ppermute | solution.py:484
  113.2 2.1 %collective-permute-start.20 = (f32[21,2,16,128]{3,2,1,0:T(8,128)S(1)}, f32[21,2,16,128]{3,2,1,0:T(8,128)S(1)}, u32[]{:S(2)}, u32[]{:S(2)}) collective-permute-start(f32[21,2,16,128]{3,2,1,0:T(8,128)S(1)} %copy-done.9), channel_id=1, source_target_pairs={{0,7},{1,6},{2,5},{3,4},{4,3},{5,2},{6,1},{7,0},{8,15},{9,14},{10,... | collective-permute-start | bytes 1032200 | tf_op jit(solution)/shard_map/ppermute | solution.py:484
  115.4 3.7 %collective-permute-done.16 = f32[21,2,16,128]{3,2,1,0:T(8,128)S(1)} collective-permute-done((f32[21,2,16,128]{3,2,1,0:T(8,128)}, f32[21,2,16,128]{3,2,1,0:T(8,128)S(1)}, u32[]{:S(2)}, u32[]{:S(2)}) %collective-permute-start.16) | collective-permute-done | bytes 344096 | tf_op jit(solution)/shard_map/ppermute | solution.py:484
  121.3 7.4 %collective-permute-done.18 = f32[21,2,16,128]{3,2,1,0:T(8,128)S(1)} collective-permute-done((f32[21,2,16,128]{3,2,1,0:T(8,128)}, f32[21,2,16,128]{3,2,1,0:T(8,128)S(1)}, u32[]{:S(2)}, u32[]{:S(2)}) %collective-permute-start.18) | collective-permute-done | bytes 344096 | tf_op jit(solution)/shard_map/ppermute | solution.py:484
  (68 shorter events, 29.7 us)
Async XLA Ops:
  3.9 8.4 %collective-permute-start = (f32[24,16,128]{2,1,0:T(8,128)}, f32[24,16,128]{2,1,0:T(8,128)S(1)}, u32[]{:S(2)}, u32[]{:S(2)}) collective-permute-start(f32[24,16,128]{2,1,0:T(8,128)} %get-tuple-element.31), channel_id=1, source_target_pairs={{0,1},{1,0},{2,3},{3,2},{4,5},{5,4},{6,7},{7,6},{8,9},{9,8},{10,11... | collective-permute-start | bytes 589832 | tf_op jit(solution)/shard_map/ppermute | solution.py:484
  7.2 6.7 %collective-permute-start.1 = (f32[24,16,128]{2,1,0:T(8,128)}, f32[24,16,128]{2,1,0:T(8,128)S(1)}, u32[]{:S(2)}, u32[]{:S(2)}) collective-permute-start(f32[24,16,128]{2,1,0:T(8,128)} %get-tuple-element.32), channel_id=1, source_target_pairs={{0,2},{1,3},{2,0},{3,1},{4,6},{5,7},{6,4},{7,5},{8,10},{9,11},{10,... | collective-permute-start | bytes 589832 | tf_op jit(solution)/shard_map/ppermute | solution.py:484
  7.2 16.1 %collective-permute-start.2 = (f32[24,16,128]{2,1,0:T(8,128)}, f32[24,16,128]{2,1,0:T(8,128)S(1)}, u32[]{:S(2)}, u32[]{:S(2)}) collective-permute-start(f32[24,16,128]{2,1,0:T(8,128)} %get-tuple-element.33), channel_id=1, source_target_pairs={{0,3},{1,2},{2,1},{3,0},{4,7},{5,6},{6,5},{7,4},{8,11},{9,10},{10,... | collective-permute-start | bytes 589832 | tf_op jit(solution)/shard_map/ppermute | solution.py:484
  9.0 14.4 %collective-permute-start.3 = (f32[24,16,128]{2,1,0:T(8,128)}, f32[24,16,128]{2,1,0:T(8,128)S(1)}, u32[]{:S(2)}, u32[]{:S(2)}) collective-permute-start(f32[24,16,128]{2,1,0:T(8,128)} %get-tuple-element.34), channel_id=1, source_target_pairs={{0,4},{1,5},{2,6},{3,7},{4,0},{5,1},{6,2},{7,3},{8,12},{9,13},{10,... | collective-permute-start | bytes 589832 | tf_op jit(solution)/shard_map/ppermute | solution.py:484
  10.0 18.1 %collective-permute-start.4 = (f32[24,16,128]{2,1,0:T(8,128)}, f32[24,16,128]{2,1,0:T(8,128)S(1)}, u32[]{:S(2)}, u32[]{:S(2)}) collective-permute-start(f32[24,16,128]{2,1,0:T(8,128)} %get-tuple-element.35), channel_id=1, source_target_pairs={{0,5},{1,4},{2,7},{3,6},{4,1},{5,0},{6,3},{7,2},{8,13},{9,12},{10,... | collective-permute-start | bytes 589832 | tf_op jit(solution)/shard_map/ppermute | solution.py:484
  12.3 17.9 %collective-permute-start.5 = (f32[24,16,128]{2,1,0:T(8,128)}, f32[24,16,128]{2,1,0:T(8,128)S(1)}, u32[]{:S(2)}, u32[]{:S(2)}) collective-permute-start(f32[24,16,128]{2,1,0:T(8,128)} %get-tuple-element.36), channel_id=1, source_target_pairs={{0,6},{1,7},{2,4},{3,5},{4,2},{5,3},{6,0},{7,1},{8,14},{9,15},{10,... | collective-permute-start | bytes 589832 | tf_op jit(solution)/shard_map/ppermute | solution.py:484
  13.9 21.6 %collective-permute-start.6 = (f32[24,16,128]{2,1,0:T(8,128)}, f32[24,16,128]{2,1,0:T(8,128)S(1)}, u32[]{:S(2)}, u32[]{:S(2)}) collective-permute-start(f32[24,16,128]{2,1,0:T(8,128)} %get-tuple-element.37), channel_id=1, source_target_pairs={{0,7},{1,6},{2,5},{3,4},{4,3},{5,2},{6,1},{7,0},{8,15},{9,14},{10,... | collective-permute-start | bytes 589832 | tf_op jit(solution)/shard_map/ppermute | solution.py:484
  19.0 32.4 %all-to-all-start = ((f32[8,24,16,128]{3,2,1,0:T(8,128)}), f32[8,24,16,128]{3,2,1,0:T(8,128)}, u32[]{:S(2)}, u32[]{:S(2)}) async-start(f32[8,24,16,128]{3,2,1,0:T(8,128)} %pack_middle.1), calls=%async_computation | async-start | bytes 3145728 | tf_op jit(solution)/shard_map/all_to_all | solution.py:477
  38.5 24.5 %collective-permute-start.9 = (f32[84,16,128]{2,1,0:T(8,128)}, f32[84,16,128]{2,1,0:T(8,128)S(1)}, u32[]{:S(2)}, u32[]{:S(2)}) collective-permute-start(f32[84,16,128]{2,1,0:T(8,128)} %get-tuple-element.39), channel_id=1, source_target_pairs={{4,12},{5,13},{6,14},{7,15},{8,0},{9,1},{10,2},{11,3},{12,20},{13,... | collective-permute-start | bytes 2064392 | tf_op jit(solution)/shard_map/ppermute | solution.py:521
  39.8 23.2 %collective-permute-start.10 = (f32[84,16,128]{2,1,0:T(8,128)}, f32[84,16,128]{2,1,0:T(8,128)S(1)}, u32[]{:S(2)}, u32[]{:S(2)}) collective-permute-start(f32[84,16,128]{2,1,0:T(8,128)} %get-tuple-element.40), channel_id=1, source_target_pairs={{0,8},{1,9},{2,10},{3,11},{8,16},{9,17},{10,18},{11,19},{12,4},{13... | collective-permute-start | bytes 2064392 | tf_op jit(solution)/shard_map/ppermute | solution.py:521
  43.9 7.6 %collective-permute-start.7 = (f32[7,2,16,128]{3,2,1,0:T(8,128)S(1)}, f32[7,2,16,128]{3,2,1,0:T(8,128)S(1)}, u32[]{:S(2)}, u32[]{:S(2)}) collective-permute-start(f32[7,2,16,128]{3,2,1,0:T(8,128)S(1)} %get-tuple-element.59), channel_id=1, source_target_pairs={{0,0},{1,2},{2,4},{3,6},{4,1},{5,3},{6,5},{7,7},{8,8},{9,10},{10,1... | collective-permute-start | bytes 344072 | tf_op jit(solution)/shard_map/ppermute | solution.py:530
  56.9 24.8 %all-to-all-start.1 = ((f32[8,21,16,128]{3,2,1,0:T(8,128)}), f32[8,21,16,128]{3,2,1,0:T(8,128)}, u32[]{:S(2)}, u32[]{:S(2)}) async-start(f32[8,21,16,128]{3,2,1,0:T(8,128)} %get-tuple-element.38.refs_9_), calls=%async_computation.1 | async-start | bytes 2752512 | tf_op jit(solution)/shard_map/all_to_all | solution.py:477
  68.3 18.9 %collective-permute-start.11 = (f32[84,16,128]{2,1,0:T(8,128)}, f32[84,16,128]{2,1,0:T(8,128)S(1)}, u32[]{:S(2)}, u32[]{:S(2)}) collective-permute-start(f32[84,16,128]{2,1,0:T(8,128)} %get-tuple-element.44), channel_id=1, source_target_pairs={{0,8},{8,16},{16,24},{24,32},{32,40},{40,48},{48,56},{56,64},{64,7... | collective-permute-start | bytes 2064392 | tf_op jit(solution)/shard_map/ppermute | solution.py:536
  70.3 19.0 %collective-permute-start.12 = (f32[84,16,128]{2,1,0:T(8,128)}, f32[84,16,128]{2,1,0:T(8,128)S(1)}, u32[]{:S(2)}, u32[]{:S(2)}) collective-permute-start(f32[84,16,128]{2,1,0:T(8,128)} %get-tuple-element.45), channel_id=1, source_target_pairs={{8,0},{16,8},{24,16},{32,24},{40,32},{48,40},{56,48},{64,56},{72,6... | collective-permute-start | bytes 2064392 | tf_op jit(solution)/shard_map/ppermute | solution.py:537
  71.6 15.6 %collective-permute-start.13 = (f32[4,4,24,128]{3,2,1,0:T(8,128)}, f32[4,4,24,128]{3,2,1,0:T(8,128)S(1)}, u32[]{:S(2)}, u32[]{:S(2)}) collective-permute-start(f32[4,4,24,128]{3,2,1,0:T(8,128)} %get-tuple-element.46), channel_id=1, source_target_pairs={{0,1},{1,2},{2,3},{3,4},{4,5},{5,6},{6,7},{8,9},{9,10},{10,11},{11... | collective-permute-start | bytes 589832 | tf_op jit(solution)/shard_map/ppermute | solution.py:538
  75.5 11.7 %collective-permute-start.14 = (f32[4,4,24,128]{3,2,1,0:T(8,128)}, f32[4,4,24,128]{3,2,1,0:T(8,128)}, u32[]{:S(2)}, u32[]{:S(2)}) collective-permute-start(f32[4,4,24,128]{3,2,1,0:T(8,128)} %get-tuple-element.47), channel_id=1, source_target_pairs={{1,0},{2,1},{3,2},{4,3},{5,4},{6,5},{7,6},{9,8},{10,9},{11,10},{12... | collective-permute-start | bytes 589832 | tf_op jit(solution)/shard_map/ppermute | solution.py:539
  81.7 50.1 %all-to-all-start.2 = ((f32[8,21,16,128]{3,2,1,0:T(8,128)}), f32[8,21,16,128]{3,2,1,0:T(8,128)}, u32[]{:S(2)}, u32[]{:S(2)}) async-start(f32[8,21,16,128]{3,2,1,0:T(8,128)} %get-tuple-element.43.refs_10_), calls=%async_computation.2 | async-start | bytes 2752512 | tf_op jit(solution)/shard_map/all_to_all | solution.py:477
  97.1 16.1 %collective-permute-start.15 = (f32[21,2,16,128]{3,2,1,0:T(8,128)}, f32[21,2,16,128]{3,2,1,0:T(8,128)S(1)}, u32[]{:S(2)}, u32[]{:S(2)}) collective-permute-start(f32[21,2,16,128]{3,2,1,0:T(8,128)} %get-tuple-element.49), channel_id=1, source_target_pairs={{0,4},{1,5},{2,6},{3,7},{4,0},{5,1},{6,2},{7,3},{8,12},{9,13},{10,... | collective-permute-start | bytes 1032200 | tf_op jit(solution)/shard_map/ppermute | solution.py:484
  100.0 19.1 %collective-permute-start.16 = (f32[21,2,16,128]{3,2,1,0:T(8,128)}, f32[21,2,16,128]{3,2,1,0:T(8,128)S(1)}, u32[]{:S(2)}, u32[]{:S(2)}) collective-permute-start(f32[21,2,16,128]{3,2,1,0:T(8,128)} %get-tuple-element.50), channel_id=1, source_target_pairs={{0,2},{1,3},{2,0},{3,1},{4,6},{5,7},{6,4},{7,5},{8,10},{9,11},{10,... | collective-permute-start | bytes 1032200 | tf_op jit(solution)/shard_map/ppermute | solution.py:484
  100.2 21.1 %collective-permute-start.17 = (f32[21,2,16,128]{3,2,1,0:T(8,128)}, f32[21,2,16,128]{3,2,1,0:T(8,128)S(1)}, u32[]{:S(2)}, u32[]{:S(2)}) collective-permute-start(f32[21,2,16,128]{3,2,1,0:T(8,128)} %get-tuple-element.51), channel_id=1, source_target_pairs={{0,6},{1,7},{2,4},{3,5},{4,2},{5,3},{6,0},{7,1},{8,14},{9,15},{10,... | collective-permute-start | bytes 1032200 | tf_op jit(solution)/shard_map/ppermute | solution.py:484
  100.8 27.9 %collective-permute-start.18 = (f32[21,2,16,128]{3,2,1,0:T(8,128)}, f32[21,2,16,128]{3,2,1,0:T(8,128)S(1)}, u32[]{:S(2)}, u32[]{:S(2)}) collective-permute-start(f32[21,2,16,128]{3,2,1,0:T(8,128)} %get-tuple-element.52), channel_id=1, source_target_pairs={{0,5},{1,4},{2,7},{3,6},{4,1},{5,0},{6,3},{7,2},{8,13},{9,12},{10,... | collective-permute-start | bytes 1032200 | tf_op jit(solution)/shard_map/ppermute | solution.py:484
  105.2 29.1 %collective-permute-start.19 = (f32[21,2,16,128]{3,2,1,0:T(8,128)}, f32[21,2,16,128]{3,2,1,0:T(8,128)S(1)}, u32[]{:S(2)}, u32[]{:S(2)}) collective-permute-start(f32[21,2,16,128]{3,2,1,0:T(8,128)} %get-tuple-element.55), channel_id=1, source_target_pairs={{0,3},{1,2},{2,1},{3,0},{4,7},{5,6},{6,5},{7,4},{8,11},{9,10},{10,... | collective-permute-start | bytes 1032200 | tf_op jit(solution)/shard_map/ppermute | solution.py:484
  113.2 22.5 %collective-permute-start.20 = (f32[21,2,16,128]{3,2,1,0:T(8,128)S(1)}, f32[21,2,16,128]{3,2,1,0:T(8,128)S(1)}, u32[]{:S(2)}, u32[]{:S(2)}) collective-permute-start(f32[21,2,16,128]{3,2,1,0:T(8,128)S(1)} %copy-done.9), channel_id=1, source_target_pairs={{0,7},{1,6},{2,5},{3,4},{4,3},{5,2},{6,1},{7,0},{8,15},{9,14},{10,... | collective-permute-start | bytes 1032200 | tf_op jit(solution)/shard_map/ppermute | solution.py:484
  119.1 17.4 %collective-permute-start.21 = (f32[21,2,16,128]{3,2,1,0:T(8,128)S(1)}, f32[21,2,16,128]{3,2,1,0:T(8,128)S(1)}, u32[]{:S(2)}, u32[]{:S(2)}) collective-permute-start(f32[21,2,16,128]{3,2,1,0:T(8,128)S(1)} %copy-done.8), channel_id=1, source_target_pairs={{0,1},{1,0},{2,3},{3,2},{4,5},{5,4},{6,7},{7,6},{8,9},{9,8},{10,11... | collective-permute-start | bytes 1032200 | tf_op jit(solution)/shard_map/ppermute | solution.py:484
  (11 other events, 126.4 us)

commit v4 on v3

--- a/solution.py
+++ b/solution.py
@@ -442,6 +442,7 @@
         ],
         compiler_params=pltpu.CompilerParams(vmem_limit_bytes=VMEM_BYTES),
         input_output_aliases={14: 1, 15: 2} if edge else {},
+        cost_estimate=None if edge else pl.CostEstimate(flops=10**10, transcendentals=0, bytes_accessed=10**7),
         name="first_edge" if edge else "first_middle",
     )(info, *arrays)
 

time: 139 us -> 138 us (level)
  waiting for transfers between devices: 44.5 us -> 39.5 us
  starting transfers between devices: 55.6 us -> 59.2 us
    ppermute x14, waiting for transfers between devices: 33.2 us -> 27.4 us  [exchange(): got[k] = lax.ppermute(pieces[k], BAND, [(i, i ^ k) for i in range(8)])]
    all_to_all x3, waiting for transfers between devices: 4.3 us -> 8.41 us  [swapped(): return lax.all_to_all(pieces, BAND, 0, 0, tiled=True)]
    ppermute x1, waiting for transfers between devices: 4.81 us -> 1.73 us  [shards(): lax.ppermute(own, BAND, [(4 * a + b, 2 * b + a) for a in range(2) for b i...]
    all_to_all x3, starting transfers between devices: 15.8 us -> 17.6 us  [swapped(): return lax.all_to_all(pieces, BAND, 0, 0, tiled=True)]
  transfers between devices with their start and end apart: 25 -> 25, of which waited for: 13 -> 13; matrix products, arithmetic and copies ran while one was open for 4% -> 5% of each run, Pallas kernels for 18% -> 18%
where the time goes in v4:
time: 138 us; the launch traced here: 137 us
  starting transfers between devices  59.2 us (43%)
  waiting for transfers between devices  39.5 us (29%)
  Pallas kernels  28.1 us (20%)
  local copies, waits for them, and re-layouts  8.28 us (6%)
    ppermute x14, waiting for transfers between devices, exchange(): got[k] = lax.ppermute(pieces[k], BAND, [(i, i ^ k) for i in range(8)])  27.4 us
    ppermute x14, starting transfers between devices, exchange(): got[k] = lax.ppermute(pieces[k], BAND, [(i, i ^ k) for i in range(8)])  22.6 us
    all_to_all x3, starting transfers between devices, swapped(): return lax.all_to_all(pieces, BAND, 0, 0, tiled=True)  17.6 us
    pallas_call x2, Pallas kernels, first(): pl.pallas_call(functools.partial(first_kernel, edge), out_shape=[PIECES,...  10.8 us
    all_to_all x3, waiting for transfers between devices, swapped(): return lax.all_to_all(pieces, BAND, 0, 0, tiled=True)  8.41 us
    pallas_call x1, Pallas kernels, second(): pl.pallas_call(second_kernel, out_shape=RES_SHAPES, in_specs=[SMEM] + [HB...  8.06 us
    pallas_call x2, Pallas kernels, pack(): pl.pallas_call(functools.partial(pack_kernel, split), out_shape=[held(24,...  6.3 us
    ppermute x2, starting transfers between devices, z_shift(): return lax.ppermute(face, ('quad',) + BAND, pairs)  5.32 us
  transfers between devices with their start and end apart: 25, of which 13 were waited for; matrix products, arithmetic and copies ran while one was open for 5% of the time, Pallas kernels for 18%

profile of v4, /device:TPU:1, one launch (start us, length us, event | category | flops | bytes accessed | tf_op | source)
XLA Modules:
  0.0 136.9 jit_solution(4669387111660972527)
XLA Ops:
  0.7 3.2 %pack_edge.1 = (f32[24,16,128]{2,1,0:T(8,128)}, f32[24,16,128]{2,1,0:T(8,128)}, f32[24,16,128]{2,1,0:T(8,128)}, f32[24,16,128]{2,1,0:T(8,128)}, f32[24,16,128]{2...) custom-call(s32[4]{0:T(128)S(1)} %pad_add_fusion.s_ref, ...), custom_call_target="tpu_custom_call" | custom-call | tf_op jit(solution)/shard_map/pack_edge/pallas_call | solution.py:124
  3.9 3.3 %collective-permute-start = (f32[24,16,128]{2,1,0:T(8,128)}, f32[24,16,128]{2,1,0:T(8,128)S(1)}, u32[]{:S(2)}, u32[]{:S(2)}) collective-permute-start(f32[24,16,128]{2,1,0:T(8,128)} %get-tuple-element.31), channel_id=1, source_target_pairs={{0,1},{1,0},{2,3},{3,2},{4,5},{5,4},{6,7},{7,6},{8,9},{9,8},{10,11... | collective-permute-start | bytes 589832 | tf_op jit(solution)/shard_map/ppermute | solution.py:485
  10.0 2.3 %collective-permute-start.4 = (f32[24,16,128]{2,1,0:T(8,128)}, f32[24,16,128]{2,1,0:T(8,128)S(1)}, u32[]{:S(2)}, u32[]{:S(2)}) collective-permute-start(f32[24,16,128]{2,1,0:T(8,128)} %get-tuple-element.35), channel_id=1, source_target_pairs={{0,5},{1,4},{2,7},{3,6},{4,1},{5,0},{6,3},{7,2},{8,13},{9,12},{10,... | collective-permute-start | bytes 589832 | tf_op jit(solution)/shard_map/ppermute | solution.py:485
  15.9 3.2 %pack_middle.1 = f32[8,24,16,128]{3,2,1,0:T(8,128)} custom-call(s32[4]{0:T(128)S(1)} %pad_add_fusion.s_ref, f32[21,2,128,128]{3,2,1,0:T(8,128)} %x_ref.3), custom_call_target="tpu_custom_call" | custom-call | tf_op jit(solution)/shard_map/pack_middle/pallas_call | solution.py:124
  19.1 4.4 %all-to-all-start = ((f32[8,24,16,128]{3,2,1,0:T(8,128)}), f32[8,24,16,128]{3,2,1,0:T(8,128)}, u32[]{:S(2)}, u32[]{:S(2)}) async-start(f32[8,24,16,128]{3,2,1,0:T(8,128)} %pack_middle.1), calls=%async_computation | async-start | bytes 3145728 | tf_op jit(solution)/shard_map/all_to_all | solution.py:478
  24.2 2.9 %collective-permute-start.7 = (f32[7,2,16,128]{3,2,1,0:T(8,128)}, f32[7,2,16,128]{3,2,1,0:T(8,128)}, u32[]{:S(2)}, u32[]{:S(2)}) collective-permute-start(f32[7,2,16,128]{3,2,1,0:T(8,128)} %get-tuple-element.59), channel_id=1, source_target_pairs={{0,0},{1,2},{2,4},{3,6},{4,1},{5,3},{6,5},{7,7},{8,8},{9,10},{10,1... | collective-permute-start | bytes 344072 | tf_op jit(solution)/shard_map/ppermute | solution.py:531
  30.0 5.5 %collective-permute-done.6.refs_7_ = f32[24,16,128]{2,1,0:T(8,128)S(1)} collective-permute-done((f32[24,16,128]{2,1,0:T(8,128)}, f32[24,16,128]{2,1,0:T(8,128)S(1)}, u32[]{:S(2)}, u32[]{:S(2)}) %collective-permute-start.6) | collective-permute-done | bytes 196640 | tf_op jit(solution)/shard_map/ppermute | solution.py:485
  35.5 2.9 %faces.1 = (f32[84,16,128]{2,1,0:T(8,128)}, f32[84,16,128]{2,1,0:T(8,128)}) custom-call(f32[24,16,128]{2,1,0:T(8,128)S(1)} %copy-done, f32[24,16,128]{2,1,0:T(8,128)S(1)} %collective-permute-done.refs_1_, f32[24,16,128]{2,1,0:T(8,128)S(1)} %collective-permute-done.1.refs_2_, f32[24,16,128]{2,1,0:T(8,128)S(1)} %collective-permute-done.2.refs_3_, ...), custom_call_target="tpu_custom_call" | custom-call | flops 999999995904 | bytes 1000000000 | tf_op jit(solution)/shard_map/faces/pallas_call | solution.py:156
  39.7 4.0 %collective-permute-start.10 = (f32[84,16,128]{2,1,0:T(8,128)}, f32[84,16,128]{2,1,0:T(8,128)S(1)}, u32[]{:S(2)}, u32[]{:S(2)}) collective-permute-start(f32[84,16,128]{2,1,0:T(8,128)} %get-tuple-element.40), channel_id=1, source_target_pairs={{0,8},{1,9},{2,10},{3,11},{8,16},{9,17},{10,18},{11,19},{12,4},{13... | collective-permute-start | bytes 2064392 | tf_op jit(solution)/shard_map/ppermute | solution.py:522
  45.5 4.0 %all-to-all-done.refs_8_ = f32[8,24,16,128]{3,2,1,0:T(8,128)} async-done(((f32[8,24,16,128]{3,2,1,0:T(8,128)}), f32[8,24,16,128]{3,2,1,0:T(8,128)}, u32[]{:S(2)}, u32[]{:S(2)}) %all-to-all-start) | async-done | bytes 1572896 | tf_op jit(solution)/shard_map/all_to_all | solution.py:478
  49.5 5.4 %first_middle.1 = (f32[8,21,16,128]{3,2,1,0:T(8,128)}, f32[4,4,24,128]{3,2,1,0:T(8,128)}, f32[4,4,24,128]{3,2,1,0:T(8,128)}) custom-call(s32[4]{0:T(128)S(1)} %copy-done.2, f32[24,16,128]{2,1,0:T(8,128)S(1)} %copy-done, f32[24,16,128]{2,1,0:T(8,128)S(1)} %collective-permute-done.refs_1_, f32[24,16,128]{2,1,0:T(8,128)S(1)} %collective-permute-done.1.refs_2_, ...), custom_call_target="tpu_custom_call" | custom-call | flops 10000000000 | bytes 10000000 | tf_op jit(solution)/shard_map/first_middle/pallas_call | solution.py:427
  54.9 7.7 %all-to-all-start.1 = ((f32[8,21,16,128]{3,2,1,0:T(8,128)}), f32[8,21,16,128]{3,2,1,0:T(8,128)}, u32[]{:S(2)}, u32[]{:S(2)}) async-start(f32[8,21,16,128]{3,2,1,0:T(8,128)} %get-tuple-element.38.refs_9_), calls=%async_computation.1 | async-start | bytes 2752512 | tf_op jit(solution)/shard_map/all_to_all | solution.py:478
  62.6 5.4 %first_edge.1 = (f32[8,21,16,128]{3,2,1,0:T(8,128)}, f32[4,4,24,128]{3,2,1,0:T(8,128)}, f32[4,4,24,128]{3,2,1,0:T(8,128)}, f32[84,16,128]{2,1,0:T(8,128)}, f32[84,16,128]{2,1,0:T(8,128)}) custom-call(s32[4]{0:T(128)S(1)} %copy-done.2, f32[24,16,128]{2,1,0:T(8,128)S(1)} %copy-done, ...), custom_call_target="tpu_custom_call", output_to_operand_aliasing={{1}: (14, {}), {2}: (15, {})} | custom-call | tf_op jit(solution)/shard_map/first_edge/pallas_call | solution.py:427
  71.2 3.8 %collective-permute-start.13 = (f32[4,4,24,128]{3,2,1,0:T(8,128)}, f32[4,4,24,128]{3,2,1,0:T(8,128)S(1)}, u32[]{:S(2)}, u32[]{:S(2)}) collective-permute-start(f32[4,4,24,128]{3,2,1,0:T(8,128)} %get-tuple-element.46), channel_id=1, source_target_pairs={{0,1},{1,2},{2,3},{3,4},{4,5},{5,6},{6,7},{8,9},{9,10},{10,11},{11... | collective-permute-start | bytes 589832 | tf_op jit(solution)/shard_map/ppermute | solution.py:539
  77.0 4.4 %all-to-all-done.1 = f32[8,21,16,128]{3,2,1,0:T(8,128)} async-done(((f32[8,21,16,128]{3,2,1,0:T(8,128)}), f32[8,21,16,128]{3,2,1,0:T(8,128)}, u32[]{:S(2)}, u32[]{:S(2)}) %all-to-all-start.1) | async-done | bytes 1376288 | tf_op jit(solution)/shard_map/all_to_all | solution.py:478
  81.4 5.5 %all-to-all-start.2 = ((f32[8,21,16,128]{3,2,1,0:T(8,128)}), f32[8,21,16,128]{3,2,1,0:T(8,128)}, u32[]{:S(2)}, u32[]{:S(2)}) async-start(f32[8,21,16,128]{3,2,1,0:T(8,128)} %get-tuple-element.43.refs_10_), calls=%async_computation.2 | async-start | bytes 2752512 | tf_op jit(solution)/shard_map/all_to_all | solution.py:478
  86.9 2.0 %collective-permute-done.12.refs_12_ = f32[84,16,128]{2,1,0:T(8,128)S(1)} collective-permute-done((f32[84,16,128]{2,1,0:T(8,128)}, f32[84,16,128]{2,1,0:T(8,128)S(1)}, u32[]{:S(2)}, u32[]{:S(2)}) %collective-permute-start.12) | collective-permute-done | bytes 688160 | tf_op jit(solution)/shard_map/ppermute | solution.py:538
  88.9 8.1 %second.1 = (f32[21,2,16,128]{3,2,1,0:T(8,128)}, f32[21,2,16,128]{3,2,1,0:T(8,128)}, f32[21,2,16,128]{3,2,1,0:T(8,128)}, f32[21,2,16,128]{3,2,1,0:T(8,128)}, f32...) custom-call(s32[4]{0:T(128)S(1)} %copy-done.2, ...), custom_call_target="tpu_custom_call" | custom-call | flops 999999995904 | bytes 1000000000 | tf_op jit(solution)/shard_map/second/pallas_call | solution.py:451
  97.0 2.9 %collective-permute-start.15 = (f32[21,2,16,128]{3,2,1,0:T(8,128)}, f32[21,2,16,128]{3,2,1,0:T(8,128)S(1)}, u32[]{:S(2)}, u32[]{:S(2)}) collective-permute-start(f32[21,2,16,128]{3,2,1,0:T(8,128)} %get-tuple-element.49), channel_id=1, source_target_pairs={{0,4},{1,5},{2,6},{3,7},{4,0},{5,1},{6,2},{7,3},{8,12},{9,13},{10,... | collective-permute-start | bytes 1032200 | tf_op jit(solution)/shard_map/ppermute | solution.py:485
  100.6 4.5 %collective-permute-start.18 = (f32[21,2,16,128]{3,2,1,0:T(8,128)}, f32[21,2,16,128]{3,2,1,0:T(8,128)S(1)}, u32[]{:S(2)}, u32[]{:S(2)}) collective-permute-start(f32[21,2,16,128]{3,2,1,0:T(8,128)} %get-tuple-element.52), channel_id=1, source_target_pairs={{0,5},{1,4},{2,7},{3,6},{4,1},{5,0},{6,3},{7,2},{8,13},{9,12},{10,... | collective-permute-start | bytes 1032200 | tf_op jit(solution)/shard_map/ppermute | solution.py:485
  105.5 7.4 %collective-permute-done.15 = f32[21,2,16,128]{3,2,1,0:T(8,128)S(1)} collective-permute-done((f32[21,2,16,128]{3,2,1,0:T(8,128)}, f32[21,2,16,128]{3,2,1,0:T(8,128)S(1)}, u32[]{:S(2)}, u32[]{:S(2)}) %collective-permute-start.15) | collective-permute-done | bytes 344096 | tf_op jit(solution)/shard_map/ppermute | solution.py:485
  112.9 2.1 %collective-permute-start.20 = (f32[21,2,16,128]{3,2,1,0:T(8,128)S(1)}, f32[21,2,16,128]{3,2,1,0:T(8,128)S(1)}, u32[]{:S(2)}, u32[]{:S(2)}) collective-permute-start(f32[21,2,16,128]{3,2,1,0:T(8,128)S(1)} %copy-done.9), channel_id=1, source_target_pairs={{0,7},{1,6},{2,5},{3,4},{4,3},{5,2},{6,1},{7,0},{8,15},{9,14},{10,... | collective-permute-start | bytes 1032200 | tf_op jit(solution)/shard_map/ppermute | solution.py:485
  115.1 3.7 %collective-permute-done.16 = f32[21,2,16,128]{3,2,1,0:T(8,128)S(1)} collective-permute-done((f32[21,2,16,128]{3,2,1,0:T(8,128)}, f32[21,2,16,128]{3,2,1,0:T(8,128)S(1)}, u32[]{:S(2)}, u32[]{:S(2)}) %collective-permute-start.16) | collective-permute-done | bytes 344096 | tf_op jit(solution)/shard_map/ppermute | solution.py:485
  121.0 7.4 %collective-permute-done.18 = f32[21,2,16,128]{3,2,1,0:T(8,128)S(1)} collective-permute-done((f32[21,2,16,128]{3,2,1,0:T(8,128)}, f32[21,2,16,128]{3,2,1,0:T(8,128)S(1)}, u32[]{:S(2)}, u32[]{:S(2)}) %collective-permute-start.18) | collective-permute-done | bytes 344096 | tf_op jit(solution)/shard_map/ppermute | solution.py:485
  (68 shorter events, 30.0 us)
Async XLA Ops:
  3.9 8.4 %collective-permute-start = (f32[24,16,128]{2,1,0:T(8,128)}, f32[24,16,128]{2,1,0:T(8,128)S(1)}, u32[]{:S(2)}, u32[]{:S(2)}) collective-permute-start(f32[24,16,128]{2,1,0:T(8,128)} %get-tuple-element.31), channel_id=1, source_target_pairs={{0,1},{1,0},{2,3},{3,2},{4,5},{5,4},{6,7},{7,6},{8,9},{9,8},{10,11... | collective-permute-start | bytes 589832 | tf_op jit(solution)/shard_map/ppermute | solution.py:485
  7.2 17.0 %collective-permute-start.2 = (f32[24,16,128]{2,1,0:T(8,128)}, f32[24,16,128]{2,1,0:T(8,128)S(1)}, u32[]{:S(2)}, u32[]{:S(2)}) collective-permute-start(f32[24,16,128]{2,1,0:T(8,128)} %get-tuple-element.33), channel_id=1, source_target_pairs={{0,3},{1,2},{2,1},{3,0},{4,7},{5,6},{6,5},{7,4},{8,11},{9,10},{10,... | collective-permute-start | bytes 589832 | tf_op jit(solution)/shard_map/ppermute | solution.py:485
  9.0 18.1 %collective-permute-start.3 = (f32[24,16,128]{2,1,0:T(8,128)}, f32[24,16,128]{2,1,0:T(8,128)S(1)}, u32[]{:S(2)}, u32[]{:S(2)}) collective-permute-start(f32[24,16,128]{2,1,0:T(8,128)} %get-tuple-element.34), channel_id=1, source_target_pairs={{0,4},{1,5},{2,6},{3,7},{4,0},{5,1},{6,2},{7,3},{8,12},{9,13},{10,... | collective-permute-start | bytes 589832 | tf_op jit(solution)/shard_map/ppermute | solution.py:485
  10.0 19.0 %collective-permute-start.4 = (f32[24,16,128]{2,1,0:T(8,128)}, f32[24,16,128]{2,1,0:T(8,128)S(1)}, u32[]{:S(2)}, u32[]{:S(2)}) collective-permute-start(f32[24,16,128]{2,1,0:T(8,128)} %get-tuple-element.35), channel_id=1, source_target_pairs={{0,5},{1,4},{2,7},{3,6},{4,1},{5,0},{6,3},{7,2},{8,13},{9,12},{10,... | collective-permute-start | bytes 589832 | tf_op jit(solution)/shard_map/ppermute | solution.py:485
  12.3 17.7 %collective-permute-start.5 = (f32[24,16,128]{2,1,0:T(8,128)}, f32[24,16,128]{2,1,0:T(8,128)S(1)}, u32[]{:S(2)}, u32[]{:S(2)}) collective-permute-start(f32[24,16,128]{2,1,0:T(8,128)} %get-tuple-element.36), channel_id=1, source_target_pairs={{0,6},{1,7},{2,4},{3,5},{4,2},{5,3},{6,0},{7,1},{8,14},{9,15},{10,... | collective-permute-start | bytes 589832 | tf_op jit(solution)/shard_map/ppermute | solution.py:485
  13.9 21.6 %collective-permute-start.6 = (f32[24,16,128]{2,1,0:T(8,128)}, f32[24,16,128]{2,1,0:T(8,128)S(1)}, u32[]{:S(2)}, u32[]{:S(2)}) collective-permute-start(f32[24,16,128]{2,1,0:T(8,128)} %get-tuple-element.37), channel_id=1, source_target_pairs={{0,7},{1,6},{2,5},{3,4},{4,3},{5,2},{6,1},{7,0},{8,15},{9,14},{10,... | collective-permute-start | bytes 589832 | tf_op jit(solution)/shard_map/ppermute | solution.py:485
  19.1 30.5 %all-to-all-start = ((f32[8,24,16,128]{3,2,1,0:T(8,128)}), f32[8,24,16,128]{3,2,1,0:T(8,128)}, u32[]{:S(2)}, u32[]{:S(2)}) async-start(f32[8,24,16,128]{3,2,1,0:T(8,128)} %pack_middle.1), calls=%async_computation | async-start | bytes 3145728 | tf_op jit(solution)/shard_map/all_to_all | solution.py:478
  24.2 21.3 %collective-permute-start.7 = (f32[7,2,16,128]{3,2,1,0:T(8,128)}, f32[7,2,16,128]{3,2,1,0:T(8,128)}, u32[]{:S(2)}, u32[]{:S(2)}) collective-permute-start(f32[7,2,16,128]{3,2,1,0:T(8,128)} %get-tuple-element.59), channel_id=1, source_target_pairs={{0,0},{1,2},{2,4},{3,6},{4,1},{5,3},{6,5},{7,7},{8,8},{9,10},{10,1... | collective-permute-start | bytes 344072 | tf_op jit(solution)/shard_map/ppermute | solution.py:531
  27.1 18.4 %collective-permute-start.8 = (f32[7,2,16,128]{3,2,1,0:T(8,128)}, f32[7,2,16,128]{3,2,1,0:T(8,128)}, u32[]{:S(2)}, u32[]{:S(2)}) collective-permute-start(f32[7,2,16,128]{3,2,1,0:T(8,128)} %get-tuple-element.58), channel_id=1, source_target_pairs={{0,1},{1,3},{2,5},{3,7},{4,0},{5,2},{6,4},{7,6},{8,9},{9,11},{10,1... | collective-permute-start | bytes 344072 | tf_op jit(solution)/shard_map/ppermute | solution.py:532
  38.4 24.2 %collective-permute-start.9 = (f32[84,16,128]{2,1,0:T(8,128)}, f32[84,16,128]{2,1,0:T(8,128)S(1)}, u32[]{:S(2)}, u32[]{:S(2)}) collective-permute-start(f32[84,16,128]{2,1,0:T(8,128)} %get-tuple-element.39), channel_id=1, source_target_pairs={{4,12},{5,13},{6,14},{7,15},{8,0},{9,1},{10,2},{11,3},{12,20},{13,... | collective-permute-start | bytes 2064392 | tf_op jit(solution)/shard_map/ppermute | solution.py:522
  39.7 22.9 %collective-permute-start.10 = (f32[84,16,128]{2,1,0:T(8,128)}, f32[84,16,128]{2,1,0:T(8,128)S(1)}, u32[]{:S(2)}, u32[]{:S(2)}) collective-permute-start(f32[84,16,128]{2,1,0:T(8,128)} %get-tuple-element.40), channel_id=1, source_target_pairs={{0,8},{1,9},{2,10},{3,11},{8,16},{9,17},{10,18},{11,19},{12,4},{13... | collective-permute-start | bytes 2064392 | tf_op jit(solution)/shard_map/ppermute | solution.py:522
  54.9 26.4 %all-to-all-start.1 = ((f32[8,21,16,128]{3,2,1,0:T(8,128)}), f32[8,21,16,128]{3,2,1,0:T(8,128)}, u32[]{:S(2)}, u32[]{:S(2)}) async-start(f32[8,21,16,128]{3,2,1,0:T(8,128)} %get-tuple-element.38.refs_9_), calls=%async_computation.1 | async-start | bytes 2752512 | tf_op jit(solution)/shard_map/all_to_all | solution.py:478
  68.0 18.8 %collective-permute-start.11 = (f32[84,16,128]{2,1,0:T(8,128)}, f32[84,16,128]{2,1,0:T(8,128)S(1)}, u32[]{:S(2)}, u32[]{:S(2)}) collective-permute-start(f32[84,16,128]{2,1,0:T(8,128)} %get-tuple-element.44), channel_id=1, source_target_pairs={{0,8},{8,16},{16,24},{24,32},{32,40},{40,48},{48,56},{56,64},{64,7... | collective-permute-start | bytes 2064392 | tf_op jit(solution)/shard_map/ppermute | solution.py:537
  69.9 19.0 %collective-permute-start.12 = (f32[84,16,128]{2,1,0:T(8,128)}, f32[84,16,128]{2,1,0:T(8,128)S(1)}, u32[]{:S(2)}, u32[]{:S(2)}) collective-permute-start(f32[84,16,128]{2,1,0:T(8,128)} %get-tuple-element.45), channel_id=1, source_target_pairs={{8,0},{16,8},{24,16},{32,24},{40,32},{48,40},{56,48},{64,56},{72,6... | collective-permute-start | bytes 2064392 | tf_op jit(solution)/shard_map/ppermute | solution.py:538
  71.2 15.7 %collective-permute-start.13 = (f32[4,4,24,128]{3,2,1,0:T(8,128)}, f32[4,4,24,128]{3,2,1,0:T(8,128)S(1)}, u32[]{:S(2)}, u32[]{:S(2)}) collective-permute-start(f32[4,4,24,128]{3,2,1,0:T(8,128)} %get-tuple-element.46), channel_id=1, source_target_pairs={{0,1},{1,2},{2,3},{3,4},{4,5},{5,6},{6,7},{8,9},{9,10},{10,11},{11... | collective-permute-start | bytes 589832 | tf_op jit(solution)/shard_map/ppermute | solution.py:539
  75.0 11.8 %collective-permute-start.14 = (f32[4,4,24,128]{3,2,1,0:T(8,128)}, f32[4,4,24,128]{3,2,1,0:T(8,128)S(1)}, u32[]{:S(2)}, u32[]{:S(2)}) collective-permute-start(f32[4,4,24,128]{3,2,1,0:T(8,128)} %get-tuple-element.47), channel_id=1, source_target_pairs={{1,0},{2,1},{3,2},{4,3},{5,4},{6,5},{7,6},{9,8},{10,9},{11,10},{12... | collective-permute-start | bytes 589832 | tf_op jit(solution)/shard_map/ppermute | solution.py:540
  81.4 50.1 %all-to-all-start.2 = ((f32[8,21,16,128]{3,2,1,0:T(8,128)}), f32[8,21,16,128]{3,2,1,0:T(8,128)}, u32[]{:S(2)}, u32[]{:S(2)}) async-start(f32[8,21,16,128]{3,2,1,0:T(8,128)} %get-tuple-element.43.refs_10_), calls=%async_computation.2 | async-start | bytes 2752512 | tf_op jit(solution)/shard_map/all_to_all | solution.py:478
  97.0 15.9 %collective-permute-start.15 = (f32[21,2,16,128]{3,2,1,0:T(8,128)}, f32[21,2,16,128]{3,2,1,0:T(8,128)S(1)}, u32[]{:S(2)}, u32[]{:S(2)}) collective-permute-start(f32[21,2,16,128]{3,2,1,0:T(8,128)} %get-tuple-element.49), channel_id=1, source_target_pairs={{0,4},{1,5},{2,6},{3,7},{4,0},{5,1},{6,2},{7,3},{8,12},{9,13},{10,... | collective-permute-start | bytes 1032200 | tf_op jit(solution)/shard_map/ppermute | solution.py:485
  99.9 18.9 %collective-permute-start.16 = (f32[21,2,16,128]{3,2,1,0:T(8,128)}, f32[21,2,16,128]{3,2,1,0:T(8,128)S(1)}, u32[]{:S(2)}, u32[]{:S(2)}) collective-permute-start(f32[21,2,16,128]{3,2,1,0:T(8,128)} %get-tuple-element.50), channel_id=1, source_target_pairs={{0,2},{1,3},{2,0},{3,1},{4,6},{5,7},{6,4},{7,5},{8,10},{9,11},{10,... | collective-permute-start | bytes 1032200 | tf_op jit(solution)/shard_map/ppermute | solution.py:485
  100.0 20.9 %collective-permute-start.17 = (f32[21,2,16,128]{3,2,1,0:T(8,128)}, f32[21,2,16,128]{3,2,1,0:T(8,128)S(1)}, u32[]{:S(2)}, u32[]{:S(2)}) collective-permute-start(f32[21,2,16,128]{3,2,1,0:T(8,128)} %get-tuple-element.51), channel_id=1, source_target_pairs={{0,6},{1,7},{2,4},{3,5},{4,2},{5,3},{6,0},{7,1},{8,14},{9,15},{10,... | collective-permute-start | bytes 1032200 | tf_op jit(solution)/shard_map/ppermute | solution.py:485
  100.6 27.7 %collective-permute-start.18 = (f32[21,2,16,128]{3,2,1,0:T(8,128)}, f32[21,2,16,128]{3,2,1,0:T(8,128)S(1)}, u32[]{:S(2)}, u32[]{:S(2)}) collective-permute-start(f32[21,2,16,128]{3,2,1,0:T(8,128)} %get-tuple-element.52), channel_id=1, source_target_pairs={{0,5},{1,4},{2,7},{3,6},{4,1},{5,0},{6,3},{7,2},{8,13},{9,12},{10,... | collective-permute-start | bytes 1032200 | tf_op jit(solution)/shard_map/ppermute | solution.py:485
  105.1 28.9 %collective-permute-start.19 = (f32[21,2,16,128]{3,2,1,0:T(8,128)}, f32[21,2,16,128]{3,2,1,0:T(8,128)S(1)}, u32[]{:S(2)}, u32[]{:S(2)}) collective-permute-start(f32[21,2,16,128]{3,2,1,0:T(8,128)} %get-tuple-element.55), channel_id=1, source_target_pairs={{0,3},{1,2},{2,1},{3,0},{4,7},{5,6},{6,5},{7,4},{8,11},{9,10},{10,... | collective-permute-start | bytes 1032200 | tf_op jit(solution)/shard_map/ppermute | solution.py:485
  112.9 22.5 %collective-permute-start.20 = (f32[21,2,16,128]{3,2,1,0:T(8,128)S(1)}, f32[21,2,16,128]{3,2,1,0:T(8,128)S(1)}, u32[]{:S(2)}, u32[]{:S(2)}) collective-permute-start(f32[21,2,16,128]{3,2,1,0:T(8,128)S(1)} %copy-done.9), channel_id=1, source_target_pairs={{0,7},{1,6},{2,5},{3,4},{4,3},{5,2},{6,1},{7,0},{8,15},{9,14},{10,... | collective-permute-start | bytes 1032200 | tf_op jit(solution)/shard_map/ppermute | solution.py:485
  118.8 17.4 %collective-permute-start.21 = (f32[21,2,16,128]{3,2,1,0:T(8,128)S(1)}, f32[21,2,16,128]{3,2,1,0:T(8,128)S(1)}, u32[]{:S(2)}, u32[]{:S(2)}) collective-permute-start(f32[21,2,16,128]{3,2,1,0:T(8,128)S(1)} %copy-done.8), channel_id=1, source_target_pairs={{0,1},{1,0},{2,3},{3,2},{4,5},{5,4},{6,7},{7,6},{8,9},{9,8},{10,11... | collective-permute-start | bytes 1032200 | tf_op jit(solution)/shard_map/ppermute | solution.py:485
  (11 other events, 122.4 us)

commit v5 on v4

--- a/solution.py
+++ b/solution.py
@@ -83,56 +83,63 @@
     return pltpu.SemaphoreType.DMA((count,))
 
 
-def pack_kernel(split, s_ref, x_ref, *refs):
-    count = BANDS if split else 1
-    outs, (xv, hv, sem_in, sem_main, sem_halo) = refs[:count], refs[count:]
+def pack_kernel(s_ref, x_ref, *refs):
+    outer, inner = refs[:BANDS], refs[BANDS]
+    xv, hv, sem_in, sem_main, sem_halo = refs[BANDS + 1 :]
     h = s_ref[0]
     band = 4 * h + s_ref[1]
-    load = pltpu.make_async_copy(x_ref.at[:, h if split else 1 - h], xv, sem_in)
-    load.start()
-    load.wait()
+    loads = start_all([(x_ref.at[:, h], xv.at[0]), (x_ref.at[:, 1 - h], xv.at[1])], sem_in)
     copies = []
-    for k in range(BANDS):
-        if split:
-            d, out = jnp.bitwise_xor(band, k), outs[k]
-            rows = pl.ds(pl.multiple_of(d * ROWS, ROWS), ROWS)
-            above = jnp.maximum(d * ROWS - 1, 0)
-            below = jnp.minimum(d * ROWS + ROWS, 127)
-        else:
-            d, out = k, outs[0].at[k]
-            rows = pl.ds(d * ROWS, ROWS)
-            above, below = max(d * ROWS - 1, 0), min(d * ROWS + ROWS, 127)
-        c = pltpu.make_async_copy(xv.at[:, rows, :], out.at[pl.ds(0, T4)], sem_main.at[k])
-        c.start()
-        copies.append(c)
-        for j in range(T4):
-            up = xv[j, pl.ds(above, 1), :]
-            dn = xv[j, pl.ds(below, 1), :]
-            up = jnp.where(d == 0, jnp.zeros_like(up), up)
-            dn = jnp.where(d == BANDS - 1, jnp.zeros_like(dn), dn)
-            a, b = j, 24 + j
-            hv[k, a // 16, pl.ds(a % 16, 1), :] = up
-            hv[k, b // 16, pl.ds(b % 16, 1), :] = dn
-        c = pltpu.make_async_copy(hv.at[k], out.at[pl.ds(T4, 3)], sem_halo.at[k])
-        c.start()
-        copies.append(c)
+    for n in range(2):
+        loads[n].wait()
+        places = []
+        for k in range(BANDS):
+            if n == 0:
+                d, out = jnp.bitwise_xor(band, k), outer[k]
+                rows = pl.ds(pl.multiple_of(d * ROWS, ROWS), ROWS)
+                above = jnp.maximum(d * ROWS - 1, 0)
+                below = jnp.minimum(d * ROWS + ROWS, 127)
+            else:
+                d, out = k, inner.at[k]
+                rows = pl.ds(d * ROWS, ROWS)
+                above, below = max(d * ROWS - 1, 0), min(d * ROWS + ROWS, 127)
+            places.append((d, out, above, below))
+            c = pltpu.make_async_copy(
+                xv.at[n, :, rows, :], out.at[pl.ds(0, T4)], sem_main.at[n * BANDS + k]
+            )
+            c.start()
+            copies.append(c)
+        for k, (d, out, above, below) in enumerate(places):
+            for j in range(T4):
+                up = xv[n, j, pl.ds(above, 1), :]
+                dn = xv[n, j, pl.ds(below, 1), :]
+                up = jnp.where(d == 0, jnp.zeros_like(up), up)
+                dn = jnp.where(d == BANDS - 1, jnp.zeros_like(dn), dn)
+                a, b = j, 24 + j
+                hv[n, k, a // 16, pl.ds(a % 16, 1), :] = up
+                hv[n, k, b // 16, pl.ds(b % 16, 1), :] = dn
+            c = pltpu.make_async_copy(
+                hv.at[n, k], out.at[pl.ds(T4, 3)], sem_halo.at[n * BANDS + k]
+            )
+            c.start()
+            copies.append(c)
     for c in copies:
         c.wait()
 
 
-def pack(split, info, x):
+def pack(info, x):
     return pl.pallas_call(
-        functools.partial(pack_kernel, split),
-        out_shape=[held(24, ROWS, LANES)] * BANDS if split else [held(BANDS, 24, ROWS, LANES)],
+        pack_kernel,
+        out_shape=[held(24, ROWS, LANES)] * BANDS + [held(BANDS, 24, ROWS, LANES)],
         in_specs=[SMEM, HBM],
-        out_specs=[HBM] * (BANDS if split else 1),
+        out_specs=[HBM] * (BANDS + 1),
         scratch_shapes=[
-            pltpu.VMEM((T4, 128, LANES), F32),
-            pltpu.VMEM((BANDS, 3, ROWS, LANES), F32),
-            pltpu.SemaphoreType.DMA, dma(8), dma(8),
+            pltpu.VMEM((2, T4, 128, LANES), F32),
+            pltpu.VMEM((2, BANDS, 3, ROWS, LANES), F32),
+            dma(2), dma(16), dma(16),
         ],
         compiler_params=pltpu.CompilerParams(vmem_limit_bytes=VMEM_BYTES),
-        name="pack_edge" if split else "pack_middle",
+        name="pack",
     )(info, fixed(x))
 
 
@@ -508,8 +515,8 @@
     up = [(i, i + 1) for i in range(quads - 1)]
     down = [(i + 1, i) for i in range(quads - 1)]
 
-    outer = exchange(pack(True, info, right_side))
-    inner = pack(False, info, right_side)[0]
+    *outer, inner = pack(info, right_side)
+    outer = exchange(outer)
     inner = swapped(inner)
 
     def z_shift(face, lower_half):

time: 138 us -> 138 us (level)
  waiting for transfers between devices: 39.5 us -> 42.9 us
  Pallas kernels: 28.1 us -> 25.6 us
    ppermute x14, waiting for transfers between devices: 27.4 us -> 30.7 us  [exchange(): got[k] = lax.ppermute(pieces[k], BAND, [(i, i ^ k) for i in range(8)])]
    pallas_call x2 -> x1, Pallas kernels: 6.3 us -> 3.81 us  [pack(): pl.pallas_call(pack_kernel, out_shape=[held(24, ROWS, LANES)] * BANDS + [...]
  transfers between devices with their start and end apart: 25 -> 25, of which waited for: 13 -> 14; matrix products, arithmetic and copies ran while one was open for 5% -> 5% of each run, Pallas kernels for 18% -> 16%
where the time goes in v5:
time: 138 us
  starting transfers between devices  59 us (43%)
  waiting for transfers between devices  42.9 us (31%)
  Pallas kernels  25.6 us (19%)
  local copies, waits for them, and re-layouts  8.28 us (6%)
    ppermute x14, waiting for transfers between devices, exchange(): got[k] = lax.ppermute(pieces[k], BAND, [(i, i ^ k) for i in range(8)])  30.7 us
    ppermute x14, starting transfers between devices, exchange(): got[k] = lax.ppermute(pieces[k], BAND, [(i, i ^ k) for i in range(8)])  22.6 us
    all_to_all x3, starting transfers between devices, swapped(): return lax.all_to_all(pieces, BAND, 0, 0, tiled=True)  17.4 us
    pallas_call x2, Pallas kernels, first(): pl.pallas_call(functools.partial(first_kernel, edge), out_shape=[PIECES,...  10.8 us
    all_to_all x3, waiting for transfers between devices, swapped(): return lax.all_to_all(pieces, BAND, 0, 0, tiled=True)  8.41 us
    pallas_call x1, Pallas kernels, second(): pl.pallas_call(second_kernel, out_shape=RES_SHAPES, in_specs=[SMEM] + [HB...  8.06 us
    ppermute x2, starting transfers between devices, z_shift(): return lax.ppermute(face, ('quad',) + BAND, pairs)  5.32 us
    ppermute x1, starting transfers between devices, shards(): yup = lax.ppermute(y15, BAND, [(i, i + 1) for i in range(7)])  3.83 us
  transfers between devices with their start and end apart: 25, of which 14 were waited for; matrix products, arithmetic and copies ran while one was open for 5% of the time, Pallas kernels for 16%

profile of v5, /device:TPU:1, one launch (start us, length us, event | category | flops | bytes accessed | tf_op | source)
XLA Modules:
  0.0 137.5 jit_solution(13434606351245231029)
XLA Ops:
  0.7 3.8 %pack.1 = (f32[24,16,128]{2,1,0:T(8,128)}, f32[24,16,128]{2,1,0:T(8,128)}, f32[24,16,128]{2,1,0:T(8,128)}, f32[24,16,128]{2,1,0:T(8,128)}, f32[24,16,128]{2,1,0:...) custom-call(s32[4]{0:T(128)S(1)} %pad_add_fusion.s_ref, ...), custom_call_target="tpu_custom_call" | custom-call | tf_op jit(solution)/shard_map/pack/pallas_call | solution.py:131
  4.6 3.3 %collective-permute-start = (f32[24,16,128]{2,1,0:T(8,128)}, f32[24,16,128]{2,1,0:T(8,128)S(1)}, u32[]{:S(2)}, u32[]{:S(2)}) collective-permute-start(f32[24,16,128]{2,1,0:T(8,128)} %get-tuple-element.32), channel_id=1, source_target_pairs={{0,1},{1,0},{2,3},{3,2},{4,5},{5,4},{6,7},{7,6},{8,9},{9,8},{10,11... | collective-permute-start | bytes 589832 | tf_op jit(solution)/shard_map/ppermute | solution.py:492
  10.6 2.3 %collective-permute-start.4 = (f32[24,16,128]{2,1,0:T(8,128)}, f32[24,16,128]{2,1,0:T(8,128)S(1)}, u32[]{:S(2)}, u32[]{:S(2)}) collective-permute-start(f32[24,16,128]{2,1,0:T(8,128)} %get-tuple-element.36), channel_id=1, source_target_pairs={{0,5},{1,4},{2,7},{3,6},{4,1},{5,0},{6,3},{7,2},{8,13},{9,12},{10,... | collective-permute-start | bytes 589832 | tf_op jit(solution)/shard_map/ppermute | solution.py:492
  16.6 4.2 %all-to-all-start = ((f32[8,24,16,128]{3,2,1,0:T(8,128)}), f32[8,24,16,128]{3,2,1,0:T(8,128)}, u32[]{:S(2)}, u32[]{:S(2)}) async-start(f32[8,24,16,128]{3,2,1,0:T(8,128)} %get-tuple-element.39), calls=%async_computation | async-start | bytes 3145728 | tf_op jit(solution)/shard_map/all_to_all | solution.py:485
  21.5 2.9 %collective-permute-start.7 = (f32[7,2,16,128]{3,2,1,0:T(8,128)}, f32[7,2,16,128]{3,2,1,0:T(8,128)}, u32[]{:S(2)}, u32[]{:S(2)}) collective-permute-start(f32[7,2,16,128]{3,2,1,0:T(8,128)} %get-tuple-element.61), channel_id=1, source_target_pairs={{0,0},{1,2},{2,4},{3,6},{4,1},{5,3},{6,5},{7,7},{8,8},{9,10},{10,1... | collective-permute-start | bytes 344072 | tf_op jit(solution)/shard_map/ppermute | solution.py:538
  26.4 2.4 %collective-permute-done.4.refs_5_ = f32[24,16,128]{2,1,0:T(8,128)S(1)} collective-permute-done((f32[24,16,128]{2,1,0:T(8,128)}, f32[24,16,128]{2,1,0:T(8,128)S(1)}, u32[]{:S(2)}, u32[]{:S(2)}) %collective-permute-start.4) | collective-permute-done | bytes 196640 | tf_op jit(solution)/shard_map/ppermute | solution.py:492
  28.8 2.1 %collective-permute-done.5.refs_6_ = f32[24,16,128]{2,1,0:T(8,128)S(1)} collective-permute-done((f32[24,16,128]{2,1,0:T(8,128)}, f32[24,16,128]{2,1,0:T(8,128)S(1)}, u32[]{:S(2)}, u32[]{:S(2)}) %collective-permute-start.5) | collective-permute-done | bytes 196640 | tf_op jit(solution)/shard_map/ppermute | solution.py:492
  30.9 5.3 %collective-permute-done.6.refs_7_ = f32[24,16,128]{2,1,0:T(8,128)S(1)} collective-permute-done((f32[24,16,128]{2,1,0:T(8,128)}, f32[24,16,128]{2,1,0:T(8,128)S(1)}, u32[]{:S(2)}, u32[]{:S(2)}) %collective-permute-start.6) | collective-permute-done | bytes 196640 | tf_op jit(solution)/shard_map/ppermute | solution.py:492
  36.2 2.9 %faces.1 = (f32[84,16,128]{2,1,0:T(8,128)}, f32[84,16,128]{2,1,0:T(8,128)}) custom-call(f32[24,16,128]{2,1,0:T(8,128)S(1)} %copy-done, f32[24,16,128]{2,1,0:T(8,128)S(1)} %collective-permute-done.refs_1_, f32[24,16,128]{2,1,0:T(8,128)S(1)} %collective-permute-done.1.refs_2_, f32[24,16,128]{2,1,0:T(8,128)S(1)} %collective-permute-done.2.refs_3_, ...), custom_call_target="tpu_custom_call" | custom-call | flops 999999995904 | bytes 1000000000 | tf_op jit(solution)/shard_map/faces/pallas_call | solution.py:163
  40.4 4.0 %collective-permute-start.10 = (f32[84,16,128]{2,1,0:T(8,128)}, f32[84,16,128]{2,1,0:T(8,128)S(1)}, u32[]{:S(2)}, u32[]{:S(2)}) collective-permute-start(f32[84,16,128]{2,1,0:T(8,128)} %get-tuple-element.42), channel_id=1, source_target_pairs={{0,8},{1,9},{2,10},{3,11},{8,16},{9,17},{10,18},{11,19},{12,4},{13... | collective-permute-start | bytes 2064392 | tf_op jit(solution)/shard_map/ppermute | solution.py:529
  46.2 4.0 %all-to-all-done.refs_8_ = f32[8,24,16,128]{3,2,1,0:T(8,128)} async-done(((f32[8,24,16,128]{3,2,1,0:T(8,128)}), f32[8,24,16,128]{3,2,1,0:T(8,128)}, u32[]{:S(2)}, u32[]{:S(2)}) %all-to-all-start) | async-done | bytes 1572896 | tf_op jit(solution)/shard_map/all_to_all | solution.py:485
  50.2 5.4 %first_middle.1 = (f32[8,21,16,128]{3,2,1,0:T(8,128)}, f32[4,4,24,128]{3,2,1,0:T(8,128)}, f32[4,4,24,128]{3,2,1,0:T(8,128)}) custom-call(s32[4]{0:T(128)S(1)} %copy-done.2, f32[24,16,128]{2,1,0:T(8,128)S(1)} %copy-done, f32[24,16,128]{2,1,0:T(8,128)S(1)} %collective-permute-done.refs_1_, f32[24,16,128]{2,1,0:T(8,128)S(1)} %collective-permute-done.1.refs_2_, ...), custom_call_target="tpu_custom_call" | custom-call | flops 10000000000 | bytes 10000000 | tf_op jit(solution)/shard_map/first_middle/pallas_call | solution.py:434
  55.6 7.7 %all-to-all-start.1 = ((f32[8,21,16,128]{3,2,1,0:T(8,128)}), f32[8,21,16,128]{3,2,1,0:T(8,128)}, u32[]{:S(2)}, u32[]{:S(2)}) async-start(f32[8,21,16,128]{3,2,1,0:T(8,128)} %get-tuple-element.40.refs_9_), calls=%async_computation.1 | async-start | bytes 2752512 | tf_op jit(solution)/shard_map/all_to_all | solution.py:485
  63.3 5.4 %first_edge.1 = (f32[8,21,16,128]{3,2,1,0:T(8,128)}, f32[4,4,24,128]{3,2,1,0:T(8,128)}, f32[4,4,24,128]{3,2,1,0:T(8,128)}, f32[84,16,128]{2,1,0:T(8,128)}, f32[84,16,128]{2,1,0:T(8,128)}) custom-call(s32[4]{0:T(128)S(1)} %copy-done.2, f32[24,16,128]{2,1,0:T(8,128)S(1)} %copy-done, ...), custom_call_target="tpu_custom_call", output_to_operand_aliasing={{1}: (14, {}), {2}: (15, {})} | custom-call | tf_op jit(solution)/shard_map/first_edge/pallas_call | solution.py:434
  71.9 3.8 %collective-permute-start.13 = (f32[4,4,24,128]{3,2,1,0:T(8,128)}, f32[4,4,24,128]{3,2,1,0:T(8,128)S(1)}, u32[]{:S(2)}, u32[]{:S(2)}) collective-permute-start(f32[4,4,24,128]{3,2,1,0:T(8,128)} %get-tuple-element.48), channel_id=1, source_target_pairs={{0,1},{1,2},{2,3},{3,4},{4,5},{5,6},{6,7},{8,9},{9,10},{10,11},{11... | collective-permute-start | bytes 589832 | tf_op jit(solution)/shard_map/ppermute | solution.py:546
  77.6 4.4 %all-to-all-done.1 = f32[8,21,16,128]{3,2,1,0:T(8,128)} async-done(((f32[8,21,16,128]{3,2,1,0:T(8,128)}), f32[8,21,16,128]{3,2,1,0:T(8,128)}, u32[]{:S(2)}, u32[]{:S(2)}) %all-to-all-start.1) | async-done | bytes 1376288 | tf_op jit(solution)/shard_map/all_to_all | solution.py:485
  82.0 5.5 %all-to-all-start.2 = ((f32[8,21,16,128]{3,2,1,0:T(8,128)}), f32[8,21,16,128]{3,2,1,0:T(8,128)}, u32[]{:S(2)}, u32[]{:S(2)}) async-start(f32[8,21,16,128]{3,2,1,0:T(8,128)} %get-tuple-element.45.refs_10_), calls=%async_computation.2 | async-start | bytes 2752512 | tf_op jit(solution)/shard_map/all_to_all | solution.py:485
  89.6 8.1 %second.1 = (f32[21,2,16,128]{3,2,1,0:T(8,128)}, f32[21,2,16,128]{3,2,1,0:T(8,128)}, f32[21,2,16,128]{3,2,1,0:T(8,128)}, f32[21,2,16,128]{3,2,1,0:T(8,128)}, f32...) custom-call(s32[4]{0:T(128)S(1)} %copy-done.2, ...), custom_call_target="tpu_custom_call" | custom-call | flops 999999995904 | bytes 1000000000 | tf_op jit(solution)/shard_map/second/pallas_call | solution.py:458
  97.7 2.9 %collective-permute-start.15 = (f32[21,2,16,128]{3,2,1,0:T(8,128)}, f32[21,2,16,128]{3,2,1,0:T(8,128)S(1)}, u32[]{:S(2)}, u32[]{:S(2)}) collective-permute-start(f32[21,2,16,128]{3,2,1,0:T(8,128)} %get-tuple-element.51), channel_id=1, source_target_pairs={{0,4},{1,5},{2,6},{3,7},{4,0},{5,1},{6,2},{7,3},{8,12},{9,13},{10,... | collective-permute-start | bytes 1032200 | tf_op jit(solution)/shard_map/ppermute | solution.py:492
  101.3 4.5 %collective-permute-start.18 = (f32[21,2,16,128]{3,2,1,0:T(8,128)}, f32[21,2,16,128]{3,2,1,0:T(8,128)S(1)}, u32[]{:S(2)}, u32[]{:S(2)}) collective-permute-start(f32[21,2,16,128]{3,2,1,0:T(8,128)} %get-tuple-element.54), channel_id=1, source_target_pairs={{0,5},{1,4},{2,7},{3,6},{4,1},{5,0},{6,3},{7,2},{8,13},{9,12},{10,... | collective-permute-start | bytes 1032200 | tf_op jit(solution)/shard_map/ppermute | solution.py:492
  106.1 7.4 %collective-permute-done.15 = f32[21,2,16,128]{3,2,1,0:T(8,128)S(1)} collective-permute-done((f32[21,2,16,128]{3,2,1,0:T(8,128)}, f32[21,2,16,128]{3,2,1,0:T(8,128)S(1)}, u32[]{:S(2)}, u32[]{:S(2)}) %collective-permute-start.15) | collective-permute-done | bytes 344096 | tf_op jit(solution)/shard_map/ppermute | solution.py:492
  113.6 2.1 %collective-permute-start.20 = (f32[21,2,16,128]{3,2,1,0:T(8,128)S(1)}, f32[21,2,16,128]{3,2,1,0:T(8,128)S(1)}, u32[]{:S(2)}, u32[]{:S(2)}) collective-permute-start(f32[21,2,16,128]{3,2,1,0:T(8,128)S(1)} %copy-done.9), channel_id=1, source_target_pairs={{0,7},{1,6},{2,5},{3,4},{4,3},{5,2},{6,1},{7,0},{8,15},{9,14},{10,... | collective-permute-start | bytes 1032200 | tf_op jit(solution)/shard_map/ppermute | solution.py:492
  115.7 3.7 %collective-permute-done.16 = f32[21,2,16,128]{3,2,1,0:T(8,128)S(1)} collective-permute-done((f32[21,2,16,128]{3,2,1,0:T(8,128)}, f32[21,2,16,128]{3,2,1,0:T(8,128)S(1)}, u32[]{:S(2)}, u32[]{:S(2)}) %collective-permute-start.16) | collective-permute-done | bytes 344096 | tf_op jit(solution)/shard_map/ppermute | solution.py:492
  121.7 7.4 %collective-permute-done.18 = f32[21,2,16,128]{3,2,1,0:T(8,128)S(1)} collective-permute-done((f32[21,2,16,128]{3,2,1,0:T(8,128)}, f32[21,2,16,128]{3,2,1,0:T(8,128)S(1)}, u32[]{:S(2)}, u32[]{:S(2)}) %collective-permute-start.18) | collective-permute-done | bytes 344096 | tf_op jit(solution)/shard_map/ppermute | solution.py:492
  (67 shorter events, 31.0 us)
Async XLA Ops:
  4.6 8.4 %collective-permute-start = (f32[24,16,128]{2,1,0:T(8,128)}, f32[24,16,128]{2,1,0:T(8,128)S(1)}, u32[]{:S(2)}, u32[]{:S(2)}) collective-permute-start(f32[24,16,128]{2,1,0:T(8,128)} %get-tuple-element.32), channel_id=1, source_target_pairs={{0,1},{1,0},{2,3},{3,2},{4,5},{5,4},{6,7},{7,6},{8,9},{9,8},{10,11... | collective-permute-start | bytes 589832 | tf_op jit(solution)/shard_map/ppermute | solution.py:492
  7.9 13.6 %collective-permute-start.2 = (f32[24,16,128]{2,1,0:T(8,128)}, f32[24,16,128]{2,1,0:T(8,128)S(1)}, u32[]{:S(2)}, u32[]{:S(2)}) collective-permute-start(f32[24,16,128]{2,1,0:T(8,128)} %get-tuple-element.34), channel_id=1, source_target_pairs={{0,3},{1,2},{2,1},{3,0},{4,7},{5,6},{6,5},{7,4},{8,11},{9,10},{10,... | collective-permute-start | bytes 589832 | tf_op jit(solution)/shard_map/ppermute | solution.py:492
  9.6 14.8 %collective-permute-start.3 = (f32[24,16,128]{2,1,0:T(8,128)}, f32[24,16,128]{2,1,0:T(8,128)S(1)}, u32[]{:S(2)}, u32[]{:S(2)}) collective-permute-start(f32[24,16,128]{2,1,0:T(8,128)} %get-tuple-element.35), channel_id=1, source_target_pairs={{0,4},{1,5},{2,6},{3,7},{4,0},{5,1},{6,2},{7,3},{8,12},{9,13},{10,... | collective-permute-start | bytes 589832 | tf_op jit(solution)/shard_map/ppermute | solution.py:492
  10.6 18.1 %collective-permute-start.4 = (f32[24,16,128]{2,1,0:T(8,128)}, f32[24,16,128]{2,1,0:T(8,128)S(1)}, u32[]{:S(2)}, u32[]{:S(2)}) collective-permute-start(f32[24,16,128]{2,1,0:T(8,128)} %get-tuple-element.36), channel_id=1, source_target_pairs={{0,5},{1,4},{2,7},{3,6},{4,1},{5,0},{6,3},{7,2},{8,13},{9,12},{10,... | collective-permute-start | bytes 589832 | tf_op jit(solution)/shard_map/ppermute | solution.py:492
  12.9 17.9 %collective-permute-start.5 = (f32[24,16,128]{2,1,0:T(8,128)}, f32[24,16,128]{2,1,0:T(8,128)S(1)}, u32[]{:S(2)}, u32[]{:S(2)}) collective-permute-start(f32[24,16,128]{2,1,0:T(8,128)} %get-tuple-element.37), channel_id=1, source_target_pairs={{0,6},{1,7},{2,4},{3,5},{4,2},{5,3},{6,0},{7,1},{8,14},{9,15},{10,... | collective-permute-start | bytes 589832 | tf_op jit(solution)/shard_map/ppermute | solution.py:492
  14.6 21.6 %collective-permute-start.6 = (f32[24,16,128]{2,1,0:T(8,128)}, f32[24,16,128]{2,1,0:T(8,128)S(1)}, u32[]{:S(2)}, u32[]{:S(2)}) collective-permute-start(f32[24,16,128]{2,1,0:T(8,128)} %get-tuple-element.38), channel_id=1, source_target_pairs={{0,7},{1,6},{2,5},{3,4},{4,3},{5,2},{6,1},{7,0},{8,15},{9,14},{10,... | collective-permute-start | bytes 589832 | tf_op jit(solution)/shard_map/ppermute | solution.py:492
  16.6 33.6 %all-to-all-start = ((f32[8,24,16,128]{3,2,1,0:T(8,128)}), f32[8,24,16,128]{3,2,1,0:T(8,128)}, u32[]{:S(2)}, u32[]{:S(2)}) async-start(f32[8,24,16,128]{3,2,1,0:T(8,128)} %get-tuple-element.39), calls=%async_computation | async-start | bytes 3145728 | tf_op jit(solution)/shard_map/all_to_all | solution.py:485
  21.5 24.6 %collective-permute-start.7 = (f32[7,2,16,128]{3,2,1,0:T(8,128)}, f32[7,2,16,128]{3,2,1,0:T(8,128)}, u32[]{:S(2)}, u32[]{:S(2)}) collective-permute-start(f32[7,2,16,128]{3,2,1,0:T(8,128)} %get-tuple-element.61), channel_id=1, source_target_pairs={{0,0},{1,2},{2,4},{3,6},{4,1},{5,3},{6,5},{7,7},{8,8},{9,10},{10,1... | collective-permute-start | bytes 344072 | tf_op jit(solution)/shard_map/ppermute | solution.py:538
  24.5 21.7 %collective-permute-start.8 = (f32[7,2,16,128]{3,2,1,0:T(8,128)}, f32[7,2,16,128]{3,2,1,0:T(8,128)}, u32[]{:S(2)}, u32[]{:S(2)}) collective-permute-start(f32[7,2,16,128]{3,2,1,0:T(8,128)} %get-tuple-element.60), channel_id=1, source_target_pairs={{0,1},{1,3},{2,5},{3,7},{4,0},{5,2},{6,4},{7,6},{8,9},{9,11},{10,1... | collective-permute-start | bytes 344072 | tf_op jit(solution)/shard_map/ppermute | solution.py:539
  39.1 24.2 %collective-permute-start.9 = (f32[84,16,128]{2,1,0:T(8,128)}, f32[84,16,128]{2,1,0:T(8,128)S(1)}, u32[]{:S(2)}, u32[]{:S(2)}) collective-permute-start(f32[84,16,128]{2,1,0:T(8,128)} %get-tuple-element.41), channel_id=1, source_target_pairs={{4,12},{5,13},{6,14},{7,15},{8,0},{9,1},{10,2},{11,3},{12,20},{13,... | collective-permute-start | bytes 2064392 | tf_op jit(solution)/shard_map/ppermute | solution.py:529
  40.4 22.9 %collective-permute-start.10 = (f32[84,16,128]{2,1,0:T(8,128)}, f32[84,16,128]{2,1,0:T(8,128)S(1)}, u32[]{:S(2)}, u32[]{:S(2)}) collective-permute-start(f32[84,16,128]{2,1,0:T(8,128)} %get-tuple-element.42), channel_id=1, source_target_pairs={{0,8},{1,9},{2,10},{3,11},{8,16},{9,17},{10,18},{11,19},{12,4},{13... | collective-permute-start | bytes 2064392 | tf_op jit(solution)/shard_map/ppermute | solution.py:529
  55.6 26.4 %all-to-all-start.1 = ((f32[8,21,16,128]{3,2,1,0:T(8,128)}), f32[8,21,16,128]{3,2,1,0:T(8,128)}, u32[]{:S(2)}, u32[]{:S(2)}) async-start(f32[8,21,16,128]{3,2,1,0:T(8,128)} %get-tuple-element.40.refs_9_), calls=%async_computation.1 | async-start | bytes 2752512 | tf_op jit(solution)/shard_map/all_to_all | solution.py:485
  68.7 18.8 %collective-permute-start.11 = (f32[84,16,128]{2,1,0:T(8,128)}, f32[84,16,128]{2,1,0:T(8,128)S(1)}, u32[]{:S(2)}, u32[]{:S(2)}) collective-permute-start(f32[84,16,128]{2,1,0:T(8,128)} %get-tuple-element.46), channel_id=1, source_target_pairs={{0,8},{8,16},{16,24},{24,32},{32,40},{40,48},{48,56},{56,64},{64,7... | collective-permute-start | bytes 2064392 | tf_op jit(solution)/shard_map/ppermute | solution.py:544
  70.6 19.0 %collective-permute-start.12 = (f32[84,16,128]{2,1,0:T(8,128)}, f32[84,16,128]{2,1,0:T(8,128)S(1)}, u32[]{:S(2)}, u32[]{:S(2)}) collective-permute-start(f32[84,16,128]{2,1,0:T(8,128)} %get-tuple-element.47), channel_id=1, source_target_pairs={{8,0},{16,8},{24,16},{32,24},{40,32},{48,40},{56,48},{64,56},{72,6... | collective-permute-start | bytes 2064392 | tf_op jit(solution)/shard_map/ppermute | solution.py:545
  71.9 15.7 %collective-permute-start.13 = (f32[4,4,24,128]{3,2,1,0:T(8,128)}, f32[4,4,24,128]{3,2,1,0:T(8,128)S(1)}, u32[]{:S(2)}, u32[]{:S(2)}) collective-permute-start(f32[4,4,24,128]{3,2,1,0:T(8,128)} %get-tuple-element.48), channel_id=1, source_target_pairs={{0,1},{1,2},{2,3},{3,4},{4,5},{5,6},{6,7},{8,9},{9,10},{10,11},{11... | collective-permute-start | bytes 589832 | tf_op jit(solution)/shard_map/ppermute | solution.py:546
  75.7 11.8 %collective-permute-start.14 = (f32[4,4,24,128]{3,2,1,0:T(8,128)}, f32[4,4,24,128]{3,2,1,0:T(8,128)S(1)}, u32[]{:S(2)}, u32[]{:S(2)}) collective-permute-start(f32[4,4,24,128]{3,2,1,0:T(8,128)} %get-tuple-element.49), channel_id=1, source_target_pairs={{1,0},{2,1},{3,2},{4,3},{5,4},{6,5},{7,6},{9,8},{10,9},{11,10},{12... | collective-permute-start | bytes 589832 | tf_op jit(solution)/shard_map/ppermute | solution.py:547
  82.0 50.1 %all-to-all-start.2 = ((f32[8,21,16,128]{3,2,1,0:T(8,128)}), f32[8,21,16,128]{3,2,1,0:T(8,128)}, u32[]{:S(2)}, u32[]{:S(2)}) async-start(f32[8,21,16,128]{3,2,1,0:T(8,128)} %get-tuple-element.45.refs_10_), calls=%async_computation.2 | async-start | bytes 2752512 | tf_op jit(solution)/shard_map/all_to_all | solution.py:485
  97.7 15.9 %collective-permute-start.15 = (f32[21,2,16,128]{3,2,1,0:T(8,128)}, f32[21,2,16,128]{3,2,1,0:T(8,128)S(1)}, u32[]{:S(2)}, u32[]{:S(2)}) collective-permute-start(f32[21,2,16,128]{3,2,1,0:T(8,128)} %get-tuple-element.51), channel_id=1, source_target_pairs={{0,4},{1,5},{2,6},{3,7},{4,0},{5,1},{6,2},{7,3},{8,12},{9,13},{10,... | collective-permute-start | bytes 1032200 | tf_op jit(solution)/shard_map/ppermute | solution.py:492
  100.5 18.9 %collective-permute-start.16 = (f32[21,2,16,128]{3,2,1,0:T(8,128)}, f32[21,2,16,128]{3,2,1,0:T(8,128)S(1)}, u32[]{:S(2)}, u32[]{:S(2)}) collective-permute-start(f32[21,2,16,128]{3,2,1,0:T(8,128)} %get-tuple-element.52), channel_id=1, source_target_pairs={{0,2},{1,3},{2,0},{3,1},{4,6},{5,7},{6,4},{7,5},{8,10},{9,11},{10,... | collective-permute-start | bytes 1032200 | tf_op jit(solution)/shard_map/ppermute | solution.py:492
  100.7 20.9 %collective-permute-start.17 = (f32[21,2,16,128]{3,2,1,0:T(8,128)}, f32[21,2,16,128]{3,2,1,0:T(8,128)S(1)}, u32[]{:S(2)}, u32[]{:S(2)}) collective-permute-start(f32[21,2,16,128]{3,2,1,0:T(8,128)} %get-tuple-element.53), channel_id=1, source_target_pairs={{0,6},{1,7},{2,4},{3,5},{4,2},{5,3},{6,0},{7,1},{8,14},{9,15},{10,... | collective-permute-start | bytes 1032200 | tf_op jit(solution)/shard_map/ppermute | solution.py:492
  101.3 27.7 %collective-permute-start.18 = (f32[21,2,16,128]{3,2,1,0:T(8,128)}, f32[21,2,16,128]{3,2,1,0:T(8,128)S(1)}, u32[]{:S(2)}, u32[]{:S(2)}) collective-permute-start(f32[21,2,16,128]{3,2,1,0:T(8,128)} %get-tuple-element.54), channel_id=1, source_target_pairs={{0,5},{1,4},{2,7},{3,6},{4,1},{5,0},{6,3},{7,2},{8,13},{9,12},{10,... | collective-permute-start | bytes 1032200 | tf_op jit(solution)/shard_map/ppermute | solution.py:492
  105.8 28.9 %collective-permute-start.19 = (f32[21,2,16,128]{3,2,1,0:T(8,128)}, f32[21,2,16,128]{3,2,1,0:T(8,128)S(1)}, u32[]{:S(2)}, u32[]{:S(2)}) collective-permute-start(f32[21,2,16,128]{3,2,1,0:T(8,128)} %get-tuple-element.57), channel_id=1, source_target_pairs={{0,3},{1,2},{2,1},{3,0},{4,7},{5,6},{6,5},{7,4},{8,11},{9,10},{10,... | collective-permute-start | bytes 1032200 | tf_op jit(solution)/shard_map/ppermute | solution.py:492
  113.6 22.5 %collective-permute-start.20 = (f32[21,2,16,128]{3,2,1,0:T(8,128)S(1)}, f32[21,2,16,128]{3,2,1,0:T(8,128)S(1)}, u32[]{:S(2)}, u32[]{:S(2)}) collective-permute-start(f32[21,2,16,128]{3,2,1,0:T(8,128)S(1)} %copy-done.9), channel_id=1, source_target_pairs={{0,7},{1,6},{2,5},{3,4},{4,3},{5,2},{6,1},{7,0},{8,15},{9,14},{10,... | collective-permute-start | bytes 1032200 | tf_op jit(solution)/shard_map/ppermute | solution.py:492
  119.4 17.4 %collective-permute-start.21 = (f32[21,2,16,128]{3,2,1,0:T(8,128)S(1)}, f32[21,2,16,128]{3,2,1,0:T(8,128)S(1)}, u32[]{:S(2)}, u32[]{:S(2)}) collective-permute-start(f32[21,2,16,128]{3,2,1,0:T(8,128)S(1)} %copy-done.8), channel_id=1, source_target_pairs={{0,1},{1,0},{2,3},{3,2},{4,5},{5,4},{6,7},{7,6},{8,9},{9,8},{10,11... | collective-permute-start | bytes 1032200 | tf_op jit(solution)/shard_map/ppermute | solution.py:492
  (11 other events, 157.3 us)
